TPU v7x, 32 devices: a whole 2x2x4 slice. The times are simulated.
32 devices in a mesh: grp: 4 (over x, core), seq: 8 (over z, y).
Axes of the slice: x: 2, y: 2, z: 4, core: 2. Of those that a mesh axis runs over, the one named last changes fastest.
Arguments:
- targets: bfloat16 [16384, 1024], P(('grp', 'seq')), may hold values from -30 to 30
- context: bfloat16 [256, 1024], P('seq'), may hold values from -9 to 9
- w_query: bfloat16 [1024, 1024], replicated, as said below
- w_key: bfloat16 [1024, 1024], replicated, as said below
- w_value: bfloat16 [1024, 1024], replicated, may hold values from -0.1875 to 0.1875
- w_out: bfloat16 [1024, 1024], replicated, may hold values from -0.1875 to 0.1875
- visible: int32 [8, 16], replicated, may hold values from 0 to 1, as said below
- grad_out: bfloat16 [16384, 1024], P(('grp', 'seq')), may hold values from -24 to 24
Outputs:
- d_targets: bfloat16 [16384, 1024], P(('grp', 'seq'))
- d_context: bfloat16 [256, 1024], P(('grp', 'seq'))
- grad_wq: float32 [1024, 1024], P(('grp', 'seq'))
- grad_wo: float32 [1024, 1024], P(('grp', 'seq'))
Inputs may be any that keep to these rules, and one draw needn't show every extreme that they name: Every row of visible holds at least one 1. `w_query`: entries have a spread of about one over the square root of 1024. `w_key`: entries have a spread of about one over the square root of 1024.
All inputs are finite; a program needn't handle non-finite values.
Results may differ from a plain program's by a relative error of at most 0.018.
The roundings to bfloat16 on the way count: a program that leaves them out, or rounds other values in their place, can miss the bound.
Values may be sent and summed in bfloat16 or wider, within the bound.
No kernel may reach another device: no remote copies, remote signals or barrier semaphores. Data moves between devices by JAX's collectives and lax.ppermute only.
A program may use at most 128 MiB of HBM per device.

v0:
```python
from functools import partial

import jax
import jax.numpy as jnp
from jax import lax
from jax.sharding import PartitionSpec as P

HEADS = 16
TVIEWS = 8
CVIEWS = 16


def merge_groups(stack):
    return jnp.moveaxis(stack, 0, 1).reshape(stack.shape[1], stack.shape[0] * stack.shape[2])


def on_device(targets, context, w_query, w_key, w_value, w_out, visible, grad_out):
    query_rows, model_width = targets.shape
    head_size = model_width // HEADS
    group_heads = 4
    group_count = HEADS // group_heads
    group_width = group_heads * head_size
    score_scale = head_size ** (-0.5)
    grp_count = lax.axis_size("grp")
    seq_count = lax.axis_size("seq")
    device_index = lax.axis_index("grp") * seq_count + lax.axis_index("seq")
    queries = jnp.dot(targets, w_query, preferred_element_type=jnp.float32).astype(jnp.bfloat16)
    keys_local = jnp.dot(context, w_key, preferred_element_type=jnp.float32).astype(jnp.bfloat16)
    values_local = jnp.dot(context, w_value, preferred_element_type=jnp.float32).astype(
        jnp.bfloat16
    )
    grad_attn = jnp.dot(grad_out, w_out.T, preferred_element_type=jnp.float32).astype(jnp.bfloat16)
    keys_all, values_all = (
        lax.all_gather(keys_local, "seq", axis=0, tiled=True),
        lax.all_gather(values_local, "seq", axis=0, tiled=True),
    )
    context_rows = keys_all.shape[0]
    view_tokens = query_rows * grp_count * seq_count // TVIEWS
    context_view = context_rows // CVIEWS
    query_views = (
        device_index * query_rows + jnp.arange(query_rows, dtype=jnp.int32)
    ) // view_tokens
    query_onehot = (query_views[:, None] == jnp.arange(TVIEWS, dtype=jnp.int32)[None, :]).astype(
        jnp.float32
    )
    visible_rows = jnp.dot(query_onehot, visible.astype(jnp.float32))
    context_places = jnp.arange(context_rows, dtype=jnp.int32)

    def heads_of(matrix, group_index):
        block_cols = lax.dynamic_slice_in_dim(matrix, group_index * group_width, group_width, 1)
        return block_cols.reshape(matrix.shape[0], group_heads, head_size)

    key_onehot = (
        context_places[:, None] // context_view == jnp.arange(CVIEWS, dtype=jnp.int32)[None, :]
    ).astype(jnp.float32)
    allowed_all = jnp.dot(visible_rows, key_onehot.T) > 0.5

    def forward_group(group_index, keep_parts):
        query_g = heads_of(queries, group_index)
        grad_g = heads_of(grad_attn, group_index)
        key_g = heads_of(keys_all, group_index)
        value_g = heads_of(values_all, group_index)
        scores = (
            jnp.einsum("bhd,khd->hbk", query_g, key_g, preferred_element_type=jnp.float32)
            * score_scale
        )
        masked = jnp.where(allowed_all[None], scores, -1e30)
        row_max = jnp.max(masked, axis=2, keepdims=True)
        unnormed = jnp.where(allowed_all[None], jnp.exp(masked - row_max), 0.0)
        row_sum = jnp.sum(unnormed, axis=2, keepdims=True)
        probs_low = (unnormed / row_sum).astype(jnp.bfloat16)
        attended = jnp.einsum(
            "hbk,khd->bhd", probs_low, value_g, preferred_element_type=jnp.float32
        ).astype(jnp.bfloat16)
        row_dot = jnp.sum(attended.astype(jnp.float32) * grad_g.astype(jnp.float32), axis=2).T[
            :, :, None
        ]
        grad_scores = jnp.einsum(
            "bhd,khd->hbk", grad_g, value_g, preferred_element_type=jnp.float32
        )
        grad_logits = (probs_low.astype(jnp.float32) * (grad_scores - row_dot)).astype(jnp.bfloat16)
        query_grad = (
            jnp.einsum("hbk,khd->bhd", grad_logits, key_g, preferred_element_type=jnp.float32)
            * score_scale
        ).astype(jnp.bfloat16)
        results = (
            attended.reshape(query_rows, group_width),
            query_grad.reshape(query_rows, group_width),
            row_max,
            row_sum,
            row_dot,
        )
        key_part = (
            jnp.einsum("hbk,bhd->khd", grad_logits, query_g, preferred_element_type=jnp.float32)
            * score_scale
        )
        value_part = jnp.einsum(
            "hbk,bhd->khd", probs_low, grad_g, preferred_element_type=jnp.float32
        )
        results = results + (
            key_part.reshape(context_rows, group_width),
            value_part.reshape(context_rows, group_width),
        )
        return results

    group_list = jnp.arange(group_count, dtype=jnp.int32)
    stacked = lax.map(partial(forward_group, keep_parts=True), group_list)
    both_full = jnp.concatenate([merge_groups(stacked[5]), merge_groups(stacked[6])], axis=1)
    attended = merge_groups(stacked[0])
    query_grad = merge_groups(stacked[1])
    weight_stack = jnp.concatenate([w_key.T, w_value.T], axis=0).astype(jnp.float32)
    summed = lax.psum_scatter(both_full, ("grp", "seq"), scatter_dimension=0, tiled=True)
    d_context = jnp.dot(summed, weight_stack, precision=lax.Precision.HIGHEST).astype(jnp.bfloat16)
    d_targets = jnp.dot(query_grad, w_query.T, preferred_element_type=jnp.float32).astype(
        jnp.bfloat16
    )
    contract = (((0,), (0,)), ((), ()))
    wq_term = lax.dot_general(targets, query_grad, contract, preferred_element_type=jnp.float32)
    wo_term = lax.dot_general(attended, grad_out, contract, preferred_element_type=jnp.float32)
    grad_wq, grad_wo = (
        lax.psum_scatter(wq_term, ("grp", "seq"), scatter_dimension=0, tiled=True),
        lax.psum_scatter(wo_term, ("grp", "seq"), scatter_dimension=0, tiled=True),
    )
    return (d_targets, d_context, grad_wq, grad_wo)


def solution(mesh):
    in_specs = (
        P(("grp", "seq"), None),
        P("seq", None),
        P(),
        P(),
        P(),
        P(),
        P(),
        P(("grp", "seq"), None),
    )
    out_specs = (
        P(("grp", "seq"), None),
        P(("grp", "seq"), None),
        P(("grp", "seq"), None),
        P(("grp", "seq"), None),
    )
    return jax.shard_map(
        on_device, mesh=mesh, in_specs=in_specs, out_specs=out_specs, check_vma=False
    )
```

profile of v0, /device:TPU:0, one launch (start us, length us, event | category | flops | bytes accessed | tf_op | source)
XLA Modules:
  0.0 574.5 jit_solution(16385634799071898158)
XLA Ops:
  7.3 2.2 convolution_convert_fusion.4
  11.4 33.0 %all_gather.6 = bf16[256,1024]{1,0:T(8,128)(2,1)S(1)} all-gather(bf16[32,1024]{1,0:T(8,128)(2,1)S(1)} %convolution_convert_fusion.5), channel_id=1, replica_groups=mesh['grp'=4,'seq'=8] {'seq'}, dimensions={0}, use_global_device_ids=true | all-gather | bytes 589824 | tf_op jit(solution)/shard_map/all_gather | solution.py:35
  44.4 31.2 %all_gather.7 = bf16[256,1024]{1,0:T(8,128)(2,1)S(1)} all-gather(bf16[32,1024]{1,0:T(8,128)(2,1)S(1)} %convolution_convert_fusion.4), channel_id=1, replica_groups=mesh['grp'=4,'seq'=8] {'seq'}, dimensions={0}, use_global_device_ids=true | all-gather | bytes 589824 | tf_op jit(solution)/shard_map/all_gather | solution.py:34
  75.6 4.3 convolution_convert_fusion.2
  79.9 2.2 convolution_convert_fusion.3
  82.1 47.7 %while.16 = (s32[]{:T(128)}, bf16[4,512,256]{1,2,0:T(8,128)(2,1)}, bf16[4,512,256]{1,2,0:T(8,128)(2,1)}, f32[4,256,256]{1,2,0:T(8,128)}, f32[4,256,256]{1,2,0:T(...) while((s32[]{:T(128)}, bf16[4,512,256]{1,2,0:T(8,128)(2,1)}, ...), condition=%wide.region_4.5_spmd, body=%wide.region_0.4_spmd.sunk | while | flops 409401600 | bytes 28737908 | solution.py:107
  83.8 1.0 constant_dynamic-slice_fusion.10
  86.1 2.4 fusion.85
  88.5 1.9 divide_convert_fusion.2
  95.7 1.0 constant_dynamic-slice_fusion.10
  96.8 1.0 constant_dynamic-slice_fusion.9
  98.0 2.4 fusion.85
  100.4 1.9 divide_convert_fusion.2
  107.6 1.0 constant_dynamic-slice_fusion.10
  108.8 1.0 constant_dynamic-slice_fusion.9
  109.9 2.4 fusion.85
  112.3 1.9 divide_convert_fusion.2
  119.5 1.0 constant_dynamic-slice_fusion.10
  121.8 2.4 fusion.85
  124.2 1.9 divide_convert_fusion.2
  129.8 3.0 pad_maximum_fusion
  132.8 2.9 copy.39
  135.8 1.1 copy-done.9
  136.9 4.5 convolution_bitcast_fusion
  141.4 5.4 copy.41
  148.0 4.5 fusion.30
  152.5 1.2 copy-done.11
  153.7 2.3 convolution_convert_fusion.1
  155.9 120.7 %reduce-scatter.10.cloned.1.call-done = f32[8,2048]{1,0:T(8,128)} async-done(((f32[256,2048]{1,0:T(8,128)}), f32[8,2048]{1,0:T(8,128)}) %reduce-scatter.10.cloned.1.call-update) | async-done | bytes 65552
  276.6 6.2 %fusion.16 = bf16[8,1024]{1,0:T(8,128)(2,1)} fusion(f32[8,2048]{1,0:T(8,128)} %reduce-scatter.10.cloned.1.call-done, bf16[1024,1024]{0,1:T(8,128)(2,1)} %bitcast.125, bf16[1024,1024]{0,1:T(8,128)(2,1)} %bitcast.126), kind=kOutput, calls=%fused_computation.38 | convolution fusion | flops 209723392 | bytes 4276224 | tf_op jit(solution)/shard_map/dot_general | solution.py:113
  282.9 138.8 %reduce-scatter.12.cloned.1.call-done = f32[32,1024]{1,0:T(8,128)} async-done(((f32[1024,1024]{1,0:T(8,128)}), f32[32,1024]{1,0:T(8,128)}) %reduce-scatter.12.cloned.1.call-update) | async-done | bytes 131088
  421.7 146.3 %reduce-scatter.8.cloned.1.call-done = f32[32,1024]{1,0:T(8,128)} async-done(((f32[1024,1024]{1,0:T(8,128)}), f32[32,1024]{1,0:T(8,128)}) %reduce-scatter.8.cloned.1.call-update) | async-done | bytes 131088 | tf_op jit(solution)/shard_map/reduce_scatter | solution.py:122
  (128 shorter events, 24.6 us)
Async XLA Ops:
  7.2 72.7 %copy-start = (bf16[1024,1024]{1,0:T(8,128)(2,1)S(1)}, bf16[1024,1024]{1,0:T(8,128)(2,1)}, u32[]{:S(2)}) copy-start(bf16[1024,1024]{1,0:T(8,128)(2,1)} %param.12) | copy-start | bytes 6291460
  7.2 2.4 copy-start.6
  7.2 269.5 %reduce-scatter.10.cloned.1.call-start = ((), (), s32[]{:S(2)}) async-start(), calls=%async_computation.4 | async-start | bytes 2162688
  7.3 2.3 copy-start.5
  7.3 2.8 copy-start.12
  75.6 4.3 copy-start.8
  82.1 1.6 copy-start.1
  82.1 2.8 copy-start.3
  83.7 2.3 copy-start.7
  92.0 2.0 copy-start.2
  92.1 2.0 copy-start.4
  94.0 1.6 copy-start.1
  94.0 2.8 copy-start.3
  95.7 2.3 copy-start.7
  104.0 2.0 copy-start.2
  104.0 2.0 copy-start.4
  106.0 1.6 copy-start.1
  106.0 2.8 copy-start.3
  107.6 2.3 copy-start.7
  115.9 2.0 copy-start.2
  115.9 2.0 copy-start.4
  117.9 1.6 copy-start.1
  117.9 2.8 copy-start.3
  119.5 2.3 copy-start.7
  127.8 2.0 copy-start.2
  127.8 2.0 copy-start.4
  135.7 1.2 copy-start.9
  135.7 285.9 %reduce-scatter.12.cloned.1.call-start = ((), (), s32[]{:S(2)}) async-start(), calls=%async_computation.5 | async-start | bytes 4325376
  146.8 1.2 copy-start.10
  146.8 421.2 %reduce-scatter.8.cloned.1.call-start = ((), (), s32[]{:S(2)}) async-start(), calls=%async_computation.3 | async-start | bytes 4325376 | tf_op jit(solution)/shard_map/reduce_scatter | solution.py:122
  152.4 1.2 copy-start.11
Sparse Core Ops, SparseCore 0:
  135.9 140.7 reduce-scatter.9
  279.5 142.1 reduce-scatter.11
  424.5 143.4 reduce-scatter.7
where the time goes:
time: 575 us
  waiting for transfers between devices  406 us (71%)
  blocking collectives  64.2 us (11%)
  matrix products  44.6 us (8%)
  local copies, waits for them, and re-layouts  32 us (6%)
  between operations  13.9 us (2%)
  other arithmetic  10.5 us (2%)
    unnamed x5, waiting for transfers between devices  260 us
    reduce_scatter x1, waiting for transfers between devices, on_device(): lax.psum_scatter(wo_term, ('grp', 'seq'), scatter_dimension=0, tiled=True)  146 us
    all_gather x1, blocking collectives, on_device(): lax.all_gather(values_local, 'seq', axis=0, tiled=True)  33 us
    all_gather x1, blocking collectives, on_device(): lax.all_gather(keys_local, 'seq', axis=0, tiled=True)  31.2 us
    unnamed x18, local copies, waits for them, and re-layouts  11.7 us
  transfers between devices with their start and end apart: 3, of which 3 were waited for; matrix products, arithmetic and copies ran while one was open for 4% of the time, Pallas kernels for 0%

commit v1 on v0

v1 whole, which is shorter than its diff:
```python
from functools import partial

import jax
import jax.numpy as jnp
from jax import lax
from jax.experimental import pallas as pl
from jax.experimental.pallas import tpu as pltpu
from jax.sharding import PartitionSpec as P

HEADS = 16
TVIEWS = 8
CVIEWS = 16
AXES = ("grp", "seq")
CHUNK = 256

F32 = jnp.float32
BF16 = jnp.bfloat16


def dot(left, right, dims):
    return lax.dot_general(left, right, (dims, ((), ())), preferred_element_type=F32)


def forward_kernel(chunk, block_rows, q_ref, k_ref, v_ref, bias_ref, att_ref, probs_ref):
    rows = q_ref.shape[1]
    key_block = k_ref[...]
    value_block = v_ref[...]
    for start in range(0, rows, chunk):
        cols = pl.ds(start, chunk)
        scores = dot(key_block, q_ref[:, cols], ((0,), (0,)))
        scores = scores + bias_ref[start // block_rows][:, :1]
        row_max = jnp.max(scores, axis=0, keepdims=True)
        unnormed = jnp.exp(scores - row_max)
        row_sum = jnp.sum(unnormed, axis=0, keepdims=True)
        probs = (unnormed * (1.0 / row_sum)).astype(BF16)
        probs_ref[0, :, cols] = probs
        att_ref[:, cols] = dot(value_block, probs, ((1,), (0,))).astype(BF16)


def backward_kernel(
    chunk, scale, q_ref, g_ref, k_ref, v_ref, att_ref, probs_ref, qg_ref, kvg_ref
):
    rows = q_ref.shape[1]
    key_block = k_ref[...]
    value_block = v_ref[...]
    key_grad = jnp.zeros(key_block.shape, F32)
    value_grad = jnp.zeros(key_block.shape, F32)
    for start in range(0, rows, chunk):
        cols = pl.ds(start, chunk)
        grad = g_ref[:, cols]
        probs = probs_ref[0, :, cols]
        row_dot = jnp.sum(att_ref[:, cols].astype(F32) * grad.astype(F32), axis=0, keepdims=True)
        grad_scores = dot(value_block, grad, ((0,), (0,)))
        logits = (probs.astype(F32) * (grad_scores - row_dot)).astype(BF16)
        qg_ref[:, cols] = dot(key_block, logits, ((1,), (0,))).astype(BF16)
        key_grad += dot(q_ref[:, cols], logits, ((1,), (1,)))
        value_grad += dot(grad, probs, ((1,), (1,)))
    kvg_ref[0] = (key_grad * scale).astype(BF16)
    kvg_ref[1] = value_grad.astype(BF16)


def on_device(targets, context, w_query, w_key, w_value, w_out, visible, grad_out):
    query_rows, width = targets.shape
    head_size = width // HEADS
    score_scale = head_size ** (-0.5)
    grp_count = lax.axis_size("grp")
    seq_count = lax.axis_size("seq")
    device_count = grp_count * seq_count
    grp = lax.axis_index("grp")
    seq = lax.axis_index("seq")
    me = grp * seq_count + seq
    core = grp % 2
    core_mask = seq_count
    high_count = grp_count // 2
    half_width = width // 2
    half_heads = HEADS // 2
    context_rows = context.shape[0] * seq_count

    def swap(array, mask):
        return lax.ppermute(array, AXES, [(i, i ^ mask) for i in range(device_count)])

    def bit_of(mask):
        return (me // mask) % 2

    own_half = context.shape[0] // 2
    held = lax.dynamic_slice_in_dim(context, core * own_half, own_half, 0)[None]
    mask = 1
    while mask < seq_count:
        other = swap(held, mask)
        upper = bit_of(mask) == 1
        held = jnp.concatenate(
            [jnp.where(upper, other, held), jnp.where(upper, held, other)], axis=0
        )
        mask *= 2
    other = swap(held, core_mask)
    held = jnp.stack(
        [jnp.where(core == 1, other, held), jnp.where(core == 1, held, other)], axis=1
    )
    context_all = held.reshape(context_rows, width)

    targets_two = jnp.concatenate([targets, swap(targets, core_mask)], axis=0)
    grad_two = jnp.concatenate([grad_out, swap(grad_out, core_mask)], axis=0)

    def columns_of(matrix, which):
        split = matrix.reshape(width, high_count, 2, width // grp_count)
        return lax.dynamic_index_in_dim(split, which, 2, keepdims=False).reshape(width, half_width)

    wq_mine = columns_of(w_query, core)
    wq_both = jnp.concatenate([wq_mine, columns_of(w_query, 1 - core)], axis=1)
    wkv = jnp.concatenate([columns_of(w_key, core), columns_of(w_value, core)], axis=1)
    wo_mine = lax.dynamic_index_in_dim(
        w_out.reshape(high_count, 2, width // grp_count, width), core, 1, keepdims=False
    ).reshape(half_width, width)

    queries = dot(wq_mine, targets_two, ((0,), (1,))).astype(BF16)
    grads = dot(wo_mine, grad_two, ((1,), (1,))).astype(BF16)
    kv_scale = jnp.where(jnp.arange(width) < half_width, score_scale, 1.0).astype(BF16)
    key_values = dot(wkv, context_all, ((0,), (1,))).astype(BF16) * kv_scale[:, None]

    view_rows = query_rows * device_count // TVIEWS
    context_view = context_rows // CVIEWS
    firsts = jnp.stack([me, me ^ core_mask]) * query_rows
    seen = visible[firsts // view_rows]
    seen = jnp.repeat(seen, context_view, axis=1)
    bias = jnp.where(seen == 1, 0.0, -1e30).astype(F32)
    bias = jnp.broadcast_to(bias[:, :, None], (2, context_rows, 128))

    rows = 2 * query_rows
    head_rows = pl.BlockSpec((head_size, rows), lambda h: (h, 0))
    key_spec = pl.BlockSpec((head_size, context_rows), lambda h: (h, 0))
    value_spec = pl.BlockSpec((head_size, context_rows), lambda h: (h + half_heads, 0))
    probs_spec = pl.BlockSpec((1, context_rows, rows), lambda h: (h, 0, 0))
    wide = jax.ShapeDtypeStruct((half_width, rows), BF16)
    unit = 2 * half_width * rows * context_rows

    attended, probs = pl.pallas_call(
        partial(forward_kernel, CHUNK, query_rows),
        grid=(half_heads,),
        in_specs=[
            head_rows,
            key_spec,
            value_spec,
            pl.BlockSpec((2, context_rows, 128), lambda h: (0, 0, 0)),
        ],
        out_specs=[head_rows, probs_spec],
        out_shape=[wide, jax.ShapeDtypeStruct((half_heads, context_rows, rows), BF16)],
        cost_estimate=pl.CostEstimate(
            flops=8 * unit, bytes_accessed=8 << 20, transcendentals=unit // 128
        ),
        name="attend",
    )(queries, key_values, key_values, bias)

    wo_term = dot(attended, grad_two, ((1,), (0,))).astype(BF16)

    query_grad, kv_grad = pl.pallas_call(
        partial(backward_kernel, CHUNK, score_scale),
        grid=(half_heads,),
        in_specs=[head_rows, head_rows, key_spec, value_spec, head_rows, probs_spec],
        out_specs=[
            head_rows,
            pl.BlockSpec((2, head_size, context_rows), lambda h: (0, h, 0)),
        ],
        out_shape=[wide, jax.ShapeDtypeStruct((2, half_width, context_rows), BF16)],
        cost_estimate=pl.CostEstimate(flops=8 * unit, bytes_accessed=8 << 20, transcendentals=0),
        name="attend_back",
    )(queries, grads, key_values, key_values, attended, probs)

    wq_term = dot(targets_two, query_grad, ((0,), (1,))).astype(BF16)
    ctx_term = dot(kv_grad.reshape(width, context_rows), wkv, ((0,), (1,))).astype(BF16)

    high_masks = []
    mask = core_mask * high_count
    while mask > core_mask:
        high_masks.append(mask)
        mask //= 2
    seq_masks = []
    mask = seq_count // 2
    while mask >= 1:
        seq_masks.append(mask)
        mask //= 2
    all_masks = high_masks + seq_masks
    bits = [2] * len(all_masks)
    first, second = high_masks[-1], seq_masks[-1]
    rest = seq_masks[-2::-1] + high_masks[:-1]

    def halve(array, masks, mask, last=False):
        axis = masks.index(mask)
        bit = bit_of(mask)
        sent = lax.dynamic_index_in_dim(array, 1 - bit, axis, keepdims=False)
        kept = lax.dynamic_index_in_dim(array, bit, axis, keepdims=False)
        total = kept.astype(F32) + swap(sent, mask).astype(F32)
        left = masks[:axis] + masks[axis + 1 :]
        return (total if last else total.astype(BF16)), left

    def reduce_scatter(array):
        cut = array.shape[-1] // 2
        one, masks_one = halve(array[..., :cut], all_masks, first)
        two, masks_two = halve(array[..., cut:], all_masks, second)
        one, masks = halve(one, masks_one, second)
        two, _ = halve(two, masks_two, first)
        both = jnp.concatenate([one, two], axis=-1)
        for step, mask in enumerate(rest):
            both, masks = halve(both, masks, mask, step == len(rest) - 1)
        return both

    out_rows = width // device_count
    ctx_out = context_rows // device_count
    grad_wo = reduce_scatter(wo_term.reshape(*bits, out_rows, width))

    ctx_split = ctx_term.reshape(high_count, 2, seq_count, ctx_out, width)
    ctx_kept = lax.dynamic_index_in_dim(ctx_split, core, 1, keepdims=False)
    ctx_sent = lax.dynamic_index_in_dim(ctx_split, 1 - core, 1, keepdims=False)
    ctx_pair = (ctx_kept.astype(F32) + swap(ctx_sent, core_mask).astype(F32)).astype(BF16)
    ctx_part = jnp.swapaxes(
        ctx_pair.reshape(high_count * seq_count, ctx_out, 2, half_width), 1, 2
    ).reshape(high_count * seq_count, 2 * ctx_out, half_width)
    wq_part = jnp.swapaxes(
        wq_term.reshape(high_count, 2, seq_count, out_rows, half_width), 1, 2
    ).reshape(high_count * seq_count, 2 * out_rows, half_width)
    tail = jnp.concatenate([wq_part, ctx_part], axis=1)
    tail = reduce_scatter(tail.reshape(*bits, 2 * out_rows + 2 * ctx_out, half_width))

    wq_sum = tail[: 2 * out_rows].reshape(2, out_rows, half_width)
    mine = lax.dynamic_index_in_dim(wq_sum, core, 0, keepdims=False)
    theirs = swap(lax.dynamic_index_in_dim(wq_sum, 1 - core, 0, keepdims=False), core_mask)
    mine = mine.reshape(out_rows, high_count, width // grp_count)
    theirs = theirs.reshape(out_rows, high_count, width // grp_count)
    grad_wq = jnp.stack(
        [jnp.where(core == 0, mine, theirs), jnp.where(core == 0, theirs, mine)], axis=2
    ).reshape(out_rows, width)
    ctx_sum = tail[2 * out_rows :].reshape(2, ctx_out, half_width)
    d_context = jnp.swapaxes(ctx_sum, 0, 1).reshape(ctx_out, width).astype(BF16)

    back = swap(query_grad[:, query_rows:], core_mask)
    query_both = jnp.concatenate([query_grad[:, :query_rows], back], axis=0)
    d_targets = dot(query_both, wq_both, ((0,), (1,))).astype(BF16)
    return (d_targets, d_context, grad_wq, grad_wo)


def solution(mesh):
    in_specs = (
        P(AXES, None),
        P("seq", None),
        P(),
        P(),
        P(),
        P(),
        P(),
        P(AXES, None),
    )
    out_specs = (P(AXES, None), P(AXES, None), P(AXES, None), P(AXES, None))
    return jax.shard_map(
        on_device, mesh=mesh, in_specs=in_specs, out_specs=out_specs, check_vma=False
    )
```

time: 575 us -> 126 us (0.22)
  waiting for transfers between devices: 406 us -> 29.6 us
  blocking collectives: 64.2 us -> 0 us
  matrix products: 44.6 us -> 16.6 us
  Pallas kernels: 0 us -> 25.3 us
  starting transfers between devices: 0.3 us -> 21.1 us
  between operations: 13.9 us -> 1.2 us
  other arithmetic: 10.5 us -> 1.96 us
    unnamed x5 -> x0, waiting for transfers between devices: 260 us -> none
    reduce_scatter x1 -> x0, waiting for transfers between devices: 146 us -> none  [on_device(): lax.psum_scatter(wo_term, ('grp', 'seq'), scatter_dimension=0, tiled=True)]
    all_gather x2 -> x0, blocking collectives: 64.2 us -> none  [the longest x1 33 us: on_device(): lax.all_gather(values_local, 'seq', axis=0, tiled=True)]
    ppermute x0 -> x21, waiting for transfers between devices: none -> 29.6 us  [swap(): lax.ppermute(array, AXES, [(i, i ^ mask) for i in range(device_count)])]
    pallas_call x0 -> x2, Pallas kernels: none -> 25.3 us  [the longest x1 13.6 us: on_device(): pl.pallas_call(partial(forward_kernel, CHUNK, query_rows), grid=(half_hea...]
    ppermute x0 -> x21, starting transfers between devices: none -> 21.1 us  [swap(): lax.ppermute(array, AXES, [(i, i ^ mask) for i in range(device_count)])]
    dot_general x29 -> x7, matrix products: 35 us -> 16.6 us  [dot(): lax.dot_general(left, right, (dims, ((), ())), preferred_element_type=F32)]
    sub x4 -> x0, matrix products: 9.64 us -> none  [forward_group(): unnormed = jnp.where(allowed_all[None], jnp.exp(masked - row_max), 0.0)]
  transfers between devices with their start and end apart: 3 -> 21, of which waited for: 3 -> 10; matrix products, arithmetic and copies ran while one was open for 4% -> 25% of each run, Pallas kernels for 0% -> 0%
where the time goes in v1:
time: 126 us; the launch traced here: 125 us
  waiting for transfers between devices  29.6 us (23%)
  local copies, waits for them, and re-layouts  29.5 us (23%)
  Pallas kernels  25.3 us (20%)
  starting transfers between devices  21.1 us (17%)
  matrix products  16.6 us (13%)
  other arithmetic  1.96 us (2%)
    ppermute x21, waiting for transfers between devices, swap(): lax.ppermute(array, AXES, [(i, i ^ mask) for i in range(device_count)])  29.6 us
    ppermute x21, starting transfers between devices, swap(): lax.ppermute(array, AXES, [(i, i ^ mask) for i in range(device_count)])  21.1 us
    unnamed x40, local copies, waits for them, and re-layouts  17.4 us
    dot_general x7, matrix products, dot(): lax.dot_general(left, right, (dims, ((), ())), preferred_element_type=F32)  16.6 us
    pallas_call x1, Pallas kernels, on_device(): pl.pallas_call(partial(forward_kernel, CHUNK, query_rows), grid=(half_hea...  13.6 us
    pallas_call x1, Pallas kernels, on_device(): pl.pallas_call(partial(backward_kernel, CHUNK, score_scale), grid=(half_h...  11.7 us
    dynamic_slice x2, local copies, waits for them, and re-layouts, columns_of(): lax.dynamic_index_in_dim(split, which, 2, keepdims=False)  4.26 us
  transfers between devices with their start and end apart: 21, of which 10 were waited for; matrix products, arithmetic and copies ran while one was open for 25% of the time, Pallas kernels for 0%

profile of v1, /device:TPU:0, one launch (start us, length us, event | category | flops | bytes accessed | tf_op | source)
XLA Modules:
  0.0 125.2 jit_solution(9664000380859925239)
XLA Ops:
  1.6 3.0 %collective-permute-start.2 = (bf16[1,16,1024]{2,1,0:T(8,128)(2,1)S(1)}, bf16[1,16,1024]{2,1,0:T(8,128)(2,1)S(1)}, u32[]{:S(2)}, u32[]{:S(2)}) collective-permute-start(bf16[1,16,1024]{2,1,0:T(8,128)(2,1)S(1)} %dynamic-slice_bitcast_fusion.8), channel_id=1, source_target_pairs={{0,1},{1,0},{2,3},{3,2},{4,5},{5,4},{6,7},{7,6},{8,9},{9,8},{10,11... | collective-permute-start | bytes 98312 | tf_op jit(solution)/shard_map/ppermute | solution.py:80
  5.2 1.2 gather_fusion
  6.4 3.9 %copy.20 = bf16[1024,1024]{0,1:T(8,128)(2,1)} copy(bf16[1024,1024]{1,0:T(8,128)(2,1)} %param.10) | data formatting | bytes 4194304 | tf_op args[2]
  10.4 2.9 %constant_dynamic-slice_fusion.11 = (bf16[1024,2,1,256]{0,3,2,1:T(8,128)(2,1)S(1)}, bf16[1024,2,1,256]{0,3,2,1:T(8,128)(2,1)}) fusion(bf16[1024,2,2,256]{0,3,2,1:T(8,128)(2,1)} %bitcast.138, s32[]{:T(128)S(6)} %select_n.256, s32[]{:T(128)S(6)} %select_n.280), kind=kLoop, calls=%fused_computation.112 | loop fusion | bytes 4194312 | tf_op jit(solution)/shard_map/jit(dynamic_index_in_dim)/dynamic_slice | solution.py:106
  14.3 1.6 %collective-permute-start.3 = (bf16[2,16,1024]{2,1,0:T(8,128)(2,1)S(1)}, bf16[2,16,1024]{2,1,0:T(8,128)(2,1)S(1)}, u32[]{:S(2)}, u32[]{:S(2)}) collective-permute-start(bf16[2,16,1024]{2,1,0:T(8,128)(2,1)S(1)} %pad_maximum_fusion.13), channel_id=1, source_target_pairs={{0,2},{1,3},{2,0},{3,1},{4,6},{5,7},{6,4},{7,5},{8,10},{9,11},{10,... | collective-permute-start | bytes 196616 | tf_op jit(solution)/shard_map/ppermute | solution.py:80
  16.0 2.3 %constant_dynamic-update-slice_fusion.3 = bf16[1024,1024]{1,0:T(8,128)(2,1)} fusion(bf16[512,1024]{1,0:T(8,128)(2,1)} %param.15), kind=kLoop, calls=%fused_computation.116 | loop fusion | bytes 2097152
  18.4 4.0 %copy.21 = bf16[1024,1024]{0,1:T(8,128)(2,1)} copy(bf16[1024,1024]{1,0:T(8,128)(2,1)} %param.11) | data formatting | bytes 4194304 | tf_op args[3]
  22.4 3.9 %copy.22 = bf16[1024,1024]{0,1:T(8,128)(2,1)} copy(bf16[1024,1024]{1,0:T(8,128)(2,1)} %param.12) | data formatting | bytes 4194304 | tf_op args[4]
  26.4 2.7 %collective-permute-start.4 = (bf16[4,16,1024]{2,1,0:T(8,128)(2,1)S(1)}, bf16[4,16,1024]{2,1,0:T(8,128)(2,1)S(1)}, u32[]{:S(2)}, u32[]{:S(2)}) collective-permute-start(bf16[4,16,1024]{2,1,0:T(8,128)(2,1)S(1)} %pad_maximum_fusion.11), channel_id=1, source_target_pairs={{0,4},{1,5},{2,6},{3,7},{4,0},{5,1},{6,2},{7,3},{8,12},{9,13},{10,... | collective-permute-start | bytes 393224 | tf_op jit(solution)/shard_map/ppermute | solution.py:80
  29.1 6.1 %collective-permute-done.4 = bf16[4,16,1024]{2,1,0:T(8,128)(2,1)S(1)} collective-permute-done((bf16[4,16,1024]{2,1,0:T(8,128)(2,1)S(1)}, bf16[4,16,1024]{2,1,0:T(8,128)(2,1)S(1)}, u32[]{:S(2)}, u32[]{:S(2)}) %collective-permute-start.4) | collective-permute-done | bytes 131104 | tf_op jit(solution)/shard_map/ppermute | solution.py:80
  35.3 1.4 %constant_dynamic-slice_fusion.8 = (bf16[1024,2,1,256]{0,3,2,1:T(8,128)(2,1)S(1)}, bf16[1024,2,1,256]{0,3,2,1:T(8,128)(2,1)S(1)}) fusion(bf16[1024,2,2,256]{0,3,2,1:T(8,128)(2,1)} %bitcast.140, s32[]{:T(128)S(6)} %select_n.256, bf16[1024,2,2,256]{0,3,2,1:T(8,128)(2,1)S(1)} %bitcast.139), kind=kLoop, calls=%fused_computation.109 | loop fusion | bytes 4194308 | tf_op jit(solution)/shard_map/jit(dynamic_index_in_dim)/dynamic_slice | solution.py:106
  36.9 1.6 %fusion.11.k_ref.v_ref = bf16[1024,256]{1,0:T(8,128)(2,1)} fusion(bf16[256,1024]{1,0:T(8,128)(2,1)S(1)} %bitcast.156, bf16[1024,512]{0,1:T(8,128)(2,1)S(1)} %bitcast.147, bf16[1024,512]{0,1:T(8,128)(2,1)S(1)} %bitcast.149, bf16[1024]{0:T(1024)(128)(2,1)S(1)} %select_convert_fusion), kind=kOutput, calls=%fused_computation.17 | convolution fusion | flops 541589504 | bytes 3147776 | tf_op jit(solution)/shard_map/dot_general | solution.py:21
  39.3 1.3 %constant_dynamic-update-slice_fusion = bf16[1024,1024]{1,0:T(8,128)(2,1)S(1)} fusion(bf16[1024,1024]{1,0:T(8,128)(2,1)S(1)} %copy-done.10, bf16[512,1024]{1,0:T(8,128)(2,1)} %collective-permute-done), kind=kLoop, calls=%fused_computation.113 | loop fusion | bytes 2097152 | tf_op jit(solution)/shard_map/concatenate | solution.py:101
  40.6 2.3 %convolution_convert_fusion.3.q_ref = bf16[512,1024]{1,0:T(8,128)(2,1)} fusion(bf16[1024,512]{0,1:T(8,128)(2,1)S(1)} %bitcast.144, bf16[1024,1024]{1,0:T(8,128)(2,1)S(1)} %constant_dynamic-update-slice_fusion), kind=kOutput, calls=%fused_computation.10 | convolution fusion | flops 1074266112 | bytes 4194304 | tf_op jit(solution)/shard_map/dot_general | solution.py:21
  43.1 1.3 %constant_dynamic-update-slice_fusion.2 = bf16[1024,1024]{1,0:T(8,128)(2,1)S(1)} fusion(bf16[1024,1024]{1,0:T(8,128)(2,1)S(1)} %copy-done.12, bf16[512,1024]{1,0:T(8,128)(2,1)} %collective-permute-done.1), kind=kLoop, calls=%fused_computation.115 | loop fusion | bytes 2097152 | tf_op jit(solution)/shard_map/concatenate | solution.py:102
  44.4 2.3 %convolution_convert_fusion.2.g_ref = bf16[512,1024]{1,0:T(8,128)(2,1)} fusion(bf16[512,1024]{1,0:T(8,128)(2,1)S(1)} %bitcast.151, bf16[1024,1024]{1,0:T(8,128)(2,1)S(1)} %constant_dynamic-update-slice_fusion.2), kind=kOutput, calls=%fused_computation.9 | convolution fusion | flops 1074266112 | bytes 4194304 | tf_op jit(solution)/shard_map/dot_general | solution.py:21
  47.5 13.6 %attend.1 = (bf16[512,1024]{1,0:T(8,128)(2,1)}, bf16[8,256,1024]{2,1,0:T(8,128)(2,1)}) custom-call(bf16[512,1024]{1,0:T(8,128)(2,1)} %convolution_convert_fusion.3.q_ref, bf16[1024,256]{1,0:T(8,128)(2,1)} %fusion.11.k_ref.v_ref, bf16[1024,256]{1,0:T(8,128)(2,1)} %fusion.11.k_ref.v_ref, f32[2,256,128]{2,1,0:T(8,128)} %broadcast_in_dim.36.bias_ref), custom_call_target="tpu_custom_call" | custom-call | flops 2147483648 | bytes 8388608 | tf_op jit(solution)/shard_map/attend/pallas_call | solution.py:136
  61.1 4.1 %convolution_convert_fusion = bf16[512,1024]{1,0:T(8,128)(2,1)} fusion(bf16[512,1024]{1,0:T(8,128)(2,1)} %get-tuple-element.8.att_ref, bf16[1024,1024]{1,0:T(8,128)(2,1)} %copy-done.13), kind=kOutput, calls=%fused_computation.7 | convolution fusion | flops 1074266112 | bytes 4194304 | tf_op jit(solution)/shard_map/dot_general | solution.py:21
  65.2 11.7 %attend_back.1 = (bf16[512,1024]{1,0:T(8,128)(2,1)}, bf16[2,512,256]{2,1,0:T(8,128)(2,1)}) custom-call(bf16[512,1024]{1,0:T(8,128)(2,1)} %convolution_convert_fusion.3.q_ref, bf16[512,1024]{1,0:T(8,128)(2,1)} %convolution_convert_fusion.2.g_ref, bf16[1024,256]{1,0:T(8,128)(2,1)} %fusion.11.k_ref.v_ref, bf16[1024,256]{1,0:T(8,128)(2,1)} %fusion.11.k_ref.v_ref, ...), custom_call_target="tpu_custom_call" | custom-call | flops 2147483648 | bytes 8388608 | tf_op jit(solution)/shard_map/attend_back/pallas_call | solution.py:155
  76.9 3.3 %convolution_convert_fusion.1 = bf16[1024,512]{1,0:T(8,128)(2,1)S(1)} fusion(bf16[1024,1024]{1,0:T(8,128)(2,1)} %copy-done.11, bf16[512,1024]{1,0:T(8,128)(2,1)} %get-tuple-element.10), kind=kOutput, calls=%fused_computation.8 | convolution fusion | flops 1074266112 | bytes 4194304 | tf_op jit(solution)/shard_map/dot_general | solution.py:21
  83.5 1.6 %collective-permute-start.15 = (bf16[2,2,2,32,512]{4,3,0,1,2:T(8,128)(2,1)S(1)}, bf16[2,2,2,32,512]{4,3,0,1,2:T(8,128)(2,1)S(1)}, u32[]{:S(2)}, u32[]{:S(2)}) collective-permute-start(bf16[2,2,2,32,512]{4,3,0,1,2:T(8,128)(2,1)S(1)} %bitcast.159), channel_id=1, source_target_pairs={{0,16},{1,17},{2,18},{3,19},{4,20},{5,21},{6,22},{7,23},{8,24},{9,... | collective-permute-start | bytes 786440 | tf_op jit(solution)/shard_map/ppermute | solution.py:80
  85.3 6.0 %collective-permute-done.17 = bf16[2,2,2,32,512]{4,3,1,2,0:T(8,128)(2,1)S(1)} collective-permute-done((bf16[2,2,2,32,512]{4,3,1,2,0:T(8,128)(2,1)S(1)}, bf16[2,2,2,32,512]{4,3,1,2,0:T(8,128)(2,1)S(1)}, u32[]{:S(2)}, u32[]{:S(2)}) %collective-permute-start.17) | collective-permute-done | bytes 262176 | tf_op jit(solution)/shard_map/ppermute | solution.py:80
  91.4 1.6 %collective-permute-start.18 = (bf16[2,2,32,512]{3,2,0,1:T(8,128)(2,1)S(1)}, bf16[2,2,32,512]{3,2,0,1:T(8,128)(2,1)S(1)}, u32[]{:S(2)}, u32[]{:S(2)}) collective-permute-start(bf16[2,2,32,512]{3,2,0,1:T(8,128)(2,1)S(1)} %dynamic-slice_bitcast_fusion.3), channel_id=1, source_target_pairs={{0,16},{1,17},{2,18},{3,19},{4,20},{5,21},{6,22},{7,23},{8,24},{9,... | collective-permute-start | bytes 393224 | tf_op jit(solution)/shard_map/ppermute | solution.py:80
  93.8 1.5 %collective-permute-start.10 = (bf16[2,2,2,80,256]{4,3,2,1,0:T(8,128)(2,1)S(1)}, bf16[2,2,2,80,256]{4,3,2,1,0:T(8,128)(2,1)S(1)}, u32[]{:S(2)}, u32[]{:S(2)}) collective-permute-start(bf16[2,2,2,80,256]{4,3,2,1,0:T(8,128)(2,1)S(1)} %fusion.22), channel_id=1, source_target_pairs={{0,1},{1,0},{2,3},{3,2},{4,5},{5,4},{6,7},{7,6},{8,9},{9,8},{10,11... | collective-permute-start | bytes 983048 | tf_op jit(solution)/shard_map/ppermute | solution.py:80
  96.5 3.2 %collective-permute-done.16 = bf16[2,2,32,512]{3,2,0,1:T(8,128)(2,1)S(1)} collective-permute-done((bf16[2,2,32,512]{3,2,0,1:T(8,128)(2,1)S(1)}, bf16[2,2,32,512]{3,2,0,1:T(8,128)(2,1)S(1)}, u32[]{:S(2)}, u32[]{:S(2)}) %collective-permute-start.16) | collective-permute-done | bytes 131104 | tf_op jit(solution)/shard_map/ppermute | solution.py:80
  99.8 4.9 %collective-permute-done.10 = bf16[2,2,2,80,256]{4,3,2,1,0:T(8,128)(2,1)S(1)} collective-permute-done((bf16[2,2,2,80,256]{4,3,2,1,0:T(8,128)(2,1)S(1)}, bf16[2,2,2,80,256]{4,3,2,1,0:T(8,128)(2,1)S(1)}, u32[]{:S(2)}, u32[]{:S(2)}) %collective-permute-start.10) | collective-permute-done | bytes 327712 | tf_op jit(solution)/shard_map/ppermute | solution.py:80
  106.6 3.6 %collective-permute-done.11 = bf16[2,2,80,256]{3,2,1,0:T(8,128)(2,1)S(1)} collective-permute-done((bf16[2,2,80,256]{3,2,1,0:T(8,128)(2,1)S(1)}, bf16[2,2,80,256]{3,2,1,0:T(8,128)(2,1)S(1)}, u32[]{:S(2)}, u32[]{:S(2)}) %collective-permute-start.11) | collective-permute-done | bytes 163872 | tf_op jit(solution)/shard_map/ppermute | solution.py:80
  111.1 3.2 %collective-permute-start.20 = (bf16[32,1024]{1,0:T(8,128)(2,1)S(1)}, bf16[32,1024]{1,0:T(8,128)(2,1)S(1)}, u32[]{:S(2)}, u32[]{:S(2)}) collective-permute-start(bf16[32,1024]{1,0:T(8,128)(2,1)S(1)} %dynamic-slice_bitcast_fusion.6), channel_id=1, source_target_pairs={{0,4},{1,5},{2,6},{3,7},{4,0},{5,1},{6,2},{7,3},{8,12},{9,13},{10,... | collective-permute-start | bytes 196616 | tf_op jit(solution)/shard_map/ppermute | solution.py:80
  114.3 2.8 %collective-permute-done.12 = bf16[2,80,512]{2,1,0:T(8,128)(2,1)S(1)} collective-permute-done((bf16[2,80,512]{2,1,0:T(8,128)(2,1)S(1)}, bf16[2,80,512]{2,1,0:T(8,128)(2,1)S(1)}, u32[]{:S(2)}, u32[]{:S(2)}) %collective-permute-start.12) | collective-permute-done | bytes 163872 | tf_op jit(solution)/shard_map/ppermute | solution.py:80
  117.2 1.2 collective-permute-start.13
  118.4 2.3 %fusion.4 = bf16[512,1024]{1,0:T(8,128)(2,1)} fusion(bf16[1024,512]{0,1:T(8,128)(2,1)S(1)} %bitcast.146, bf16[1024,512]{0,1:T(8,128)(2,1)S(1)} %bitcast.145, bf16[512,512]{1,0:T(8,128)(2,1)S(1)} %collective-permute-done.6, bf16[512,512]{1,0:T(8,128)(2,1)S(1)} %get-tuple-element.16), kind=kOutput, calls=%fused_computation.6 | convolution fusion | flops 1080557568 | bytes 4194304 | tf_op jit(solution)/shard_map/dot_general | solution.py:21
  120.7 1.9 %collective-permute-done.13 = bf16[80,512]{1,0:T(8,128)(2,1)S(1)} collective-permute-done((bf16[80,512]{1,0:T(8,128)(2,1)S(1)}, bf16[80,512]{1,0:T(8,128)(2,1)S(1)}, u32[]{:S(2)}, u32[]{:S(2)}) %collective-permute-start.13) | collective-permute-done | bytes 81952 | tf_op jit(solution)/shard_map/ppermute | solution.py:80
  (119 shorter events, 15.8 us)
Async XLA Ops:
  0.6 28.4 %copy-start = (bf16[1024,1024]{1,0:T(8,128)(2,1)S(1)}, bf16[1024,1024]{1,0:T(8,128)(2,1)}, u32[]{:S(2)}) copy-start(bf16[1024,1024]{1,0:T(8,128)(2,1)} %param.13) | copy-start | bytes 6291460
  1.6 12.7 %collective-permute-start.2 = (bf16[1,16,1024]{2,1,0:T(8,128)(2,1)S(1)}, bf16[1,16,1024]{2,1,0:T(8,128)(2,1)S(1)}, u32[]{:S(2)}, u32[]{:S(2)}) collective-permute-start(bf16[1,16,1024]{2,1,0:T(8,128)(2,1)S(1)} %dynamic-slice_bitcast_fusion.8), channel_id=1, source_target_pairs={{0,1},{1,0},{2,3},{3,2},{4,5},{5,4},{6,7},{7,6},{8,9},{9,8},{10,11... | collective-permute-start | bytes 98312 | tf_op jit(solution)/shard_map/ppermute | solution.py:80
  4.6 33.9 %collective-permute-start = (bf16[512,1024]{1,0:T(8,128)(2,1)}, bf16[512,1024]{1,0:T(8,128)(2,1)}, u32[]{:S(2)}, u32[]{:S(2)}) collective-permute-start(bf16[512,1024]{1,0:T(8,128)(2,1)} %param.8), channel_id=1, source_target_pairs={{0,8},{1,9},{2,10},{3,11},{4,12},{5,13},{6,14},{7,15},{8,0},{9,1},... | collective-permute-start | bytes 3145736 | tf_op jit(solution)/shard_map/ppermute | solution.py:80
  4.6 38.3 %collective-permute-start.1 = (bf16[512,1024]{1,0:T(8,128)(2,1)}, bf16[512,1024]{1,0:T(8,128)(2,1)}, u32[]{:S(2)}, u32[]{:S(2)}) collective-permute-start(bf16[512,1024]{1,0:T(8,128)(2,1)} %param.15), channel_id=1, source_target_pairs={{0,8},{1,9},{2,10},{3,11},{4,12},{5,13},{6,14},{7,15},{8,0},{9,1},... | collective-permute-start | bytes 3145736 | tf_op jit(solution)/shard_map/ppermute | solution.py:80
  10.4 2.9 %copy-start.7 = (bf16[512,1024]{1,0:T(8,128)(2,1)S(1)}, bf16[512,1024]{1,0:T(8,128)(2,1)}, u32[]{:S(2)}) copy-start(bf16[512,1024]{1,0:T(8,128)(2,1)} %param.8) | copy-start | bytes 3145732
  14.3 12.0 %collective-permute-start.3 = (bf16[2,16,1024]{2,1,0:T(8,128)(2,1)S(1)}, bf16[2,16,1024]{2,1,0:T(8,128)(2,1)S(1)}, u32[]{:S(2)}, u32[]{:S(2)}) collective-permute-start(bf16[2,16,1024]{2,1,0:T(8,128)(2,1)S(1)} %pad_maximum_fusion.13), channel_id=1, source_target_pairs={{0,2},{1,3},{2,0},{3,1},{4,6},{5,7},{6,4},{7,5},{8,10},{9,11},{10,... | collective-permute-start | bytes 196616 | tf_op jit(solution)/shard_map/ppermute | solution.py:80
  26.3 9.0 %copy-start.1 = (bf16[1024,1024]{0,1:T(8,128)(2,1)S(1)}, bf16[1024,1024]{0,1:T(8,128)(2,1)}, u32[]{:S(2)}) copy-start(bf16[1024,1024]{0,1:T(8,128)(2,1)} %copy.21) | copy-start | bytes 6291460
  26.4 8.8 %collective-permute-start.4 = (bf16[4,16,1024]{2,1,0:T(8,128)(2,1)S(1)}, bf16[4,16,1024]{2,1,0:T(8,128)(2,1)S(1)}, u32[]{:S(2)}, u32[]{:S(2)}) collective-permute-start(bf16[4,16,1024]{2,1,0:T(8,128)(2,1)S(1)} %pad_maximum_fusion.11), channel_id=1, source_target_pairs={{0,4},{1,5},{2,6},{3,7},{4,0},{5,1},{6,2},{7,3},{8,12},{9,13},{10,... | collective-permute-start | bytes 393224 | tf_op jit(solution)/shard_map/ppermute | solution.py:80
  35.2 1.6 %collective-permute-start.5 = (bf16[8,16,1024]{2,1,0:T(8,128)(2,1)S(1)}, bf16[8,16,1024]{2,1,0:T(8,128)(2,1)S(1)}, u32[]{:S(2)}, u32[]{:S(2)}) collective-permute-start(bf16[8,16,1024]{2,1,0:T(8,128)(2,1)S(1)} %pad_maximum_fusion.10), channel_id=1, source_target_pairs={{0,8},{1,9},{2,10},{3,11},{4,12},{5,13},{6,14},{7,15},{8,0},{9,1},... | collective-permute-start | bytes 786440 | tf_op jit(solution)/shard_map/ppermute | solution.py:80
  36.9 2.4 %copy-start.10 = (bf16[1024,1024]{1,0:T(8,128)(2,1)S(1)}, bf16[1024,1024]{1,0:T(8,128)(2,1)}, u32[]{:S(2)}) copy-start(bf16[1024,1024]{1,0:T(8,128)(2,1)} %constant_dynamic-update-slice_fusion.1) | copy-start | bytes 6291460
  40.6 2.4 %copy-start.11 = (bf16[1024,1024]{1,0:T(8,128)(2,1)}, bf16[1024,1024]{1,0:T(8,128)(2,1)S(1)}, u32[]{:S(2)}) copy-start(bf16[1024,1024]{1,0:T(8,128)(2,1)S(1)} %constant_dynamic-update-slice_fusion) | copy-start | bytes 6291460
  40.6 2.5 %copy-start.12 = (bf16[1024,1024]{1,0:T(8,128)(2,1)S(1)}, bf16[1024,1024]{1,0:T(8,128)(2,1)}, u32[]{:S(2)}) copy-start(bf16[1024,1024]{1,0:T(8,128)(2,1)} %constant_dynamic-update-slice_fusion.3) | copy-start | bytes 6291460
  76.9 3.3 %copy-start.4 = (bf16[1024,2,1,256]{0,3,2,1:T(8,128)(2,1)S(1)}, bf16[1024,2,1,256]{0,3,2,1:T(8,128)(2,1)}, u32[]{:S(2)}) copy-start(bf16[1024,2,1,256]{0,3,2,1:T(8,128)(2,1)} %copy-done.3) | copy-start | bytes 3145732
  76.9 3.3 %copy-start.6 = (bf16[1024,2,1,256]{0,3,2,1:T(8,128)(2,1)S(1)}, bf16[1024,2,1,256]{0,3,2,1:T(8,128)(2,1)}, u32[]{:S(2)}) copy-start(bf16[1024,2,1,256]{0,3,2,1:T(8,128)(2,1)} %copy-done.5) | copy-start | bytes 3145732
  76.9 3.3 %copy-start.15 = (bf16[2,512,256]{2,1,0:T(8,128)(2,1)S(1)}, bf16[2,512,256]{2,1,0:T(8,128)(2,1)}, u32[]{:S(2)}) copy-start(bf16[2,512,256]{2,1,0:T(8,128)(2,1)} %get-tuple-element.11) | copy-start | bytes 1572868
  82.4 2.8 %copy-start.8 = (bf16[512,1024]{1,0:T(8,128)(2,1)S(1)}, bf16[512,1024]{1,0:T(8,128)(2,1)}, u32[]{:S(2)}) copy-start(bf16[512,1024]{1,0:T(8,128)(2,1)} %get-tuple-element.10) | copy-start | bytes 3145732
  82.5 10.5 %collective-permute-start.7 = (bf16[2,8,8,1024]{3,2,1,0:T(8,128)(2,1)S(1)}, bf16[2,8,8,1024]{3,2,1,0:T(8,128)(2,1)S(1)}, u32[]{:S(2)}, u32[]{:S(2)}) collective-permute-start(bf16[2,8,8,1024]{3,2,1,0:T(8,128)(2,1)S(1)} %dynamic-slice_bitcast_fusion), channel_id=1, source_target_pairs={{0,8},{1,9},{2,10},{3,11},{4,12},{5,13},{6,14},{7,15},{8,0},{9,1},... | collective-permute-start | bytes 786440 | tf_op jit(solution)/shard_map/ppermute | solution.py:80
  83.0 8.3 %collective-permute-start.17 = (bf16[2,2,2,32,512]{4,3,1,2,0:T(8,128)(2,1)S(1)}, bf16[2,2,2,32,512]{4,3,1,2,0:T(8,128)(2,1)S(1)}, u32[]{:S(2)}, u32[]{:S(2)}) collective-permute-start(bf16[2,2,2,32,512]{4,3,1,2,0:T(8,128)(2,1)S(1)} %bitcast.160), channel_id=1, source_target_pairs={{0,1},{1,0},{2,3},{3,2},{4,5},{5,4},{6,7},{7,6},{8,9},{9,8},{10,11... | collective-permute-start | bytes 786440 | tf_op jit(solution)/shard_map/ppermute | solution.py:80
  83.5 9.6 %collective-permute-start.15 = (bf16[2,2,2,32,512]{4,3,0,1,2:T(8,128)(2,1)S(1)}, bf16[2,2,2,32,512]{4,3,0,1,2:T(8,128)(2,1)S(1)}, u32[]{:S(2)}, u32[]{:S(2)}) collective-permute-start(bf16[2,2,2,32,512]{4,3,0,1,2:T(8,128)(2,1)S(1)} %bitcast.159), channel_id=1, source_target_pairs={{0,16},{1,17},{2,18},{3,19},{4,20},{5,21},{6,22},{7,23},{8,24},{9,... | collective-permute-start | bytes 786440 | tf_op jit(solution)/shard_map/ppermute | solution.py:80
  85.2 33.2 %collective-permute-start.6 = (bf16[512,512]{1,0:T(8,128)(2,1)S(1)}, bf16[512,512]{1,0:T(8,128)(2,1)S(1)}, u32[]{:S(2)}, u32[]{:S(2)}) collective-permute-start(bf16[512,512]{1,0:T(8,128)(2,1)S(1)} %get-tuple-element.17), channel_id=1, source_target_pairs={{0,8},{1,9},{2,10},{3,11},{4,12},{5,13},{6,14},{7,15},{8,0},{9,1},... | collective-permute-start | bytes 1572872 | tf_op jit(solution)/shard_map/ppermute | solution.py:80
  91.4 5.0 %collective-permute-start.18 = (bf16[2,2,32,512]{3,2,0,1:T(8,128)(2,1)S(1)}, bf16[2,2,32,512]{3,2,0,1:T(8,128)(2,1)S(1)}, u32[]{:S(2)}, u32[]{:S(2)}) collective-permute-start(bf16[2,2,32,512]{3,2,0,1:T(8,128)(2,1)S(1)} %dynamic-slice_bitcast_fusion.3), channel_id=1, source_target_pairs={{0,16},{1,17},{2,18},{3,19},{4,20},{5,21},{6,22},{7,23},{8,24},{9,... | collective-permute-start | bytes 393224 | tf_op jit(solution)/shard_map/ppermute | solution.py:80
  93.2 6.4 %collective-permute-start.16 = (bf16[2,2,32,512]{3,2,0,1:T(8,128)(2,1)S(1)}, bf16[2,2,32,512]{3,2,0,1:T(8,128)(2,1)S(1)}, u32[]{:S(2)}, u32[]{:S(2)}) collective-permute-start(bf16[2,2,32,512]{3,2,0,1:T(8,128)(2,1)S(1)} %dynamic-slice_bitcast_fusion.4), channel_id=1, source_target_pairs={{0,1},{1,0},{2,3},{3,2},{4,5},{5,4},{6,7},{7,6},{8,9},{9,8},{10,11... | collective-permute-start | bytes 393224 | tf_op jit(solution)/shard_map/ppermute | solution.py:80
  93.8 10.9 %collective-permute-start.10 = (bf16[2,2,2,80,256]{4,3,2,1,0:T(8,128)(2,1)S(1)}, bf16[2,2,2,80,256]{4,3,2,1,0:T(8,128)(2,1)S(1)}, u32[]{:S(2)}, u32[]{:S(2)}) collective-permute-start(bf16[2,2,2,80,256]{4,3,2,1,0:T(8,128)(2,1)S(1)} %fusion.22), channel_id=1, source_target_pairs={{0,1},{1,0},{2,3},{3,2},{4,5},{5,4},{6,7},{7,6},{8,9},{9,8},{10,11... | collective-permute-start | bytes 983048 | tf_op jit(solution)/shard_map/ppermute | solution.py:80
  95.4 10.0 %collective-permute-start.8 = (bf16[2,2,2,80,256]{4,3,1,0,2:T(8,128)(2,1)S(1)}, bf16[2,2,2,80,256]{4,3,1,0,2:T(8,128)(2,1)S(1)}, u32[]{:S(2)}, u32[]{:S(2)}) collective-permute-start(bf16[2,2,2,80,256]{4,3,1,0,2:T(8,128)(2,1)S(1)} %bitcast.158), channel_id=1, source_target_pairs={{0,16},{1,17},{2,18},{3,19},{4,20},{5,21},{6,22},{7,23},{8,24},{9,... | collective-permute-start | bytes 983048 | tf_op jit(solution)/shard_map/ppermute | solution.py:80
  99.7 11.3 %collective-permute-start.19 = (bf16[2,32,1024]{2,1,0:T(8,128)(2,1)S(1)}, bf16[2,32,1024]{2,1,0:T(8,128)(2,1)S(1)}, u32[]{:S(2)}, u32[]{:S(2)}) collective-permute-start(bf16[2,32,1024]{2,1,0:T(8,128)(2,1)S(1)} %fusion.36), channel_id=1, source_target_pairs={{0,2},{1,3},{2,0},{3,1},{4,6},{5,7},{6,4},{7,5},{8,10},{9,11},{10,... | collective-permute-start | bytes 393224 | tf_op jit(solution)/shard_map/ppermute | solution.py:80
  104.8 5.4 %collective-permute-start.11 = (bf16[2,2,80,256]{3,2,1,0:T(8,128)(2,1)S(1)}, bf16[2,2,80,256]{3,2,1,0:T(8,128)(2,1)S(1)}, u32[]{:S(2)}, u32[]{:S(2)}) collective-permute-start(bf16[2,2,80,256]{3,2,1,0:T(8,128)(2,1)S(1)} %dynamic-slice_bitcast_fusion.1), channel_id=1, source_target_pairs={{0,16},{1,17},{2,18},{3,19},{4,20},{5,21},{6,22},{7,23},{8,24},{9,... | collective-permute-start | bytes 491528 | tf_op jit(solution)/shard_map/ppermute | solution.py:80
  105.4 13.0 %copy-start.2 = (bf16[1024,2,1,256]{0,3,2,1:T(8,128)(2,1)S(1)}, bf16[1024,2,1,256]{0,3,2,1:T(8,128)(2,1)}, u32[]{:S(2)}) copy-start(bf16[1024,2,1,256]{0,3,2,1:T(8,128)(2,1)} %get-tuple-element.13) | copy-start | bytes 3145732
  105.5 5.4 %collective-permute-start.9 = (bf16[2,2,80,256]{3,2,1,0:T(8,128)(2,1)S(1)}, bf16[2,2,80,256]{3,2,1,0:T(8,128)(2,1)S(1)}, u32[]{:S(2)}, u32[]{:S(2)}) collective-permute-start(bf16[2,2,80,256]{3,2,1,0:T(8,128)(2,1)S(1)} %dynamic-slice_bitcast_fusion.2), channel_id=1, source_target_pairs={{0,1},{1,0},{2,3},{3,2},{4,5},{5,4},{6,7},{7,6},{8,9},{9,8},{10,11... | collective-permute-start | bytes 491528 | tf_op jit(solution)/shard_map/ppermute | solution.py:80
  111.0 6.2 %collective-permute-start.12 = (bf16[2,80,512]{2,1,0:T(8,128)(2,1)S(1)}, bf16[2,80,512]{2,1,0:T(8,128)(2,1)S(1)}, u32[]{:S(2)}, u32[]{:S(2)}) collective-permute-start(bf16[2,80,512]{2,1,0:T(8,128)(2,1)S(1)} %fusion.32), channel_id=1, source_target_pairs={{0,2},{1,3},{2,0},{3,1},{4,6},{5,7},{6,4},{7,5},{8,10},{9,11},{10,... | collective-permute-start | bytes 491528 | tf_op jit(solution)/shard_map/ppermute | solution.py:80
  111.1 11.6 %collective-permute-start.20 = (bf16[32,1024]{1,0:T(8,128)(2,1)S(1)}, bf16[32,1024]{1,0:T(8,128)(2,1)S(1)}, u32[]{:S(2)}, u32[]{:S(2)}) collective-permute-start(bf16[32,1024]{1,0:T(8,128)(2,1)S(1)} %dynamic-slice_bitcast_fusion.6), channel_id=1, source_target_pairs={{0,4},{1,5},{2,6},{3,7},{4,0},{5,1},{6,2},{7,3},{8,12},{9,13},{10,... | collective-permute-start | bytes 196616 | tf_op jit(solution)/shard_map/ppermute | solution.py:80
  117.2 5.4 %collective-permute-start.13 = (bf16[80,512]{1,0:T(8,128)(2,1)S(1)}, bf16[80,512]{1,0:T(8,128)(2,1)S(1)}, u32[]{:S(2)}, u32[]{:S(2)}) collective-permute-start(bf16[80,512]{1,0:T(8,128)(2,1)S(1)} %dynamic-slice_bitcast_fusion.5), channel_id=1, source_target_pairs={{0,4},{1,5},{2,6},{3,7},{4,0},{5,1},{6,2},{7,3},{8,12},{9,13},{10,... | collective-permute-start | bytes 245768 | tf_op jit(solution)/shard_map/ppermute | solution.py:80
  122.7 1.5 %collective-permute-start.14 = (f32[32,512]{1,0:T(8,128)S(1)}, f32[32,512]{1,0:T(8,128)S(1)}, u32[]{:S(2)}, u32[]{:S(2)}) collective-permute-start(f32[32,512]{1,0:T(8,128)S(1)} %get-tuple-element.31), channel_id=1, source_target_pairs={{0,8},{1,9},{2,10},{3,11},{4,12},{5,13},{6,14},{7,15},{8,0},{9,1},... | collective-permute-start | bytes 196616 | tf_op jit(solution)/shard_map/ppermute | solution.py:80
  (5 other events, 8.1 us)

commit v2 on v1

v2 whole, which is shorter than its diff:
```python
from functools import partial

import jax
import jax.numpy as jnp
from jax import lax
from jax.experimental import pallas as pl
from jax.experimental.pallas import tpu as pltpu
from jax.sharding import PartitionSpec as P

HEADS = 16
TVIEWS = 8
CVIEWS = 16
AXES = ("grp", "seq")

F32 = jnp.float32
BF16 = jnp.bfloat16


def dot(left, right, dims):
    return lax.dot_general(left, right, (dims, ((), ())), preferred_element_type=F32)


def query_kernel(core_ref, weight_ref, own_ref, partner_ref, out_ref):
    rows = own_ref.shape[0]
    weight = weight_ref[...]
    out_ref[:, :rows] = dot(own_ref[...], weight, ((1,), (0,))).astype(BF16).T
    out_ref[:, rows:] = dot(partner_ref[...], weight, ((1,), (0,))).astype(BF16).T


def grad_kernel(core_ref, weight_ref, own_ref, partner_ref, out_ref):
    rows = own_ref.shape[0]
    weight = weight_ref[...]
    out_ref[:, :rows] = dot(weight, own_ref[...], ((1,), (1,))).astype(BF16)
    out_ref[:, rows:] = dot(weight, partner_ref[...], ((1,), (1,))).astype(BF16)


def attend_kernel(
    heads,
    scale,
    core_ref,
    context_ref,
    wk_ref,
    wv_ref,
    q_ref,
    own_ref,
    partner_ref,
    bias_ref,
    kv_ref,
    probs_ref,
    att_ref,
    wo_ref,
):
    block_rows = own_ref.shape[0]
    keys = context_ref.shape[0]
    size = q_ref.shape[0] // heads
    context = context_ref[...]
    key_block = (dot(context, wk_ref[...], ((1,), (0,))).astype(BF16).astype(F32) * scale).astype(
        BF16
    )
    value_block = dot(context, wv_ref[...], ((1,), (0,))).astype(BF16)
    kv_ref[0] = key_block.T
    kv_ref[1] = value_block.T
    lane = lax.broadcasted_iota(jnp.int32, (keys, 2 * block_rows), 1)
    bias = jnp.where(lane < block_rows, bias_ref[0][:, :1], bias_ref[1][:, :1])
    for head in range(heads):
        part = pl.ds(head * size, size)
        scores = dot(kv_ref[0, part, :].T, q_ref[part, :], ((1,), (0,))) + bias
        row_max = jnp.max(scores, axis=0, keepdims=True)
        unnormed = jnp.exp(scores - row_max)
        row_sum = jnp.sum(unnormed, axis=0, keepdims=True)
        probs = (unnormed * (1.0 / row_sum)).astype(BF16)
        probs_ref[head] = probs
        att_ref[part, :] = dot(kv_ref[1, part, :], probs, ((1,), (0,))).astype(BF16)
    total = dot(att_ref[:, :block_rows], own_ref[...], ((1,), (0,)))
    total += dot(att_ref[:, block_rows:], partner_ref[...], ((1,), (0,)))
    wo_ref[...] = total.astype(BF16)


def back_kernel(
    heads,
    scale,
    core_ref,
    wk_ref,
    wv_ref,
    q_ref,
    g_ref,
    kv_ref,
    probs_ref,
    att_ref,
    own_ref,
    partner_ref,
    prior_ref,
    qg_own_ref,
    qg_partner_ref,
    wq_ref,
    ctx_ref,
):
    block_rows = own_ref.shape[0]
    size = q_ref.shape[0] // heads
    key_parts, value_parts = [], []
    for head in range(heads):
        part = pl.ds(head * size, size)
        grad = g_ref[part, :]
        probs = probs_ref[head]
        row_dot = jnp.sum(att_ref[part, :].astype(F32) * grad.astype(F32), axis=0, keepdims=True)
        grad_scores = dot(kv_ref[1, part, :].T, grad, ((1,), (0,)))
        value_parts.append(dot(grad, probs, ((1,), (1,))))
        logits = (probs.astype(F32) * (grad_scores - row_dot)).astype(BF16)
        query_grad = dot(kv_ref[0, part, :], logits, ((1,), (0,))).astype(BF16)
        qg_own_ref[part, :] = query_grad[:, :block_rows]
        qg_partner_ref[part, :] = query_grad[:, block_rows:]
        key_parts.append(dot(q_ref[part, :], logits, ((1,), (1,))) * scale)
    weight = dot(qg_own_ref[...], own_ref[...], ((1,), (0,)))
    weight += dot(qg_partner_ref[...], partner_ref[...], ((1,), (0,)))
    wq_ref[...] = weight.astype(BF16).T
    key_grad = jnp.concatenate(key_parts, axis=0).astype(BF16).T
    value_grad = jnp.concatenate(value_parts, axis=0).astype(BF16).T
    term = dot(key_grad, wk_ref[...], ((1,), (1,))) + dot(value_grad, wv_ref[...], ((1,), (1,)))

    @pl.when(pl.program_id(0) == 0)
    def _():
        ctx_ref[...] = prior_ref[...] + term

    @pl.when(pl.program_id(0) > 0)
    def _():
        ctx_ref[...] += term


def targets_kernel(core_ref, mine_ref, theirs_ref, wq_mine_ref, wq_theirs_ref, out_ref, acc_ref):
    term = dot(mine_ref[...], wq_mine_ref[...], ((0,), (1,)))
    term += dot(theirs_ref[...], wq_theirs_ref[...], ((0,), (1,)))
    step = pl.program_id(0)

    @pl.when(step == 0)
    def _():
        acc_ref[...] = term

    @pl.when(step > 0)
    def _():
        acc_ref[...] += term

    @pl.when(step == pl.num_programs(0) - 1)
    def _():
        out_ref[...] = acc_ref[...].astype(BF16)


def fixed(shape):
    return pl.BlockSpec(
        shape, lambda i, core: (0,) * len(shape), pipeline_mode=pl.Buffered(buffer_count=1)
    )


def call(kernel, name, steps, in_specs, out_specs, out_shape, flops, scratch=(), aliases=None):
    return pl.pallas_call(
        kernel,
        grid_spec=pltpu.PrefetchScalarGridSpec(
            num_scalar_prefetch=1,
            grid=(steps,),
            in_specs=in_specs,
            out_specs=out_specs,
            scratch_shapes=scratch,
        ),
        out_shape=out_shape,
        input_output_aliases=aliases or {},
        cost_estimate=pl.CostEstimate(flops=flops, bytes_accessed=4 << 20, transcendentals=0),
        name=name,
    )


def on_device(targets, context, w_query, w_key, w_value, w_out, visible, grad_out):
    query_rows, width = targets.shape
    head_size = width // HEADS
    score_scale = head_size ** (-0.5)
    grp_count = lax.axis_size("grp")
    seq_count = lax.axis_size("seq")
    device_count = grp_count * seq_count
    grp = lax.axis_index("grp")
    seq = lax.axis_index("seq")
    me = grp * seq_count + seq
    core = grp % 2
    core_mask = seq_count
    high_count = grp_count // 2
    half_width = width // 2
    block = width // grp_count
    context_rows = context.shape[0] * seq_count
    rows = 2 * query_rows
    core_index = core.reshape(1).astype(jnp.int32)

    def swap(array, mask):
        return lax.ppermute(array, AXES, [(i, i ^ mask) for i in range(device_count)])

    def bit_of(mask):
        return (me // mask) % 2

    def shaped(*shape, dtype=BF16):
        return jax.ShapeDtypeStruct(shape, dtype)

    own_half = context.shape[0] // 2
    held = lax.dynamic_slice_in_dim(context, core * own_half, own_half, 0)[None]
    targets_swapped = None
    mask = 1
    while mask < seq_count:
        with jax.named_scope(f"gather_{mask}"):
            other = swap(held, mask)
        if targets_swapped is None:
            with jax.named_scope("swap_targets"):
                targets_swapped = swap(targets, core_mask)
            with jax.named_scope("swap_grads"):
                grad_swapped = swap(grad_out, core_mask)
        upper = bit_of(mask) == 1
        held = jnp.concatenate(
            [jnp.where(upper, other, held), jnp.where(upper, held, other)], axis=0
        )
        mask *= 2
    with jax.named_scope("gather_core"):
        other = swap(held, core_mask)
    held = jnp.stack(
        [jnp.where(core == 1, other, held), jnp.where(core == 1, held, other)], axis=1
    )
    context_all = held.reshape(context_rows, width)

    product = 2 * half_width * rows * width
    row_block = fixed((query_rows, width))
    with jax.named_scope("project_q"):
        queries = call(
            query_kernel,
            "project_q",
            high_count,
            [
                pl.BlockSpec((width, block), lambda i, core: (0, 2 * i + core[0])),
                row_block,
                row_block,
            ],
            pl.BlockSpec((block, rows), lambda i, core: (i, 0)),
            shaped(half_width, rows),
            product,
        )(core_index, w_query, targets, targets_swapped)
    with jax.named_scope("project_g"):
        grads = call(
            grad_kernel,
            "project_g",
            high_count,
            [
                pl.BlockSpec((block, width), lambda i, core: (2 * i + core[0], 0)),
                row_block,
                row_block,
            ],
            pl.BlockSpec((block, rows), lambda i, core: (i, 0)),
            shaped(half_width, rows),
            product,
        )(core_index, w_out, grad_out, grad_swapped)

    view_rows = query_rows * device_count // TVIEWS
    context_view = context_rows // CVIEWS
    firsts = jnp.stack([me, me ^ core_mask]) * query_rows // view_rows
    view_hot = firsts[:, None] == jnp.arange(TVIEWS)
    seen = jnp.sum(jnp.where(view_hot[:, :, None], visible[None], 0), axis=1)
    key_hot = jnp.arange(context_rows)[:, None] // context_view == jnp.arange(CVIEWS)
    seen = jnp.sum(jnp.where(key_hot[None], seen[:, None, :], 0), axis=2)
    bias = jnp.where(seen == 1, 0.0, -1e30).astype(F32)
    bias = jnp.broadcast_to(bias[:, :, None], (2, context_rows, 128))

    step_heads = 128 // head_size
    step_width = step_heads * head_size
    per_block = block // step_width
    steps = half_width // step_width

    def weight_spec(offset):
        def index(i, core):
            at = i + offset
            return (0, (2 * (at // per_block) + core[0]) * per_block + at % per_block)

        return pl.BlockSpec((width, step_width), index)

    def head_spec(offset):
        return pl.BlockSpec((step_width, rows), lambda i, core: (i + offset, 0))

    def kv_spec(offset):
        return pl.BlockSpec((2, step_width, context_rows), lambda i, core: (0, i + offset, 0))

    def probs_spec(offset):
        return pl.BlockSpec((step_heads, context_rows, rows), lambda i, core: (i + offset, 0, 0))

    attention = 8 * half_width * rows * context_rows
    with jax.named_scope("attend"):
        key_values, probs, attended, wo_term = call(
            partial(attend_kernel, step_heads, score_scale),
            "attend",
            steps,
            [
                fixed((context_rows, width)),
                weight_spec(0),
                weight_spec(0),
                head_spec(0),
                row_block,
                row_block,
                fixed((2, context_rows, 128)),
            ],
            [
                kv_spec(0),
                probs_spec(0),
                head_spec(0),
                pl.BlockSpec((step_width, width), lambda i, core: (i, 0)),
            ],
            [
                shaped(2, half_width, context_rows),
                shaped(half_width // head_size, context_rows, rows),
                shaped(half_width, rows),
                shaped(half_width, width),
            ],
            product + attention,
        )(core_index, context_all, w_key, w_value, queries, grad_out, grad_swapped, bias)

    def back(part, prior, earlier):
        offset = part * per_block
        qg_spec = pl.BlockSpec((step_width, query_rows), lambda i, core: (i + offset, 0))
        in_specs = [
            weight_spec(offset),
            weight_spec(offset),
            head_spec(offset),
            head_spec(offset),
            kv_spec(offset),
            probs_spec(offset),
            head_spec(offset),
            row_block,
            row_block,
            fixed((context_rows, width)),
        ]
        operands = [
            core_index,
            w_key,
            w_value,
            queries,
            grads,
            key_values,
            probs,
            attended,
            targets,
            targets_swapped,
            prior,
        ]
        kernel = partial(back_kernel, step_heads, score_scale)
        aliases = {}
        if earlier is not None:
            inner = kernel

            def kernel(*refs):
                return inner(*refs[:11], *refs[13:])

            in_specs = in_specs + [pl.BlockSpec(memory_space=pl.ANY)] * 2
            operands = operands + list(earlier)
            aliases = {11: 0, 12: 1}
        return call(
            kernel,
            "back",
            per_block,
            in_specs,
            [
                qg_spec,
                qg_spec,
                pl.BlockSpec((width, step_width), lambda i, core: (0, i)),
                pl.BlockSpec((context_rows, width), lambda i, core: (0, 0)),
            ],
            [
                shaped(half_width, query_rows),
                shaped(half_width, query_rows),
                shaped(width, block),
                shaped(context_rows, width, dtype=F32),
            ],
            (product + attention) // high_count,
            aliases=aliases,
        )(*operands)

    high_masks = []
    mask = core_mask * high_count
    while mask > core_mask:
        high_masks.append(mask)
        mask //= 2
    seq_masks = []
    mask = seq_count // 2
    while mask >= 1:
        seq_masks.append(mask)
        mask //= 2
    all_masks = high_masks + seq_masks
    orders = [(high_masks[-1], seq_masks[-1]), (seq_masks[-1], high_masks[-1])]
    rest = seq_masks[-2::-1] + high_masks[:-1]
    high_bits = [2] * len(high_masks)
    seq_bits = [2] * len(seq_masks)

    def halve(array, masks, mask, label, last=False):
        axis = masks.index(mask)
        bit = bit_of(mask)
        sent = lax.dynamic_index_in_dim(array, 1 - bit, axis, keepdims=False)
        kept = lax.dynamic_index_in_dim(array, bit, axis, keepdims=False)
        with jax.named_scope(label):
            moved = swap(sent, mask)
        total = kept.astype(F32) + moved.astype(F32)
        left = masks[:axis] + masks[axis + 1 :]
        return (total if last else total.astype(BF16)), left

    def halve_twice(array, masks, which, label):
        for step, mask in enumerate(orders[which]):
            array, masks = halve(array, masks, mask, f"{label}_{step}")
        return array, masks

    def halve_rest(array, masks, label):
        for step, mask in enumerate(rest):
            array, masks = halve(array, masks, mask, f"{label}_{step}", step == len(rest) - 1)
        return array

    out_rows = width // device_count
    ctx_out = context_rows // device_count

    wo_split = wo_term.reshape(*high_bits, *seq_bits, out_rows, width)
    wo_one, masks = halve_twice(wo_split[..., :half_width], all_masks, 0, "wo_a")
    wo_two, _ = halve_twice(wo_split[..., half_width:], all_masks, 1, "wo_b")
    grad_wo = halve_rest(jnp.concatenate([wo_one, wo_two], axis=-1), masks, "wo")

    ctx_term = jnp.zeros((context_rows, width), F32)
    query_parts = None
    wq_parts = []
    core_masks = high_masks + [0] + seq_masks
    for part in range(high_count):
        with jax.named_scope(f"back_{part}"):
            *query_parts, wq_term, ctx_term = back(part, ctx_term, query_parts)
        wq_split = wq_term.reshape(*high_bits, 2, *seq_bits, out_rows, block)
        wq_part, wq_masks = halve_twice(wq_split, core_masks, part % 2, f"wq_{part}")
        wq_parts.append(wq_part)

    ctx_split = ctx_term.reshape(high_count, 2, seq_count, ctx_out, width)
    ctx_kept = lax.dynamic_index_in_dim(ctx_split, core, 1, keepdims=False)
    ctx_sent = lax.dynamic_index_in_dim(ctx_split, 1 - core, 1, keepdims=False).astype(BF16)
    with jax.named_scope("ctx_core"):
        ctx_moved = swap(ctx_sent, core_mask)
    ctx_pair = (ctx_kept + ctx_moved.astype(F32)).astype(BF16)
    ctx_pair = ctx_pair.reshape(*high_bits, *seq_bits, ctx_out, width)
    ctx_pair, masks = halve_twice(ctx_pair, all_masks, 0, "ctx")
    ctx_pair = jnp.moveaxis(ctx_pair.reshape(*ctx_pair.shape[:-1], 2, half_width), -2, 0)
    ctx_pair = jnp.moveaxis(ctx_pair, 0, len(high_masks) - 1)
    tail = jnp.concatenate([jnp.concatenate(wq_parts, axis=-1), ctx_pair], axis=-2)
    tail = halve_rest(tail, wq_masks, "tail")

    mine = lax.dynamic_index_in_dim(tail[:, :out_rows], core, 0, keepdims=False)
    sent = lax.dynamic_index_in_dim(tail[:, :out_rows], 1 - core, 0, keepdims=False)
    with jax.named_scope("wq_core"):
        theirs = swap(sent, core_mask)
    pieces = []
    for part in range(high_count):
        cut = slice(part * block, (part + 1) * block)
        pieces.append(jnp.where(core == 0, mine[:, cut], theirs[:, cut]))
        pieces.append(jnp.where(core == 0, theirs[:, cut], mine[:, cut]))
    grad_wq = jnp.concatenate(pieces, axis=1)
    d_context = jnp.concatenate([tail[0, out_rows:], tail[1, out_rows:]], axis=1).astype(BF16)

    with jax.named_scope("query_core"):
        returned = swap(query_parts[1], core_mask)
    with jax.named_scope("targets_out"):
        d_targets = call(
            targets_kernel,
            "targets_out",
            high_count,
            [
                pl.BlockSpec((block, query_rows), lambda i, core: (i, 0)),
                pl.BlockSpec((block, query_rows), lambda i, core: (i, 0)),
                pl.BlockSpec((width, block), lambda i, core: (0, 2 * i + core[0])),
                pl.BlockSpec((width, block), lambda i, core: (0, 2 * i + 1 - core[0])),
            ],
            fixed((query_rows, width)),
            shaped(query_rows, width),
            product,
            scratch=[pltpu.VMEM((query_rows, width), F32)],
        )(core_index, query_parts[0], returned, w_query, w_query)
    return (d_targets, d_context, grad_wq, grad_wo)


def solution(mesh):
    in_specs = (
        P(AXES, None),
        P("seq", None),
        P(),
        P(),
        P(),
        P(),
        P(),
        P(AXES, None),
    )
    out_specs = (P(AXES, None), P(AXES, None), P(AXES, None), P(AXES, None))
    return jax.shard_map(
        on_device, mesh=mesh, in_specs=in_specs, out_specs=out_specs, check_vma=False
    )
```

time: 126 us -> 107 us (0.85)
  local copies, waits for them, and re-layouts: 29.5 us -> 9.74 us
  matrix products: 16.6 us -> 0 us
  Pallas kernels: 25.3 us -> 40 us
  waiting for transfers between devices: 29.6 us -> 21.8 us
  starting transfers between devices: 21.1 us -> 28 us
  other arithmetic: 1.96 us -> 5.49 us
    dot_general x7 -> x0, matrix products: 16.6 us -> none  [dot(): lax.dot_general(left, right, (dims, ((), ())), preferred_element_type=F32)]
    unnamed x40 -> x12, local copies, waits for them, and re-layouts: 17.4 us -> 1.94 us
    pallas_call x2 -> x6, Pallas kernels: 25.3 us -> 40 us  [the longest x2 16.1 us: back(): call(kernel, 'back', per_block, in_specs, [qg_spec, qg_spec, pl.BlockSpec...]
    ppermute x21 -> x23, waiting for transfers between devices: 29.6 us -> 21.8 us  [swap(): lax.ppermute(array, AXES, [(i, i ^ mask) for i in range(device_count)])]
    ppermute x21 -> x23, starting transfers between devices: 21.1 us -> 28 us  [swap(): lax.ppermute(array, AXES, [(i, i ^ mask) for i in range(device_count)])]
    dynamic_slice x4 -> x2, local copies, waits for them, and re-layouts: 4.35 us -> 0.04 us  [halve(): sent = lax.dynamic_index_in_dim(array, 1 - bit, axis, keepdims=False)]
    concatenate x2 -> x0, local copies, waits for them, and re-layouts: 2.59 us -> none  [the longest x1 1.29 us: on_device(): grad_two = jnp.concatenate([grad_out, swap(grad_out, core_mask)], axis=0)]
    dynamic_slice x3 -> x4, local copies, waits for them, and re-layouts: 0.13 us -> 2.28 us  [halve(): kept = lax.dynamic_index_in_dim(array, bit, axis, keepdims=False)]
  transfers between devices with their start and end apart: 21 -> 23, of which waited for: 10 -> 10; matrix products, arithmetic and copies ran while one was open for 25% -> 9% of each run, Pallas kernels for 0% -> 27%
where the time goes in v2:
time: 107 us; the launch traced here: 106 us
  Pallas kernels  40 us (37%)
  starting transfers between devices  28 us (26%)
  waiting for transfers between devices  21.8 us (20%)
  local copies, waits for them, and re-layouts  9.74 us (9%)
  other arithmetic  5.49 us (5%)
  between operations  1.17 us (1%)
    ppermute x23, starting transfers between devices, swap(): lax.ppermute(array, AXES, [(i, i ^ mask) for i in range(device_count)])  28 us
    ppermute x23, waiting for transfers between devices, swap(): lax.ppermute(array, AXES, [(i, i ^ mask) for i in range(device_count)])  21.8 us
    pallas_call x2, Pallas kernels, back(): call(kernel, 'back', per_block, in_specs, [qg_spec, qg_spec, pl.BlockSpec...  16.1 us
    pallas_call x1, Pallas kernels, on_device(): call(partial(attend_kernel, step_heads, score_scale), 'attend', steps, [f...  11.4 us
    pallas_call x1, Pallas kernels, on_device(): call(targets_kernel, 'targets_out', high_count, [pl.BlockSpec((block, que...  4.29 us
    pallas_call x1, Pallas kernels, on_device(): call(query_kernel, 'project_q', high_count, [pl.BlockSpec((width, block),...  4.14 us
    pallas_call x1, Pallas kernels, on_device(): call(grad_kernel, 'project_g', high_count, [pl.BlockSpec((block, width),...  4 us
    dynamic_slice x4, local copies, waits for them, and re-layouts, halve(): kept = lax.dynamic_index_in_dim(array, bit, axis, keepdims=False)  2.28 us
  transfers between devices with their start and end apart: 23, of which 10 were waited for; matrix products, arithmetic and copies ran while one was open for 9% of the time, Pallas kernels for 27%

profile of v2, /device:TPU:0, one launch (start us, length us, event | category | flops | bytes accessed | tf_op | source)
XLA Modules:
  0.0 106.1 jit_solution(194114402110915353)
XLA Ops:
  1.4 3.0 %collective-permute-start.2 = (bf16[1,16,1024]{2,1,0:T(8,128)(2,1)S(1)}, bf16[1,16,1024]{2,1,0:T(8,128)(2,1)S(1)}, u32[]{:S(2)}, u32[]{:S(2)}) collective-permute-start(bf16[1,16,1024]{2,1,0:T(8,128)(2,1)S(1)} %dynamic-slice_bitcast_fusion.11), channel_id=1, source_target_pairs={{0,1},{1,0},{2,3},{3,2},{4,5},{5,4},{6,7},{7,6},{8,9},{9,8},{10,11... | collective-permute-start | bytes 98312 | tf_op jit(solution)/shard_map/gather_1/ppermute | solution.py:190
  5.0 1.3 %collective-permute-done.2 = bf16[1,16,1024]{2,1,0:T(8,128)(2,1)S(1)} collective-permute-done((bf16[1,16,1024]{2,1,0:T(8,128)(2,1)S(1)}, bf16[1,16,1024]{2,1,0:T(8,128)(2,1)S(1)}, u32[]{:S(2)}, u32[]{:S(2)}) %collective-permute-start.2) | collective-permute-done | bytes 32800 | tf_op jit(solution)/shard_map/gather_1/ppermute | solution.py:190
  7.1 2.1 %collective-permute-start.3 = (bf16[2,16,1024]{2,1,0:T(8,128)(2,1)S(1)}, bf16[2,16,1024]{2,1,0:T(8,128)(2,1)S(1)}, u32[]{:S(2)}, u32[]{:S(2)}) collective-permute-start(bf16[2,16,1024]{2,1,0:T(8,128)(2,1)S(1)} %pad_maximum_fusion.5), channel_id=1, source_target_pairs={{0,2},{1,3},{2,0},{3,1},{4,6},{5,7},{6,4},{7,5},{8,10},{9,11},{10,... | collective-permute-start | bytes 196616 | tf_op jit(solution)/shard_map/gather_2/ppermute | solution.py:190
  9.3 2.2 %collective-permute-done.3 = bf16[2,16,1024]{2,1,0:T(8,128)(2,1)S(1)} collective-permute-done((bf16[2,16,1024]{2,1,0:T(8,128)(2,1)S(1)}, bf16[2,16,1024]{2,1,0:T(8,128)(2,1)S(1)}, u32[]{:S(2)}, u32[]{:S(2)}) %collective-permute-start.3) | collective-permute-done | bytes 65568 | tf_op jit(solution)/shard_map/gather_2/ppermute | solution.py:190
  11.5 3.1 %collective-permute-start.4 = (bf16[4,16,1024]{2,1,0:T(8,128)(2,1)S(1)}, bf16[4,16,1024]{2,1,0:T(8,128)(2,1)S(1)}, u32[]{:S(2)}, u32[]{:S(2)}) collective-permute-start(bf16[4,16,1024]{2,1,0:T(8,128)(2,1)S(1)} %pad_maximum_fusion.3), channel_id=1, source_target_pairs={{0,4},{1,5},{2,6},{3,7},{4,0},{5,1},{6,2},{7,3},{8,12},{9,13},{10,... | collective-permute-start | bytes 393224 | tf_op jit(solution)/shard_map/gather_4/ppermute | solution.py:190
  15.5 2.1 %collective-permute-done.4 = bf16[4,16,1024]{2,1,0:T(8,128)(2,1)S(1)} collective-permute-done((bf16[4,16,1024]{2,1,0:T(8,128)(2,1)S(1)}, bf16[4,16,1024]{2,1,0:T(8,128)(2,1)S(1)}, u32[]{:S(2)}, u32[]{:S(2)}) %collective-permute-start.4) | collective-permute-done | bytes 131104 | tf_op jit(solution)/shard_map/gather_4/ppermute | solution.py:190
  17.9 1.4 %collective-permute-done.5 = bf16[8,16,1024]{2,1,0:T(8,128)(2,1)S(1)} collective-permute-done((bf16[8,16,1024]{2,1,0:T(8,128)(2,1)S(1)}, bf16[8,16,1024]{2,1,0:T(8,128)(2,1)S(1)}, u32[]{:S(2)}, u32[]{:S(2)}) %collective-permute-start.5) | collective-permute-done | bytes 262176 | tf_op jit(solution)/shard_map/gather_core/ppermute | solution.py:190
  19.3 0.9 pad_maximum_fusion
  20.2 1.0 copy-done
  21.1 4.1 %project_q.1.q_ref.refs_3_ = bf16[512,1024]{1,0:T(8,128)(2,1)} custom-call(s32[1]{0:T(128)} %bitcast.core_ref.refs_0_, bf16[1024,1024]{1,0:T(8,128)(2,1)} %wq_theirs_ref.1, bf16[512,1024]{1,0:T(8,128)(2,1)} %refs_8_.1, bf16[512,1024]{1,0:T(8,128)(2,1)} %copy-done), custom_call_target="tpu_custom_call" | custom-call | flops 1073741824 | bytes 4194304 | tf_op jit(solution)/shard_map/project_q/project_q/pallas_call | solution.py:225
  25.3 1.0 broadcast_in_dim.77.bias_ref
  26.4 11.4 %attend.1 = (bf16[2,512,256]{2,1,0:T(8,128)(2,1)}, bf16[8,256,1024]{2,1,0:T(8,128)(2,1)}, bf16[512,1024]{1,0:T(8,128)(2,1)}, bf16[512,1024]{1,0:T(8,128)(2,1)}) custom-call(s32[1]{0:T(128)} %bitcast.core_ref.refs_0_, bf16[256,1024]{1,0:T(8,128)(2,1)} %bitcast.125, bf16[1024,1024]{1,0:T(8,128)(2,1)} %refs_1_.1, bf16[1024,1024]{1,0:T(8,128)(2,1)} %refs_2_.1, ...), custom_call_target="tpu_custom_call" | custom-call | flops 2147483648 | bytes 4194304 | tf_op jit(solution)/shard_map/attend/attend/pallas_call | solution.py:286
  37.8 1.3 %fusion.19 = (bf16[2,2,2,2,32,512]{5,4,3,2,1,0:T(8,128)(2,1)S(1)}, bf16[2,2,2,2,32,512]{5,4,3,2,1,0:T(8,128)(2,1)S(1)}) fusion(bf16[2,2,2,2,32,1024]{5,4,3,2,1,0:T(8,128)(2,1)} %bitcast.126), kind=kLoop, calls=%fused_computation.102 | loop fusion | bytes 2097152 | tf_op jit(solution)/shard_map/slice | solution.py:416
  39.2 3.3 %collective-permute-start.19 = (bf16[2,2,2,32,512]{4,3,1,2,0:T(8,128)(2,1)S(1)}, bf16[2,2,2,32,512]{4,3,1,2,0:T(8,128)(2,1)S(1)}, u32[]{:S(2)}, u32[]{:S(2)}) collective-permute-start(bf16[2,2,2,32,512]{4,3,1,2,0:T(8,128)(2,1)S(1)} %bitcast.134), channel_id=1, source_target_pairs={{0,1},{1,0},{2,3},{3,2},{4,5},{5,4},{6,7},{7,6},{8,9},{9,8},{10,11... | collective-permute-start | bytes 786440 | tf_op jit(solution)/shard_map/wo_b_0/ppermute | solution.py:190
  42.6 1.6 %collective-permute-start.17 = (bf16[2,2,2,32,512]{4,3,0,1,2:T(8,128)(2,1)S(1)}, bf16[2,2,2,32,512]{4,3,0,1,2:T(8,128)(2,1)S(1)}, u32[]{:S(2)}, u32[]{:S(2)}) collective-permute-start(bf16[2,2,2,32,512]{4,3,0,1,2:T(8,128)(2,1)S(1)} %bitcast.133), channel_id=1, source_target_pairs={{0,16},{1,17},{2,18},{3,19},{4,20},{5,21},{6,22},{7,23},{8,24},{9,... | collective-permute-start | bytes 786440 | tf_op jit(solution)/shard_map/wo_a_0/ppermute | solution.py:190
  44.1 4.0 %project_g.1.g_ref.refs_4_ = bf16[512,1024]{1,0:T(8,128)(2,1)} custom-call(s32[1]{0:T(128)} %bitcast.core_ref.refs_0_, bf16[1024,1024]{1,0:T(8,128)(2,1)} %weight_ref.3, bf16[512,1024]{1,0:T(8,128)(2,1)} %own_ref.6, bf16[512,1024]{1,0:T(8,128)(2,1)} %copy-done.1), custom_call_target="tpu_custom_call" | custom-call | flops 1073741824 | bytes 4194304 | tf_op jit(solution)/shard_map/project_g/project_g/pallas_call | solution.py:239
  48.1 1.1 %broadcast_in_dim.78.prior_ref = f32[256,1024]{1,0:T(8,128)} broadcast(f32[]{:T(128)} %constant.267.clone.1), dimensions={} | broadcast | bytes 1048580 | tf_op jit(solution)/shard_map/broadcast_in_dim | solution.py:419
  49.2 8.1 %back.2 = (bf16[512,512]{1,0:T(8,128)(2,1)}, bf16[512,512]{1,0:T(8,128)(2,1)}, bf16[1024,256]{1,0:T(8,128)(2,1)}, f32[256,1024]{1,0:T(8,128)}) custom-call(s32[1]{0:T(128)} %bitcast.core_ref.refs_0_, bf16[1024,1024]{1,0:T(8,128)(2,1)} %refs_1_.1, bf16[1024,1024]{1,0:T(8,128)(2,1)} %refs_2_.1, bf16[512,1024]{1,0:T(8,128)(2,1)} %project_q.1.q_ref.refs_3_, ...), custom_call_target="tpu_custom_call" | custom-call | flops 1073741824 | bytes 4194304 | tf_op jit(solution)/shard_map/back_0/back/pallas_call | solution.py:353
  57.3 1.1 %constant_dynamic-slice_fusion.7 = (bf16[1,2,2,2,2,32,256]{6,5,4,3,2,1,0:T(8,128)(2,1)S(1)}, bf16[1,2,2,2,2,32,256]{6,5,4,3,2,1,0:T(8,128)(2,1)S(1)}) fusion(bf16[2,2,2,2,2,32,256]{6,5,4,3,2,1,0:T(8,128)(2,1)} %bitcast.132, s32[]{:T(128)S(6)} %select_n.273, s32[]{:T(128)S(6)} %select_n.274), kind=kLoop, calls=%fused_computation.86 | loop fusion | bytes 1048584 | tf_op jit(solution)/shard_map/jit(dynamic_index_in_dim)/dynamic_slice | solution.py:394
  59.0 8.1 %back.3 = (bf16[512,512]{1,0:T(8,128)(2,1)}, bf16[512,512]{1,0:T(8,128)(2,1)}, bf16[1024,256]{1,0:T(8,128)(2,1)}, f32[256,1024]{1,0:T(8,128)}) custom-call(s32[1]{0:T(128)} %bitcast.core_ref.refs_0_, bf16[1024,1024]{1,0:T(8,128)(2,1)} %refs_1_.1, bf16[1024,1024]{1,0:T(8,128)(2,1)} %refs_2_.1, ...), custom_call_target="tpu_custom_call", output_to_operand_aliasing={{0}: (11, {}), {1}: (12, {})} | custom-call | flops 1073741824 | bytes 4194304 | tf_op jit(solution)/shard_map/back_1/back/pallas_call | solution.py:353
  67.1 1.1 %constant_dynamic-slice_fusion.5 = (bf16[2,2,2,2,1,32,256]{6,5,4,3,2,1,0:T(8,128)(2,1)S(1)}, bf16[2,2,2,2,1,32,256]{6,5,4,3,2,1,0:T(8,128)(2,1)S(1)}) fusion(bf16[2,2,2,2,2,32,256]{6,5,4,3,2,1,0:T(8,128)(2,1)} %bitcast.131, s32[]{:T(128)S(6)} %select_n.275, s32[]{:T(128)S(6)} %select_n.276), kind=kLoop, calls=%fused_computation.84 | loop fusion | bytes 1048584 | tf_op jit(solution)/shard_map/jit(dynamic_index_in_dim)/dynamic_slice | solution.py:394
  68.4 1.1 %fusion.6 = bf16[2,8,8,1024]{3,2,1,0:T(8,128)(2,1)S(1)} fusion(f32[2,2,8,8,1024]{4,3,2,1,0:T(8,128)} %bitcast.129, s32[]{:T(128)S(6)} %select_n.278), kind=kLoop, calls=%fused_computation.19 | loop fusion | bytes 524292 | tf_op jit(solution)/shard_map/convert_element_type | solution.py:432
  70.2 2.0 %collective-permute-start.20 = (bf16[2,2,32,512]{3,2,0,1:T(8,128)(2,1)S(1)}, bf16[2,2,32,512]{3,2,0,1:T(8,128)(2,1)S(1)}, u32[]{:S(2)}, u32[]{:S(2)}) collective-permute-start(bf16[2,2,32,512]{3,2,0,1:T(8,128)(2,1)S(1)} %dynamic-slice_bitcast_fusion.1), channel_id=1, source_target_pairs={{0,16},{1,17},{2,18},{3,19},{4,20},{5,21},{6,22},{7,23},{8,24},{9,... | collective-permute-start | bytes 393224 | tf_op jit(solution)/shard_map/wo_b_1/ppermute | solution.py:190
  72.3 1.6 %collective-permute-start.18 = (bf16[2,2,32,512]{3,2,0,1:T(8,128)(2,1)S(1)}, bf16[2,2,32,512]{3,2,0,1:T(8,128)(2,1)S(1)}, u32[]{:S(2)}, u32[]{:S(2)}) collective-permute-start(bf16[2,2,32,512]{3,2,0,1:T(8,128)(2,1)S(1)} %dynamic-slice_bitcast_fusion.2), channel_id=1, source_target_pairs={{0,1},{1,0},{2,3},{3,2},{4,5},{5,4},{6,7},{7,6},{8,9},{9,8},{10,11... | collective-permute-start | bytes 393224 | tf_op jit(solution)/shard_map/wo_a_1/ppermute | solution.py:190
  74.0 3.0 %collective-permute-done.9 = bf16[2,2,2,2,32,256]{5,4,1,2,3,0:T(8,128)(2,1)S(1)} collective-permute-done((bf16[2,2,2,2,32,256]{5,4,1,2,3,0:T(8,128)(2,1)S(1)}, bf16[2,2,2,2,32,256]{5,4,1,2,3,0:T(8,128)(2,1)S(1)}, u32[]{:S(2)}, u32[]{:S(2)}) %collective-permute-start.9) | collective-permute-done | bytes 262176 | tf_op jit(solution)/shard_map/wq_1_0/ppermute | solution.py:190
  77.1 2.1 %collective-permute-start.10 = (bf16[2,2,2,32,256]{4,3,0,1,2:T(8,128)(2,1)S(1)}, bf16[2,2,2,32,256]{4,3,0,1,2:T(8,128)(2,1)S(1)}, u32[]{:S(2)}, u32[]{:S(2)}) collective-permute-start(bf16[2,2,2,32,256]{4,3,0,1,2:T(8,128)(2,1)S(1)} %dynamic-slice_bitcast_fusion.4), channel_id=1, source_target_pairs={{0,16},{1,17},{2,18},{3,19},{4,20},{5,21},{6,22},{7,23},{8,24},{9,... | collective-permute-start | bytes 393224 | tf_op jit(solution)/shard_map/wq_1_1/ppermute | solution.py:190
  80.6 3.8 %collective-permute-done.12 = bf16[2,2,2,8,1024]{4,3,2,1,0:T(8,128)(2,1)S(1)} collective-permute-done((bf16[2,2,2,8,1024]{4,3,2,1,0:T(8,128)(2,1)S(1)}, bf16[2,2,2,8,1024]{4,3,2,1,0:T(8,128)(2,1)S(1)}, u32[]{:S(2)}, u32[]{:S(2)}) %collective-permute-start.12) | collective-permute-done | bytes 131104 | tf_op jit(solution)/shard_map/ctx_0/ppermute | solution.py:190
  84.4 2.1 %collective-permute-start.13 = (bf16[2,2,8,1024]{3,2,1,0:T(8,128)(2,1)S(1)}, bf16[2,2,8,1024]{3,2,1,0:T(8,128)(2,1)S(1)}, u32[]{:S(2)}, u32[]{:S(2)}) collective-permute-start(bf16[2,2,8,1024]{3,2,1,0:T(8,128)(2,1)S(1)} %dynamic-slice_bitcast_fusion.10), channel_id=1, source_target_pairs={{0,1},{1,0},{2,3},{3,2},{4,5},{5,4},{6,7},{7,6},{8,9},{9,8},{10,11... | collective-permute-start | bytes 196616 | tf_op jit(solution)/shard_map/ctx_1/ppermute | solution.py:190
  86.6 2.1 %collective-permute-done.13 = bf16[2,2,8,1024]{3,2,1,0:T(8,128)(2,1)S(1)} collective-permute-done((bf16[2,2,8,1024]{3,2,1,0:T(8,128)(2,1)S(1)}, bf16[2,2,8,1024]{3,2,1,0:T(8,128)(2,1)S(1)}, u32[]{:S(2)}, u32[]{:S(2)}) %collective-permute-start.13) | collective-permute-done | bytes 65568 | tf_op jit(solution)/shard_map/ctx_1/ppermute | solution.py:190
  89.7 3.4 %collective-permute-start.22 = (bf16[32,1024]{1,0:T(8,128)(2,1)S(1)}, bf16[32,1024]{1,0:T(8,128)(2,1)S(1)}, u32[]{:S(2)}, u32[]{:S(2)}) collective-permute-start(bf16[32,1024]{1,0:T(8,128)(2,1)S(1)} %dynamic-slice_bitcast_fusion.7), channel_id=1, source_target_pairs={{0,4},{1,5},{2,6},{3,7},{4,0},{5,1},{6,2},{7,3},{8,12},{9,13},{10,... | collective-permute-start | bytes 196616 | tf_op jit(solution)/shard_map/wo_1/ppermute | solution.py:190
  93.9 4.3 %targets_out.1 = bf16[512,1024]{1,0:T(8,128)(2,1)} custom-call(s32[1]{0:T(128)} %bitcast.core_ref.refs_0_, bf16[512,512]{1,0:T(8,128)(2,1)} %get-tuple-element.22.mine_ref, bf16[512,512]{1,0:T(8,128)(2,1)} %copy-done.3, bf16[1024,1024]{1,0:T(8,128)(2,1)} %wq_theirs_ref.1, bf16[1024,1024]{1,0:T(8,128)(2,1)} %wq_theirs_ref.1), custom_call_target="tpu_custom_call" | custom-call | flops 1073741824 | bytes 4194304 | tf_op jit(solution)/shard_map/targets_out/targets_out/pallas_call | solution.py:458
  99.1 5.0 %collective-permute-done.15 = bf16[2,40,512]{2,1,0:T(8,128)(2,1)S(1)} collective-permute-done((bf16[2,40,512]{2,1,0:T(8,128)(2,1)S(1)}, bf16[2,40,512]{2,1,0:T(8,128)(2,1)S(1)}, u32[]{:S(2)}, u32[]{:S(2)}) %collective-permute-start.15) | collective-permute-done | bytes 81952 | tf_op jit(solution)/shard_map/tail_1/ppermute | solution.py:190
  (92 shorter events, 11.3 us)
Async XLA Ops:
  1.4 4.9 %collective-permute-start.2 = (bf16[1,16,1024]{2,1,0:T(8,128)(2,1)S(1)}, bf16[1,16,1024]{2,1,0:T(8,128)(2,1)S(1)}, u32[]{:S(2)}, u32[]{:S(2)}) collective-permute-start(bf16[1,16,1024]{2,1,0:T(8,128)(2,1)S(1)} %dynamic-slice_bitcast_fusion.11), channel_id=1, source_target_pairs={{0,1},{1,0},{2,3},{3,2},{4,5},{5,4},{6,7},{7,6},{8,9},{9,8},{10,11... | collective-permute-start | bytes 98312 | tf_op jit(solution)/shard_map/gather_1/ppermute | solution.py:190
  4.4 15.8 %collective-permute-start = (bf16[512,1024]{1,0:T(8,128)(2,1)}, bf16[512,1024]{1,0:T(8,128)(2,1)S(1)}, u32[]{:S(2)}, u32[]{:S(2)}) collective-permute-start(bf16[512,1024]{1,0:T(8,128)(2,1)} %refs_8_.1), channel_id=1, source_target_pairs={{0,8},{1,9},{2,10},{3,11},{4,12},{5,13},{6,14},{7,15},{8,0},{9,1},... | collective-permute-start | bytes 3145736 | tf_op jit(solution)/shard_map/swap_targets/ppermute | solution.py:190
  4.4 20.9 %collective-permute-start.1 = (bf16[512,1024]{1,0:T(8,128)(2,1)}, bf16[512,1024]{1,0:T(8,128)(2,1)S(1)}, u32[]{:S(2)}, u32[]{:S(2)}) collective-permute-start(bf16[512,1024]{1,0:T(8,128)(2,1)} %own_ref.6), channel_id=1, source_target_pairs={{0,8},{1,9},{2,10},{3,11},{4,12},{5,13},{6,14},{7,15},{8,0},{9,1},... | collective-permute-start | bytes 3145736 | tf_op jit(solution)/shard_map/swap_grads/ppermute | solution.py:190
  7.1 4.4 %collective-permute-start.3 = (bf16[2,16,1024]{2,1,0:T(8,128)(2,1)S(1)}, bf16[2,16,1024]{2,1,0:T(8,128)(2,1)S(1)}, u32[]{:S(2)}, u32[]{:S(2)}) collective-permute-start(bf16[2,16,1024]{2,1,0:T(8,128)(2,1)S(1)} %pad_maximum_fusion.5), channel_id=1, source_target_pairs={{0,2},{1,3},{2,0},{3,1},{4,6},{5,7},{6,4},{7,5},{8,10},{9,11},{10,... | collective-permute-start | bytes 196616 | tf_op jit(solution)/shard_map/gather_2/ppermute | solution.py:190
  11.5 6.1 %collective-permute-start.4 = (bf16[4,16,1024]{2,1,0:T(8,128)(2,1)S(1)}, bf16[4,16,1024]{2,1,0:T(8,128)(2,1)S(1)}, u32[]{:S(2)}, u32[]{:S(2)}) collective-permute-start(bf16[4,16,1024]{2,1,0:T(8,128)(2,1)S(1)} %pad_maximum_fusion.3), channel_id=1, source_target_pairs={{0,4},{1,5},{2,6},{3,7},{4,0},{5,1},{6,2},{7,3},{8,12},{9,13},{10,... | collective-permute-start | bytes 393224 | tf_op jit(solution)/shard_map/gather_4/ppermute | solution.py:190
  17.6 1.6 %collective-permute-start.5 = (bf16[8,16,1024]{2,1,0:T(8,128)(2,1)S(1)}, bf16[8,16,1024]{2,1,0:T(8,128)(2,1)S(1)}, u32[]{:S(2)}, u32[]{:S(2)}) collective-permute-start(bf16[8,16,1024]{2,1,0:T(8,128)(2,1)S(1)} %pad_maximum_fusion.2), channel_id=1, source_target_pairs={{0,8},{1,9},{2,10},{3,11},{4,12},{5,13},{6,14},{7,15},{8,0},{9,1},... | collective-permute-start | bytes 786440 | tf_op jit(solution)/shard_map/gather_core/ppermute | solution.py:190
  20.2 1.0 copy-start
  25.3 1.1 %copy-start.1 = (bf16[512,1024]{1,0:T(8,128)(2,1)}, bf16[512,1024]{1,0:T(8,128)(2,1)S(1)}, u32[]{:S(2)}) copy-start(bf16[512,1024]{1,0:T(8,128)(2,1)S(1)} %collective-permute-done.1.partner_ref) | copy-start | bytes 3145732
  39.2 30.4 %collective-permute-start.19 = (bf16[2,2,2,32,512]{4,3,1,2,0:T(8,128)(2,1)S(1)}, bf16[2,2,2,32,512]{4,3,1,2,0:T(8,128)(2,1)S(1)}, u32[]{:S(2)}, u32[]{:S(2)}) collective-permute-start(bf16[2,2,2,32,512]{4,3,1,2,0:T(8,128)(2,1)S(1)} %bitcast.134), channel_id=1, source_target_pairs={{0,1},{1,0},{2,3},{3,2},{4,5},{5,4},{6,7},{7,6},{8,9},{9,8},{10,11... | collective-permute-start | bytes 786440 | tf_op jit(solution)/shard_map/wo_b_0/ppermute | solution.py:190
  42.6 27.6 %collective-permute-start.17 = (bf16[2,2,2,32,512]{4,3,0,1,2:T(8,128)(2,1)S(1)}, bf16[2,2,2,32,512]{4,3,0,1,2:T(8,128)(2,1)S(1)}, u32[]{:S(2)}, u32[]{:S(2)}) collective-permute-start(bf16[2,2,2,32,512]{4,3,0,1,2:T(8,128)(2,1)S(1)} %bitcast.133), channel_id=1, source_target_pairs={{0,16},{1,17},{2,18},{3,19},{4,20},{5,21},{6,22},{7,23},{8,24},{9,... | collective-permute-start | bytes 786440 | tf_op jit(solution)/shard_map/wo_a_0/ppermute | solution.py:190
  58.4 13.9 %collective-permute-start.7 = (bf16[2,2,2,2,32,256]{5,4,0,1,2,3:T(8,128)(2,1)S(1)}, bf16[2,2,2,2,32,256]{5,4,0,1,2,3:T(8,128)(2,1)S(1)}, u32[]{:S(2)}, u32[]{:S(2)}) collective-permute-start(bf16[2,2,2,2,32,256]{5,4,0,1,2,3:T(8,128)(2,1)S(1)} %bitcast.135), channel_id=1, source_target_pairs={{0,16},{1,17},{2,18},{3,19},{4,20},{5,21},{6,22},{7,23},{8,24},{9,... | collective-permute-start | bytes 786440 | tf_op jit(solution)/shard_map/wq_0_0/ppermute | solution.py:190
  67.1 2.5 %copy-start.4 = (bf16[512,512]{1,0:T(8,128)(2,1)S(1)}, bf16[512,512]{1,0:T(8,128)(2,1)}, u32[]{:S(2)}) copy-start(bf16[512,512]{1,0:T(8,128)(2,1)} %get-tuple-element.23) | copy-start | bytes 1572868
  68.3 8.7 %collective-permute-start.9 = (bf16[2,2,2,2,32,256]{5,4,1,2,3,0:T(8,128)(2,1)S(1)}, bf16[2,2,2,2,32,256]{5,4,1,2,3,0:T(8,128)(2,1)S(1)}, u32[]{:S(2)}, u32[]{:S(2)}) collective-permute-start(bf16[2,2,2,2,32,256]{5,4,1,2,3,0:T(8,128)(2,1)S(1)} %bitcast.136), channel_id=1, source_target_pairs={{0,1},{1,0},{2,3},{3,2},{4,5},{5,4},{6,7},{7,6},{8,9},{9,8},{10,11... | collective-permute-start | bytes 786440 | tf_op jit(solution)/shard_map/wq_1_0/ppermute | solution.py:190
  69.5 7.6 %collective-permute-start.11 = (bf16[2,8,8,1024]{3,2,1,0:T(8,128)(2,1)S(1)}, bf16[2,8,8,1024]{3,2,1,0:T(8,128)(2,1)S(1)}, u32[]{:S(2)}, u32[]{:S(2)}) collective-permute-start(bf16[2,8,8,1024]{3,2,1,0:T(8,128)(2,1)S(1)} %fusion.6), channel_id=1, source_target_pairs={{0,8},{1,9},{2,10},{3,11},{4,12},{5,13},{6,14},{7,15},{8,0},{9,1},... | collective-permute-start | bytes 786440 | tf_op jit(solution)/shard_map/ctx_core/ppermute | solution.py:190
  69.6 23.6 %collective-permute-start.6 = (bf16[512,512]{1,0:T(8,128)(2,1)S(1)}, bf16[512,512]{1,0:T(8,128)(2,1)S(1)}, u32[]{:S(2)}, u32[]{:S(2)}) collective-permute-start(bf16[512,512]{1,0:T(8,128)(2,1)S(1)} %copy-done.4), channel_id=1, source_target_pairs={{0,8},{1,9},{2,10},{3,11},{4,12},{5,13},{6,14},{7,15},{8,0},{9,1},... | collective-permute-start | bytes 1572872 | tf_op jit(solution)/shard_map/query_core/ppermute | solution.py:190
  70.0 9.2 %copy-start.2 = (f32[256,1024]{1,0:T(8,128)S(1)}, f32[256,1024]{1,0:T(8,128)}, u32[]{:S(2)}) copy-start(f32[256,1024]{1,0:T(8,128)} %get-tuple-element.26) | copy-start | bytes 3145732
  70.2 9.1 %collective-permute-start.20 = (bf16[2,2,32,512]{3,2,0,1:T(8,128)(2,1)S(1)}, bf16[2,2,32,512]{3,2,0,1:T(8,128)(2,1)S(1)}, u32[]{:S(2)}, u32[]{:S(2)}) collective-permute-start(bf16[2,2,32,512]{3,2,0,1:T(8,128)(2,1)S(1)} %dynamic-slice_bitcast_fusion.1), channel_id=1, source_target_pairs={{0,16},{1,17},{2,18},{3,19},{4,20},{5,21},{6,22},{7,23},{8,24},{9,... | collective-permute-start | bytes 393224 | tf_op jit(solution)/shard_map/wo_b_1/ppermute | solution.py:190
  72.3 7.5 %collective-permute-start.18 = (bf16[2,2,32,512]{3,2,0,1:T(8,128)(2,1)S(1)}, bf16[2,2,32,512]{3,2,0,1:T(8,128)(2,1)S(1)}, u32[]{:S(2)}, u32[]{:S(2)}) collective-permute-start(bf16[2,2,32,512]{3,2,0,1:T(8,128)(2,1)S(1)} %dynamic-slice_bitcast_fusion.2), channel_id=1, source_target_pairs={{0,1},{1,0},{2,3},{3,2},{4,5},{5,4},{6,7},{7,6},{8,9},{9,8},{10,11... | collective-permute-start | bytes 393224 | tf_op jit(solution)/shard_map/wo_a_1/ppermute | solution.py:190
  77.0 9.5 %collective-permute-start.8 = (bf16[2,2,2,32,256]{4,3,0,1,2:T(8,128)(2,1)S(1)}, bf16[2,2,2,32,256]{4,3,0,1,2:T(8,128)(2,1)S(1)}, u32[]{:S(2)}, u32[]{:S(2)}) collective-permute-start(bf16[2,2,2,32,256]{4,3,0,1,2:T(8,128)(2,1)S(1)} %dynamic-slice_bitcast_fusion.5), channel_id=1, source_target_pairs={{0,1},{1,0},{2,3},{3,2},{4,5},{5,4},{6,7},{7,6},{8,9},{9,8},{10,11... | collective-permute-start | bytes 393224 | tf_op jit(solution)/shard_map/wq_0_1/ppermute | solution.py:190
  77.1 9.5 %collective-permute-start.10 = (bf16[2,2,2,32,256]{4,3,0,1,2:T(8,128)(2,1)S(1)}, bf16[2,2,2,32,256]{4,3,0,1,2:T(8,128)(2,1)S(1)}, u32[]{:S(2)}, u32[]{:S(2)}) collective-permute-start(bf16[2,2,2,32,256]{4,3,0,1,2:T(8,128)(2,1)S(1)} %dynamic-slice_bitcast_fusion.4), channel_id=1, source_target_pairs={{0,16},{1,17},{2,18},{3,19},{4,20},{5,21},{6,22},{7,23},{8,24},{9,... | collective-permute-start | bytes 393224 | tf_op jit(solution)/shard_map/wq_1_1/ppermute | solution.py:190
  79.3 5.0 %collective-permute-start.12 = (bf16[2,2,2,8,1024]{4,3,2,1,0:T(8,128)(2,1)S(1)}, bf16[2,2,2,8,1024]{4,3,2,1,0:T(8,128)(2,1)S(1)}, u32[]{:S(2)}, u32[]{:S(2)}) collective-permute-start(bf16[2,2,2,8,1024]{4,3,2,1,0:T(8,128)(2,1)S(1)} %dynamic-slice_bitcast_fusion.3), channel_id=1, source_target_pairs={{0,16},{1,17},{2,18},{3,19},{4,20},{5,21},{6,22},{7,23},{8,24},{9,... | collective-permute-start | bytes 393224 | tf_op jit(solution)/shard_map/ctx_0/ppermute | solution.py:190
  79.8 9.8 %collective-permute-start.21 = (bf16[2,32,1024]{2,1,0:T(8,128)(2,1)S(1)}, bf16[2,32,1024]{2,1,0:T(8,128)(2,1)S(1)}, u32[]{:S(2)}, u32[]{:S(2)}) collective-permute-start(bf16[2,32,1024]{2,1,0:T(8,128)(2,1)S(1)} %fusion.14), channel_id=1, source_target_pairs={{0,2},{1,3},{2,0},{3,1},{4,6},{5,7},{6,4},{7,5},{8,10},{9,11},{10,... | collective-permute-start | bytes 393224 | tf_op jit(solution)/shard_map/wo_0/ppermute | solution.py:190
  84.4 4.3 %collective-permute-start.13 = (bf16[2,2,8,1024]{3,2,1,0:T(8,128)(2,1)S(1)}, bf16[2,2,8,1024]{3,2,1,0:T(8,128)(2,1)S(1)}, u32[]{:S(2)}, u32[]{:S(2)}) collective-permute-start(bf16[2,2,8,1024]{3,2,1,0:T(8,128)(2,1)S(1)} %dynamic-slice_bitcast_fusion.10), channel_id=1, source_target_pairs={{0,1},{1,0},{2,3},{3,2},{4,5},{5,4},{6,7},{7,6},{8,9},{9,8},{10,11... | collective-permute-start | bytes 196616 | tf_op jit(solution)/shard_map/ctx_1/ppermute | solution.py:190
  88.9 9.3 %collective-permute-start.14 = (bf16[2,2,40,512]{3,2,0,1:T(8,128)(2,1)S(1)}, bf16[2,2,40,512]{3,2,0,1:T(8,128)(2,1)S(1)}, u32[]{:S(2)}, u32[]{:S(2)}) collective-permute-start(bf16[2,2,40,512]{3,2,0,1:T(8,128)(2,1)S(1)} %dynamic-slice_bitcast_fusion), channel_id=1, source_target_pairs={{0,2},{1,3},{2,0},{3,1},{4,6},{5,7},{6,4},{7,5},{8,10},{9,11},{10,... | collective-permute-start | bytes 491528 | tf_op jit(solution)/shard_map/tail_0/ppermute | solution.py:190
  89.7 8.7 %collective-permute-start.22 = (bf16[32,1024]{1,0:T(8,128)(2,1)S(1)}, bf16[32,1024]{1,0:T(8,128)(2,1)S(1)}, u32[]{:S(2)}, u32[]{:S(2)}) collective-permute-start(bf16[32,1024]{1,0:T(8,128)(2,1)S(1)} %dynamic-slice_bitcast_fusion.7), channel_id=1, source_target_pairs={{0,4},{1,5},{2,6},{3,7},{4,0},{5,1},{6,2},{7,3},{8,12},{9,13},{10,... | collective-permute-start | bytes 196616 | tf_op jit(solution)/shard_map/wo_1/ppermute | solution.py:190
  93.1 0.8 copy-start.3
  98.3 5.8 %collective-permute-start.15 = (bf16[2,40,512]{2,1,0:T(8,128)(2,1)S(1)}, bf16[2,40,512]{2,1,0:T(8,128)(2,1)S(1)}, u32[]{:S(2)}, u32[]{:S(2)}) collective-permute-start(bf16[2,40,512]{2,1,0:T(8,128)(2,1)S(1)} %dynamic-slice_bitcast_fusion.6), channel_id=1, source_target_pairs={{0,4},{1,5},{2,6},{3,7},{4,0},{5,1},{6,2},{7,3},{8,12},{9,13},{10,... | collective-permute-start | bytes 245768 | tf_op jit(solution)/shard_map/tail_1/ppermute | solution.py:190
  104.1 1.3 %collective-permute-start.16 = (f32[32,512]{1,0:T(8,128)S(1)}, f32[32,512]{1,0:T(8,128)S(1)}, u32[]{:S(2)}, u32[]{:S(2)}) collective-permute-start(f32[32,512]{1,0:T(8,128)S(1)} %get-tuple-element.49), channel_id=1, source_target_pairs={{0,8},{1,9},{2,10},{3,11},{4,12},{5,13},{6,14},{7,15},{8,0},{9,1},... | collective-permute-start | bytes 196616 | tf_op jit(solution)/shard_map/wq_core/ppermute | solution.py:190

commit v3 on v2

--- a/solution.py
+++ b/solution.py
@@ -6,6 +6,7 @@
 from jax.experimental import pallas as pl
 from jax.experimental.pallas import tpu as pltpu
 from jax.sharding import PartitionSpec as P
+
 
 HEADS = 16
 TVIEWS = 8
@@ -89,11 +90,11 @@
     att_ref,
     own_ref,
     partner_ref,
-    prior_ref,
     qg_own_ref,
     qg_partner_ref,
     wq_ref,
     ctx_ref,
+    prior_ref=None,
 ):
     block_rows = own_ref.shape[0]
     size = q_ref.shape[0] // heads
@@ -119,7 +120,7 @@
 
     @pl.when(pl.program_id(0) == 0)
     def _():
-        ctx_ref[...] = prior_ref[...] + term
+        ctx_ref[...] = term if prior_ref is None else prior_ref[...] + term
 
     @pl.when(pl.program_id(0) > 0)
     def _():
@@ -150,7 +151,7 @@
     )
 
 
-def call(kernel, name, steps, in_specs, out_specs, out_shape, flops, scratch=(), aliases=None):
+def call(kernel, steps, in_specs, out_specs, out_shape, flops, scratch=(), aliases=None):
     return pl.pallas_call(
         kernel,
         grid_spec=pltpu.PrefetchScalarGridSpec(
@@ -163,7 +164,6 @@
         out_shape=out_shape,
         input_output_aliases=aliases or {},
         cost_estimate=pl.CostEstimate(flops=flops, bytes_accessed=4 << 20, transcendentals=0),
-        name=name,
     )
 
 
@@ -200,20 +200,16 @@
     targets_swapped = None
     mask = 1
     while mask < seq_count:
-        with jax.named_scope(f"gather_{mask}"):
-            other = swap(held, mask)
+        other = swap(held, mask)
         if targets_swapped is None:
-            with jax.named_scope("swap_targets"):
-                targets_swapped = swap(targets, core_mask)
-            with jax.named_scope("swap_grads"):
-                grad_swapped = swap(grad_out, core_mask)
+            targets_swapped = swap(targets, core_mask)
+            grad_swapped = swap(grad_out, core_mask)
         upper = bit_of(mask) == 1
         held = jnp.concatenate(
             [jnp.where(upper, other, held), jnp.where(upper, held, other)], axis=0
         )
         mask *= 2
-    with jax.named_scope("gather_core"):
-        other = swap(held, core_mask)
+    other = swap(held, core_mask)
     held = jnp.stack(
         [jnp.where(core == 1, other, held), jnp.where(core == 1, held, other)], axis=1
     )
@@ -221,34 +217,22 @@
 
     product = 2 * half_width * rows * width
     row_block = fixed((query_rows, width))
-    with jax.named_scope("project_q"):
-        queries = call(
-            query_kernel,
-            "project_q",
-            high_count,
-            [
-                pl.BlockSpec((width, block), lambda i, core: (0, 2 * i + core[0])),
-                row_block,
-                row_block,
-            ],
-            pl.BlockSpec((block, rows), lambda i, core: (i, 0)),
-            shaped(half_width, rows),
-            product,
-        )(core_index, w_query, targets, targets_swapped)
-    with jax.named_scope("project_g"):
-        grads = call(
-            grad_kernel,
-            "project_g",
-            high_count,
-            [
-                pl.BlockSpec((block, width), lambda i, core: (2 * i + core[0], 0)),
-                row_block,
-                row_block,
-            ],
-            pl.BlockSpec((block, rows), lambda i, core: (i, 0)),
-            shaped(half_width, rows),
-            product,
-        )(core_index, w_out, grad_out, grad_swapped)
+    queries = call(
+        query_kernel,
+        high_count,
+        [pl.BlockSpec((width, block), lambda i, core: (0, 2 * i + core[0])), row_block, row_block],
+        pl.BlockSpec((block, rows), lambda i, core: (i, 0)),
+        shaped(half_width, rows),
+        product,
+    )(core_index, w_query, targets, targets_swapped)
+    grads = call(
+        grad_kernel,
+        high_count,
+        [pl.BlockSpec((block, width), lambda i, core: (2 * i + core[0], 0)), row_block, row_block],
+        pl.BlockSpec((block, rows), lambda i, core: (i, 0)),
+        shaped(half_width, rows),
+        product,
+    )(core_index, w_out, grad_out, grad_swapped)
 
     view_rows = query_rows * device_count // TVIEWS
     context_view = context_rows // CVIEWS
@@ -282,34 +266,32 @@
         return pl.BlockSpec((step_heads, context_rows, rows), lambda i, core: (i + offset, 0, 0))
 
     attention = 8 * half_width * rows * context_rows
-    with jax.named_scope("attend"):
-        key_values, probs, attended, wo_term = call(
-            partial(attend_kernel, step_heads, score_scale),
-            "attend",
-            steps,
-            [
-                fixed((context_rows, width)),
-                weight_spec(0),
-                weight_spec(0),
-                head_spec(0),
-                row_block,
-                row_block,
-                fixed((2, context_rows, 128)),
-            ],
-            [
-                kv_spec(0),
-                probs_spec(0),
-                head_spec(0),
-                pl.BlockSpec((step_width, width), lambda i, core: (i, 0)),
-            ],
-            [
-                shaped(2, half_width, context_rows),
-                shaped(half_width // head_size, context_rows, rows),
-                shaped(half_width, rows),
-                shaped(half_width, width),
-            ],
-            product + attention,
-        )(core_index, context_all, w_key, w_value, queries, grad_out, grad_swapped, bias)
+    key_values, probs, attended, wo_term = call(
+        partial(attend_kernel, step_heads, score_scale),
+        steps,
+        [
+            fixed((context_rows, width)),
+            weight_spec(0),
+            weight_spec(0),
+            head_spec(0),
+            row_block,
+            row_block,
+            fixed((2, context_rows, 128)),
+        ],
+        [
+            kv_spec(0),
+            probs_spec(0),
+            head_spec(0),
+            pl.BlockSpec((step_width, width), lambda i, core: (i, 0)),
+        ],
+        [
+            shaped(2, half_width, context_rows),
+            shaped(half_width // head_size, context_rows, rows),
+            shaped(half_width, rows),
+            shaped(half_width, width),
+        ],
+        product + attention,
+    )(core_index, context_all, w_key, w_value, queries, grad_out, grad_swapped, bias)
 
     def back(part, prior, earlier):
         offset = part * per_block
@@ -324,7 +306,6 @@
             head_spec(offset),
             row_block,
             row_block,
-            fixed((context_rows, width)),
         ]
         operands = [
             core_index,
@@ -337,7 +318,6 @@
             attended,
             targets,
             targets_swapped,
-            prior,
         ]
         kernel = partial(back_kernel, step_heads, score_scale)
         aliases = {}
@@ -345,14 +325,14 @@
             inner = kernel
 
             def kernel(*refs):
-                return inner(*refs[:11], *refs[13:])
+                return inner(*refs[:10], *refs[13:], prior_ref=refs[12])
 
             in_specs = in_specs + [pl.BlockSpec(memory_space=pl.ANY)] * 2
-            operands = operands + list(earlier)
-            aliases = {11: 0, 12: 1}
+            in_specs.append(fixed((context_rows, width)))
+            operands = operands + list(earlier) + [prior]
+            aliases = {10: 0, 11: 1}
         return call(
             kernel,
-            "back",
             per_block,
             in_specs,
             [
@@ -382,94 +362,102 @@
         seq_masks.append(mask)
         mask //= 2
     all_masks = high_masks + seq_masks
-    orders = [(high_masks[-1], seq_masks[-1]), (seq_masks[-1], high_masks[-1])]
-    rest = seq_masks[-2::-1] + high_masks[:-1]
+    core_masks = high_masks + [0] + seq_masks
     high_bits = [2] * len(high_masks)
     seq_bits = [2] * len(seq_masks)
-
-    def halve(array, masks, mask, label, last=False):
-        axis = masks.index(mask)
-        bit = bit_of(mask)
-        sent = lax.dynamic_index_in_dim(array, 1 - bit, axis, keepdims=False)
-        kept = lax.dynamic_index_in_dim(array, bit, axis, keepdims=False)
-        with jax.named_scope(label):
-            moved = swap(sent, mask)
-        total = kept.astype(F32) + moved.astype(F32)
-        left = masks[:axis] + masks[axis + 1 :]
+    order = [high_masks[-1], seq_masks[-1]] + seq_masks[-2::-1] + high_masks[:-1]
+    stages = [tuple(order[at : at + 2]) for at in range(0, len(order), 2)]
+
+    def exchange(array, masks, stage, last=False):
+        def piece(flips):
+            part = array
+            for mask, flip in sorted(zip(stage, flips), key=lambda one: -masks.index(one[0])):
+                at = (bit_of(mask) + flip) % 2
+                part = lax.dynamic_index_in_dim(part, at, masks.index(mask), keepdims=False)
+            return part
+
+        moved = []
+        for way in range(1, 2 ** len(stage)):
+            flips = [way >> at & 1 for at in range(len(stage))]
+            target = sum(mask for mask, flip in zip(stage, flips) if flip)
+            moved.append(swap(piece(flips), target))
+        total = piece([0] * len(stage)).astype(F32)
+        for one in moved:
+            total = total + one.astype(F32)
+        left = [mask for mask in masks if mask not in stage]
         return (total if last else total.astype(BF16)), left
 
-    def halve_twice(array, masks, which, label):
-        for step, mask in enumerate(orders[which]):
-            array, masks = halve(array, masks, mask, f"{label}_{step}")
-        return array, masks
-
-    def halve_rest(array, masks, label):
-        for step, mask in enumerate(rest):
-            array, masks = halve(array, masks, mask, f"{label}_{step}", step == len(rest) - 1)
+    def exchange_rest(array, masks):
+        for at, stage in enumerate(stages[1:]):
+            array, masks = exchange(array, masks, stage, at == len(stages) - 2)
         return array
 
     out_rows = width // device_count
     ctx_out = context_rows // device_count
 
     wo_split = wo_term.reshape(*high_bits, *seq_bits, out_rows, width)
-    wo_one, masks = halve_twice(wo_split[..., :half_width], all_masks, 0, "wo_a")
-    wo_two, _ = halve_twice(wo_split[..., half_width:], all_masks, 1, "wo_b")
-    grad_wo = halve_rest(jnp.concatenate([wo_one, wo_two], axis=-1), masks, "wo")
-
-    ctx_term = jnp.zeros((context_rows, width), F32)
+    wo_part, left_masks = exchange(wo_split, all_masks, stages[0])
+
+    ctx_term = None
     query_parts = None
     wq_parts = []
-    core_masks = high_masks + [0] + seq_masks
     for part in range(high_count):
-        with jax.named_scope(f"back_{part}"):
-            *query_parts, wq_term, ctx_term = back(part, ctx_term, query_parts)
+        *query_parts, wq_term, ctx_term = back(part, ctx_term, query_parts)
         wq_split = wq_term.reshape(*high_bits, 2, *seq_bits, out_rows, block)
-        wq_part, wq_masks = halve_twice(wq_split, core_masks, part % 2, f"wq_{part}")
+        wq_part, _ = exchange(wq_split, core_masks, stages[0])
         wq_parts.append(wq_part)
 
     ctx_split = ctx_term.reshape(high_count, 2, seq_count, ctx_out, width)
     ctx_kept = lax.dynamic_index_in_dim(ctx_split, core, 1, keepdims=False)
     ctx_sent = lax.dynamic_index_in_dim(ctx_split, 1 - core, 1, keepdims=False).astype(BF16)
-    with jax.named_scope("ctx_core"):
-        ctx_moved = swap(ctx_sent, core_mask)
+    ctx_moved = swap(ctx_sent, core_mask)
     ctx_pair = (ctx_kept + ctx_moved.astype(F32)).astype(BF16)
     ctx_pair = ctx_pair.reshape(*high_bits, *seq_bits, ctx_out, width)
-    ctx_pair, masks = halve_twice(ctx_pair, all_masks, 0, "ctx")
-    ctx_pair = jnp.moveaxis(ctx_pair.reshape(*ctx_pair.shape[:-1], 2, half_width), -2, 0)
-    ctx_pair = jnp.moveaxis(ctx_pair, 0, len(high_masks) - 1)
-    tail = jnp.concatenate([jnp.concatenate(wq_parts, axis=-1), ctx_pair], axis=-2)
-    tail = halve_rest(tail, wq_masks, "tail")
-
-    mine = lax.dynamic_index_in_dim(tail[:, :out_rows], core, 0, keepdims=False)
-    sent = lax.dynamic_index_in_dim(tail[:, :out_rows], 1 - core, 0, keepdims=False)
-    with jax.named_scope("wq_core"):
-        theirs = swap(sent, core_mask)
+    ctx_pair, _ = exchange(ctx_pair, all_masks, stages[0])
+
+    at_core = len(high_masks) - 1
+    early = [wo_part[..., cut * block : (cut + 1) * block] for cut in range(width // block)]
+    for wq_part in wq_parts[:-1]:
+        early += [lax.index_in_dim(wq_part, which, at_core, keepdims=False) for which in (0, 1)]
+    early = exchange_rest(jnp.concatenate(early, axis=-2), left_masks)
+    late = [lax.index_in_dim(wq_parts[-1], which, at_core, keepdims=False) for which in (0, 1)]
+    late += [ctx_pair[..., cut * block : (cut + 1) * block] for cut in range(width // block)]
+    late = exchange_rest(jnp.concatenate(late, axis=-2), left_masks)
+
+    cuts = width // block
+    grad_wo = jnp.concatenate(
+        [early[cut * out_rows : (cut + 1) * out_rows] for cut in range(cuts)], axis=1
+    )
+    wq_sums = early[cuts * out_rows :].reshape(high_count - 1, 2, out_rows, block)
+    wq_sums = jnp.concatenate([wq_sums, late[: 2 * out_rows].reshape(1, 2, out_rows, block)])
+    sent = lax.dynamic_index_in_dim(wq_sums, 1 - core, 1, keepdims=False)
+    mine = lax.dynamic_index_in_dim(wq_sums, core, 1, keepdims=False)
+    theirs = swap(sent, core_mask)
     pieces = []
     for part in range(high_count):
-        cut = slice(part * block, (part + 1) * block)
-        pieces.append(jnp.where(core == 0, mine[:, cut], theirs[:, cut]))
-        pieces.append(jnp.where(core == 0, theirs[:, cut], mine[:, cut]))
+        pieces.append(jnp.where(core == 0, mine[part], theirs[part]))
+        pieces.append(jnp.where(core == 0, theirs[part], mine[part]))
     grad_wq = jnp.concatenate(pieces, axis=1)
-    d_context = jnp.concatenate([tail[0, out_rows:], tail[1, out_rows:]], axis=1).astype(BF16)
-
-    with jax.named_scope("query_core"):
-        returned = swap(query_parts[1], core_mask)
-    with jax.named_scope("targets_out"):
-        d_targets = call(
-            targets_kernel,
-            "targets_out",
-            high_count,
-            [
-                pl.BlockSpec((block, query_rows), lambda i, core: (i, 0)),
-                pl.BlockSpec((block, query_rows), lambda i, core: (i, 0)),
-                pl.BlockSpec((width, block), lambda i, core: (0, 2 * i + core[0])),
-                pl.BlockSpec((width, block), lambda i, core: (0, 2 * i + 1 - core[0])),
-            ],
-            fixed((query_rows, width)),
-            shaped(query_rows, width),
-            product,
-            scratch=[pltpu.VMEM((query_rows, width), F32)],
-        )(core_index, query_parts[0], returned, w_query, w_query)
+    ctx_sums = late[2 * out_rows :]
+    d_context = jnp.concatenate(
+        [ctx_sums[cut * ctx_out : (cut + 1) * ctx_out] for cut in range(cuts)], axis=1
+    ).astype(BF16)
+
+    returned = swap(query_parts[1], core_mask)
+    d_targets = call(
+        targets_kernel,
+        high_count,
+        [
+            pl.BlockSpec((block, query_rows), lambda i, core: (i, 0)),
+            pl.BlockSpec((block, query_rows), lambda i, core: (i, 0)),
+            pl.BlockSpec((width, block), lambda i, core: (0, 2 * i + core[0])),
+            pl.BlockSpec((width, block), lambda i, core: (0, 2 * i + 1 - core[0])),
+        ],
+        fixed((query_rows, width)),
+        shaped(query_rows, width),
+        product,
+        scratch=[pltpu.VMEM((query_rows, width), F32)],
+    )(core_index, query_parts[0], returned, w_query, w_query)
     return (d_targets, d_context, grad_wq, grad_wo)
 
 
@@ -485,6 +473,7 @@
         P(AXES, None),
     )
     out_specs = (P(AXES, None), P(AXES, None), P(AXES, None), P(AXES, None))
+
     return jax.shard_map(
         on_device, mesh=mesh, in_specs=in_specs, out_specs=out_specs, check_vma=False
     )

time: 107 us -> 116 us (1.084)
  starting transfers between devices: 28 us -> 38.2 us
  local copies, waits for them, and re-layouts: 9.74 us -> 7.89 us
  other arithmetic: 5.49 us -> 7.09 us
    ppermute x23 -> x27, starting transfers between devices: 28 us -> 38.2 us  [swap(): lax.ppermute(array, AXES, [(i, i ^ mask) for i in range(device_count)])]
    dynamic_slice x6 -> x0, local copies, waits for them, and re-layouts: 2.32 us -> none  [the longest x4 2.28 us: halve(): kept = lax.dynamic_index_in_dim(array, bit, axis, keepdims=False)]
    squeeze x11 -> x6, local copies, waits for them, and re-layouts: 0.17 us -> 2.34 us  [piece(): part = lax.dynamic_index_in_dim(part, at, masks.index(mask), keepdims=False)]
    convert_element_type x12 -> x4, other arithmetic: 0.59 us -> 2.19 us  [exchange(): return (total if last else total.astype(BF16), left)]
    slice x2 -> x4, local copies, waits for them, and re-layouts: 1.28 us -> 0.03 us  [the longest x1 0.01 us: on_device(): early[cut * out_rows:(cut + 1) * out_rows]]
    unnamed x12 -> x22, local copies, waits for them, and re-layouts: 1.94 us -> 2.83 us
    ppermute x23 -> x27, waiting for transfers between devices: 21.8 us -> 22 us  [swap(): lax.ppermute(array, AXES, [(i, i ^ mask) for i in range(device_count)])]
  transfers between devices with their start and end apart: 23 -> 27, of which waited for: 10 -> 12; matrix products, arithmetic and copies ran while one was open for 9% -> 8% of each run, Pallas kernels for 27% -> 11%
where the time goes in v3:
time: 116 us
  Pallas kernels  39.5 us (34%)
  starting transfers between devices  38.2 us (33%)
  waiting for transfers between devices  22 us (19%)
  local copies, waits for them, and re-layouts  7.89 us (7%)
  other arithmetic  7.09 us (6%)
  between operations  1.24 us (1%)
    ppermute x27, starting transfers between devices, swap(): lax.ppermute(array, AXES, [(i, i ^ mask) for i in range(device_count)])  38.2 us
    ppermute x27, waiting for transfers between devices, swap(): lax.ppermute(array, AXES, [(i, i ^ mask) for i in range(device_count)])  22 us
    pallas_call x2, Pallas kernels, back(): call(kernel, per_block, in_specs, [qg_spec, qg_spec, pl.BlockSpec((width,...  15.7 us
    pallas_call x1, Pallas kernels, on_device(): call(partial(attend_kernel, step_heads, score_scale), steps, [fixed((cont...  11.4 us
    pallas_call x1, Pallas kernels, on_device(): call(targets_kernel, high_count, [pl.BlockSpec((block, query_rows), lambd...  4.29 us
    pallas_call x1, Pallas kernels, on_device(): call(query_kernel, high_count, [pl.BlockSpec((width, block), lambda i, co...  4.12 us
    pallas_call x1, Pallas kernels, on_device(): call(grad_kernel, high_count, [pl.BlockSpec((block, width), lambda i, cor...  4.01 us
    unnamed x22, local copies, waits for them, and re-layouts  2.83 us
  transfers between devices with their start and end apart: 27, of which 12 were waited for; matrix products, arithmetic and copies ran while one was open for 8% of the time, Pallas kernels for 11%

profile of v3, /device:TPU:0, one launch (start us, length us, event | category | flops | bytes accessed | tf_op | source)
XLA Modules:
  0.0 115.8 jit_solution(10620697825571240641)
XLA Ops:
  1.4 3.0 %collective-permute-start.2 = (bf16[1,16,1024]{2,1,0:T(8,128)(2,1)S(1)}, bf16[1,16,1024]{2,1,0:T(8,128)(2,1)S(1)}, u32[]{:S(2)}, u32[]{:S(2)}) collective-permute-start(bf16[1,16,1024]{2,1,0:T(8,128)(2,1)S(1)} %dynamic-slice_bitcast_fusion.18), channel_id=1, source_target_pairs={{0,1},{1,0},{2,3},{3,2},{4,5},{5,4},{6,7},{7,6},{8,9},{9,8},{10,11... | collective-permute-start | bytes 98312 | tf_op jit(solution)/shard_map/ppermute | solution.py:190
  5.0 1.3 %collective-permute-done.2 = bf16[1,16,1024]{2,1,0:T(8,128)(2,1)S(1)} collective-permute-done((bf16[1,16,1024]{2,1,0:T(8,128)(2,1)S(1)}, bf16[1,16,1024]{2,1,0:T(8,128)(2,1)S(1)}, u32[]{:S(2)}, u32[]{:S(2)}) %collective-permute-start.2) | collective-permute-done | bytes 32800 | tf_op jit(solution)/shard_map/ppermute | solution.py:190
  7.1 2.1 %collective-permute-start.3 = (bf16[2,16,1024]{2,1,0:T(8,128)(2,1)S(1)}, bf16[2,16,1024]{2,1,0:T(8,128)(2,1)S(1)}, u32[]{:S(2)}, u32[]{:S(2)}) collective-permute-start(bf16[2,16,1024]{2,1,0:T(8,128)(2,1)S(1)} %pad_maximum_fusion.5), channel_id=1, source_target_pairs={{0,2},{1,3},{2,0},{3,1},{4,6},{5,7},{6,4},{7,5},{8,10},{9,11},{10,... | collective-permute-start | bytes 196616 | tf_op jit(solution)/shard_map/ppermute | solution.py:190
  9.3 2.2 %collective-permute-done.3 = bf16[2,16,1024]{2,1,0:T(8,128)(2,1)S(1)} collective-permute-done((bf16[2,16,1024]{2,1,0:T(8,128)(2,1)S(1)}, bf16[2,16,1024]{2,1,0:T(8,128)(2,1)S(1)}, u32[]{:S(2)}, u32[]{:S(2)}) %collective-permute-start.3) | collective-permute-done | bytes 65568 | tf_op jit(solution)/shard_map/ppermute | solution.py:190
  11.5 3.1 %collective-permute-start.4 = (bf16[4,16,1024]{2,1,0:T(8,128)(2,1)S(1)}, bf16[4,16,1024]{2,1,0:T(8,128)(2,1)S(1)}, u32[]{:S(2)}, u32[]{:S(2)}) collective-permute-start(bf16[4,16,1024]{2,1,0:T(8,128)(2,1)S(1)} %pad_maximum_fusion.2), channel_id=1, source_target_pairs={{0,4},{1,5},{2,6},{3,7},{4,0},{5,1},{6,2},{7,3},{8,12},{9,13},{10,... | collective-permute-start | bytes 393224 | tf_op jit(solution)/shard_map/ppermute | solution.py:190
  15.5 2.1 %collective-permute-done.4 = bf16[4,16,1024]{2,1,0:T(8,128)(2,1)S(1)} collective-permute-done((bf16[4,16,1024]{2,1,0:T(8,128)(2,1)S(1)}, bf16[4,16,1024]{2,1,0:T(8,128)(2,1)S(1)}, u32[]{:S(2)}, u32[]{:S(2)}) %collective-permute-start.4) | collective-permute-done | bytes 131104 | tf_op jit(solution)/shard_map/ppermute | solution.py:190
  18.0 1.3 %collective-permute-done.5 = bf16[8,16,1024]{2,1,0:T(8,128)(2,1)S(1)} collective-permute-done((bf16[8,16,1024]{2,1,0:T(8,128)(2,1)S(1)}, bf16[8,16,1024]{2,1,0:T(8,128)(2,1)S(1)}, u32[]{:S(2)}, u32[]{:S(2)}) %collective-permute-start.5) | collective-permute-done | bytes 262176 | tf_op jit(solution)/shard_map/ppermute | solution.py:190
  21.1 4.1 %shard_map.111.q_ref.refs_3_ = bf16[512,1024]{1,0:T(8,128)(2,1)} custom-call(s32[1]{0:T(128)} %bitcast.core_ref.refs_0_, bf16[1024,1024]{1,0:T(8,128)(2,1)} %wq_theirs_ref.1, bf16[512,1024]{1,0:T(8,128)(2,1)} %refs_8_.1, bf16[512,1024]{1,0:T(8,128)(2,1)} %copy-done), custom_call_target="tpu_custom_call" | custom-call | flops 1073741824 | bytes 4194304 | tf_op jit(solution)/shard_map/pallas_call | solution.py:220
  26.2 4.0 %shard_map.112.g_ref.refs_4_ = bf16[512,1024]{1,0:T(8,128)(2,1)} custom-call(s32[1]{0:T(128)} %bitcast.core_ref.refs_0_, bf16[1024,1024]{1,0:T(8,128)(2,1)} %weight_ref.3, bf16[512,1024]{1,0:T(8,128)(2,1)} %own_ref.6, bf16[512,1024]{1,0:T(8,128)(2,1)} %copy-done.1), custom_call_target="tpu_custom_call" | custom-call | flops 1073741824 | bytes 4194304 | tf_op jit(solution)/shard_map/pallas_call | solution.py:228
  31.1 11.4 %shard_map.113 = (bf16[2,512,256]{2,1,0:T(8,128)(2,1)}, bf16[8,256,1024]{2,1,0:T(8,128)(2,1)}, bf16[512,1024]{1,0:T(8,128)(2,1)}, bf16[512,1024]{1,0:T(8,128)(2,1)}) custom-call(s32[1]{0:T(128)} %bitcast.core_ref.refs_0_, bf16[256,1024]{1,0:T(8,128)(2,1)} %bitcast.134, bf16[1024,1024]{1,0:T(8,128)(2,1)} %refs_1_.1, bf16[1024,1024]{1,0:T(8,128)(2,1)} %refs_2_.1, ...), custom_call_target="tpu_custom_call" | custom-call | flops 2147483648 | bytes 4194304 | tf_op jit(solution)/shard_map/pallas_call | solution.py:269
  42.5 7.6 %shard_map.114 = (bf16[512,512]{1,0:T(8,128)(2,1)}, bf16[512,512]{1,0:T(8,128)(2,1)}, bf16[1024,256]{1,0:T(8,128)(2,1)}, f32[256,1024]{1,0:T(8,128)}) custom-call(s32[1]{0:T(128)} %bitcast.core_ref.refs_0_, bf16[1024,1024]{1,0:T(8,128)(2,1)} %refs_1_.1, bf16[1024,1024]{1,0:T(8,128)(2,1)} %refs_2_.1, bf16[512,1024]{1,0:T(8,128)(2,1)} %shard_map.111.q_ref.refs_3_, ...), custom_call_target="tpu_custom_call" | custom-call | flops 1073741824 | bytes 4194304 | tf_op jit(solution)/shard_map/pallas_call | solution.py:334
  50.1 1.1 dynamic-slice_bitcast_fusion.5
  51.2 3.3 %collective-permute-start.20 = (bf16[2,2,2,32,256]{4,3,2,1,0:T(8,128)(2,1)S(1)}, bf16[2,2,2,32,256]{4,3,2,1,0:T(8,128)(2,1)S(1)}, u32[]{:S(2)}, u32[]{:S(2)}) collective-permute-start(bf16[2,2,2,32,256]{4,3,2,1,0:T(8,128)(2,1)S(1)} %get-tuple-element.33), channel_id=1, source_target_pairs={{0,16},{1,17},{2,18},{3,19},{4,20},{5,21},{6,22},{7,23},{8,24},{9,... | collective-permute-start | bytes 393224 | tf_op jit(solution)/shard_map/ppermute | solution.py:190
  54.4 1.5 %collective-permute-start.21 = (bf16[2,2,2,32,256]{4,3,2,1,0:T(8,128)(2,1)S(1)}, bf16[2,2,2,32,256]{4,3,2,1,0:T(8,128)(2,1)S(1)}, u32[]{:S(2)}, u32[]{:S(2)}) collective-permute-start(bf16[2,2,2,32,256]{4,3,2,1,0:T(8,128)(2,1)S(1)} %get-tuple-element.35), channel_id=1, source_target_pairs={{0,1},{1,0},{2,3},{3,2},{4,5},{5,4},{6,7},{7,6},{8,9},{9,8},{10,11... | collective-permute-start | bytes 393224 | tf_op jit(solution)/shard_map/ppermute | solution.py:190
  56.0 8.1 %shard_map.115 = (bf16[512,512]{1,0:T(8,128)(2,1)}, bf16[512,512]{1,0:T(8,128)(2,1)}, bf16[1024,256]{1,0:T(8,128)(2,1)}, f32[256,1024]{1,0:T(8,128)}) custom-call(s32[1]{0:T(128)} %bitcast.core_ref.refs_0_, bf16[1024,1024]{1,0:T(8,128)(2,1)} %refs_1_.1, bf16[1024,1024]{1,0:T(8,128)(2,1)} %refs_2_.1, ...), custom_call_target="tpu_custom_call", output_to_operand_aliasing={{0}: (10, {}), {1}: (11, {})} | custom-call | flops 1073741824 | bytes 4194304 | tf_op jit(solution)/shard_map/pallas_call | solution.py:334
  64.0 1.1 dynamic-slice_bitcast_fusion.8
  65.8 2.9 %collective-permute-start.9 = (bf16[2,2,2,32,256]{4,3,2,1,0:T(8,128)(2,1)S(1)}, bf16[2,2,2,32,256]{4,3,2,1,0:T(8,128)(2,1)S(1)}, u32[]{:S(2)}, u32[]{:S(2)}) collective-permute-start(bf16[2,2,2,32,256]{4,3,2,1,0:T(8,128)(2,1)S(1)} %get-tuple-element.37), channel_id=1, source_target_pairs={{0,17},{1,16},{2,19},{3,18},{4,21},{5,20},{6,23},{7,22},{8,25},{9,... | collective-permute-start | bytes 393224 | tf_op jit(solution)/shard_map/ppermute | solution.py:190
  68.7 1.1 fusion.4
  69.9 1.7 %collective-permute-done.7 = bf16[2,2,2,32,256]{4,3,2,1,0:T(8,128)(2,1)S(1)} collective-permute-done((bf16[2,2,2,32,256]{4,3,2,1,0:T(8,128)(2,1)S(1)}, bf16[2,2,2,32,256]{4,3,2,1,0:T(8,128)(2,1)S(1)}, u32[]{:S(2)}, u32[]{:S(2)}) %collective-permute-start.7) | collective-permute-done | bytes 131104 | tf_op jit(solution)/shard_map/ppermute | solution.py:190
  71.6 3.3 %collective-permute-done.8 = bf16[2,2,2,32,256]{4,3,2,1,0:T(8,128)(2,1)S(1)} collective-permute-done((bf16[2,2,2,32,256]{4,3,2,1,0:T(8,128)(2,1)S(1)}, bf16[2,2,2,32,256]{4,3,2,1,0:T(8,128)(2,1)S(1)}, u32[]{:S(2)}, u32[]{:S(2)}) %collective-permute-start.8) | collective-permute-done | bytes 131104 | tf_op jit(solution)/shard_map/ppermute | solution.py:190
  74.9 3.8 %collective-permute-start.17 = (bf16[2,2,32,1024]{3,2,1,0:T(8,128)(2,1)S(1)}, bf16[2,2,32,1024]{3,2,1,0:T(8,128)(2,1)S(1)}, u32[]{:S(2)}, u32[]{:S(2)}) collective-permute-start(bf16[2,2,32,1024]{3,2,1,0:T(8,128)(2,1)S(1)} %get-tuple-element.30), channel_id=1, source_target_pairs={{0,16},{1,17},{2,18},{3,19},{4,20},{5,21},{6,22},{7,23},{8,24},{9,... | collective-permute-start | bytes 786440 | tf_op jit(solution)/shard_map/ppermute | solution.py:190
  78.7 1.0 fusion.10
  79.8 1.5 %collective-permute-start.19 = (bf16[2,2,32,1024]{3,2,1,0:T(8,128)(2,1)S(1)}, bf16[2,2,32,1024]{3,2,1,0:T(8,128)(2,1)S(1)}, u32[]{:S(2)}, u32[]{:S(2)}) collective-permute-start(bf16[2,2,32,1024]{3,2,1,0:T(8,128)(2,1)S(1)} %get-tuple-element.31), channel_id=1, source_target_pairs={{0,17},{1,16},{2,19},{3,18},{4,21},{5,20},{6,23},{7,22},{8,25},{9,... | collective-permute-start | bytes 786440 | tf_op jit(solution)/shard_map/ppermute | solution.py:190
  81.9 1.0 fusion.7
  82.9 1.4 %collective-permute-done.17 = bf16[2,2,32,1024]{3,2,1,0:T(8,128)(2,1)S(1)} collective-permute-done((bf16[2,2,32,1024]{3,2,1,0:T(8,128)(2,1)S(1)}, bf16[2,2,32,1024]{3,2,1,0:T(8,128)(2,1)S(1)}, u32[]{:S(2)}, u32[]{:S(2)}) %collective-permute-start.17) | collective-permute-done | bytes 262176 | tf_op jit(solution)/shard_map/ppermute | solution.py:190
  84.3 5.8 %collective-permute-done.18 = bf16[2,2,32,1024]{3,2,1,0:T(8,128)(2,1)S(1)} collective-permute-done((bf16[2,2,32,1024]{3,2,1,0:T(8,128)(2,1)S(1)}, bf16[2,2,32,1024]{3,2,1,0:T(8,128)(2,1)S(1)}, u32[]{:S(2)}, u32[]{:S(2)}) %collective-permute-start.18) | collective-permute-done | bytes 262176 | tf_op jit(solution)/shard_map/ppermute | solution.py:190
  90.7 3.4 %collective-permute-start.13 = (bf16[2,2,8,1024]{3,2,1,0:T(8,128)(2,1)S(1)}, bf16[2,2,8,1024]{3,2,1,0:T(8,128)(2,1)S(1)}, u32[]{:S(2)}, u32[]{:S(2)}) collective-permute-start(bf16[2,2,8,1024]{3,2,1,0:T(8,128)(2,1)S(1)} %get-tuple-element.45), channel_id=1, source_target_pairs={{0,17},{1,16},{2,19},{3,18},{4,21},{5,20},{6,23},{7,22},{8,25},{9,... | collective-permute-start | bytes 196616 | tf_op jit(solution)/shard_map/ppermute | solution.py:190
  94.8 3.4 %collective-permute-start.24 = (bf16[192,256]{1,0:T(8,128)(2,1)S(1)}, bf16[192,256]{1,0:T(8,128)(2,1)S(1)}, u32[]{:S(2)}, u32[]{:S(2)}) collective-permute-start(bf16[192,256]{1,0:T(8,128)(2,1)S(1)} %get-tuple-element.43), channel_id=1, source_target_pairs={{0,4},{1,5},{2,6},{3,7},{4,0},{5,1},{6,2},{7,3},{8,12},{9,13},{10,... | collective-permute-start | bytes 294920 | tf_op jit(solution)/shard_map/ppermute | solution.py:190
  99.3 3.5 %collective-permute-start.15 = (bf16[96,256]{1,0:T(8,128)(2,1)S(1)}, bf16[96,256]{1,0:T(8,128)(2,1)S(1)}, u32[]{:S(2)}, u32[]{:S(2)}) collective-permute-start(bf16[96,256]{1,0:T(8,128)(2,1)S(1)} %get-tuple-element.55), channel_id=1, source_target_pairs={{0,4},{1,5},{2,6},{3,7},{4,0},{5,1},{6,2},{7,3},{8,12},{9,13},{10,... | collective-permute-start | bytes 147464 | tf_op jit(solution)/shard_map/ppermute | solution.py:190
  102.8 3.2 %collective-permute-start.16 = (bf16[96,256]{1,0:T(8,128)(2,1)S(1)}, bf16[96,256]{1,0:T(8,128)(2,1)S(1)}, u32[]{:S(2)}, u32[]{:S(2)}) collective-permute-start(bf16[96,256]{1,0:T(8,128)(2,1)S(1)} %get-tuple-element.54), channel_id=1, source_target_pairs={{0,6},{1,7},{2,4},{3,5},{4,2},{5,3},{6,0},{7,1},{8,14},{9,15},{10,... | collective-permute-start | bytes 147464 | tf_op jit(solution)/shard_map/ppermute | solution.py:190
  106.7 2.0 %collective-permute-done.16 = bf16[96,256]{1,0:T(8,128)(2,1)S(1)} collective-permute-done((bf16[96,256]{1,0:T(8,128)(2,1)S(1)}, bf16[96,256]{1,0:T(8,128)(2,1)S(1)}, u32[]{:S(2)}, u32[]{:S(2)}) %collective-permute-start.16) | collective-permute-done | bytes 49184 | tf_op jit(solution)/shard_map/ppermute | solution.py:190
  111.5 4.3 %shard_map.116 = bf16[512,1024]{1,0:T(8,128)(2,1)} custom-call(s32[1]{0:T(128)} %bitcast.core_ref.refs_0_, bf16[512,512]{1,0:T(8,128)(2,1)} %get-tuple-element.22.mine_ref, bf16[512,512]{1,0:T(8,128)(2,1)} %copy-done.4, bf16[1024,1024]{1,0:T(8,128)(2,1)} %wq_theirs_ref.1, bf16[1024,1024]{1,0:T(8,128)(2,1)} %wq_theirs_ref.1), custom_call_target="tpu_custom_call" | custom-call | flops 1073741824 | bytes 4194304 | tf_op jit(solution)/shard_map/pallas_call | solution.py:447
  (92 shorter events, 14.1 us)
Async XLA Ops:
  1.4 4.9 %collective-permute-start.2 = (bf16[1,16,1024]{2,1,0:T(8,128)(2,1)S(1)}, bf16[1,16,1024]{2,1,0:T(8,128)(2,1)S(1)}, u32[]{:S(2)}, u32[]{:S(2)}) collective-permute-start(bf16[1,16,1024]{2,1,0:T(8,128)(2,1)S(1)} %dynamic-slice_bitcast_fusion.18), channel_id=1, source_target_pairs={{0,1},{1,0},{2,3},{3,2},{4,5},{5,4},{6,7},{7,6},{8,9},{9,8},{10,11... | collective-permute-start | bytes 98312 | tf_op jit(solution)/shard_map/ppermute | solution.py:190
  4.4 15.7 %collective-permute-start = (bf16[512,1024]{1,0:T(8,128)(2,1)}, bf16[512,1024]{1,0:T(8,128)(2,1)S(1)}, u32[]{:S(2)}, u32[]{:S(2)}) collective-permute-start(bf16[512,1024]{1,0:T(8,128)(2,1)} %refs_8_.1), channel_id=1, source_target_pairs={{0,8},{1,9},{2,10},{3,11},{4,12},{5,13},{6,14},{7,15},{8,0},{9,1},... | collective-permute-start | bytes 3145736 | tf_op jit(solution)/shard_map/ppermute | solution.py:190
  4.4 20.8 %collective-permute-start.1 = (bf16[512,1024]{1,0:T(8,128)(2,1)}, bf16[512,1024]{1,0:T(8,128)(2,1)S(1)}, u32[]{:S(2)}, u32[]{:S(2)}) collective-permute-start(bf16[512,1024]{1,0:T(8,128)(2,1)} %own_ref.6), channel_id=1, source_target_pairs={{0,8},{1,9},{2,10},{3,11},{4,12},{5,13},{6,14},{7,15},{8,0},{9,1},... | collective-permute-start | bytes 3145736 | tf_op jit(solution)/shard_map/ppermute | solution.py:190
  7.1 4.4 %collective-permute-start.3 = (bf16[2,16,1024]{2,1,0:T(8,128)(2,1)S(1)}, bf16[2,16,1024]{2,1,0:T(8,128)(2,1)S(1)}, u32[]{:S(2)}, u32[]{:S(2)}) collective-permute-start(bf16[2,16,1024]{2,1,0:T(8,128)(2,1)S(1)} %pad_maximum_fusion.5), channel_id=1, source_target_pairs={{0,2},{1,3},{2,0},{3,1},{4,6},{5,7},{6,4},{7,5},{8,10},{9,11},{10,... | collective-permute-start | bytes 196616 | tf_op jit(solution)/shard_map/ppermute | solution.py:190
  11.5 6.1 %collective-permute-start.4 = (bf16[4,16,1024]{2,1,0:T(8,128)(2,1)S(1)}, bf16[4,16,1024]{2,1,0:T(8,128)(2,1)S(1)}, u32[]{:S(2)}, u32[]{:S(2)}) collective-permute-start(bf16[4,16,1024]{2,1,0:T(8,128)(2,1)S(1)} %pad_maximum_fusion.2), channel_id=1, source_target_pairs={{0,4},{1,5},{2,6},{3,7},{4,0},{5,1},{6,2},{7,3},{8,12},{9,13},{10,... | collective-permute-start | bytes 393224 | tf_op jit(solution)/shard_map/ppermute | solution.py:190
  17.6 1.6 %collective-permute-start.5 = (bf16[8,16,1024]{2,1,0:T(8,128)(2,1)S(1)}, bf16[8,16,1024]{2,1,0:T(8,128)(2,1)S(1)}, u32[]{:S(2)}, u32[]{:S(2)}) collective-permute-start(bf16[8,16,1024]{2,1,0:T(8,128)(2,1)S(1)} %pad_maximum_fusion.1), channel_id=1, source_target_pairs={{0,8},{1,9},{2,10},{3,11},{4,12},{5,13},{6,14},{7,15},{8,0},{9,1},... | collective-permute-start | bytes 786440 | tf_op jit(solution)/shard_map/ppermute | solution.py:190
  20.1 1.0 copy-start
  25.2 1.0 copy-start.1
  51.2 28.6 %collective-permute-start.20 = (bf16[2,2,2,32,256]{4,3,2,1,0:T(8,128)(2,1)S(1)}, bf16[2,2,2,32,256]{4,3,2,1,0:T(8,128)(2,1)S(1)}, u32[]{:S(2)}, u32[]{:S(2)}) collective-permute-start(bf16[2,2,2,32,256]{4,3,2,1,0:T(8,128)(2,1)S(1)} %get-tuple-element.33), channel_id=1, source_target_pairs={{0,16},{1,17},{2,18},{3,19},{4,20},{5,21},{6,22},{7,23},{8,24},{9,... | collective-permute-start | bytes 393224 | tf_op jit(solution)/shard_map/ppermute | solution.py:190
  54.4 26.8 %collective-permute-start.21 = (bf16[2,2,2,32,256]{4,3,2,1,0:T(8,128)(2,1)S(1)}, bf16[2,2,2,32,256]{4,3,2,1,0:T(8,128)(2,1)S(1)}, u32[]{:S(2)}, u32[]{:S(2)}) collective-permute-start(bf16[2,2,2,32,256]{4,3,2,1,0:T(8,128)(2,1)S(1)} %get-tuple-element.35), channel_id=1, source_target_pairs={{0,1},{1,0},{2,3},{3,2},{4,5},{5,4},{6,7},{7,6},{8,9},{9,8},{10,11... | collective-permute-start | bytes 393224 | tf_op jit(solution)/shard_map/ppermute | solution.py:190
  56.0 13.8 %copy-start.2 = (bf16[512,1024]{1,0:T(8,128)(2,1)S(1)}, bf16[512,1024]{1,0:T(8,128)(2,1)}, u32[]{:S(2)}) copy-start(bf16[512,1024]{1,0:T(8,128)(2,1)} %get-tuple-element.26) | copy-start | bytes 3145732
  64.0 17.3 %copy-start.5 = (bf16[512,512]{1,0:T(8,128)(2,1)S(1)}, bf16[512,512]{1,0:T(8,128)(2,1)}, u32[]{:S(2)}) copy-start(bf16[512,512]{1,0:T(8,128)(2,1)} %get-tuple-element.23) | copy-start | bytes 1572868
  65.2 6.4 %collective-permute-start.7 = (bf16[2,2,2,32,256]{4,3,2,1,0:T(8,128)(2,1)S(1)}, bf16[2,2,2,32,256]{4,3,2,1,0:T(8,128)(2,1)S(1)}, u32[]{:S(2)}, u32[]{:S(2)}) collective-permute-start(bf16[2,2,2,32,256]{4,3,2,1,0:T(8,128)(2,1)S(1)} %get-tuple-element.36), channel_id=1, source_target_pairs={{0,16},{1,17},{2,18},{3,19},{4,20},{5,21},{6,22},{7,23},{8,24},{9,... | collective-permute-start | bytes 393224 | tf_op jit(solution)/shard_map/ppermute | solution.py:190
  65.8 9.1 %collective-permute-start.8 = (bf16[2,2,2,32,256]{4,3,2,1,0:T(8,128)(2,1)S(1)}, bf16[2,2,2,32,256]{4,3,2,1,0:T(8,128)(2,1)S(1)}, u32[]{:S(2)}, u32[]{:S(2)}) collective-permute-start(bf16[2,2,2,32,256]{4,3,2,1,0:T(8,128)(2,1)S(1)} %get-tuple-element.38), channel_id=1, source_target_pairs={{0,1},{1,0},{2,3},{3,2},{4,5},{5,4},{6,7},{7,6},{8,9},{9,8},{10,11... | collective-permute-start | bytes 393224 | tf_op jit(solution)/shard_map/ppermute | solution.py:190
  65.8 12.9 %collective-permute-start.9 = (bf16[2,2,2,32,256]{4,3,2,1,0:T(8,128)(2,1)S(1)}, bf16[2,2,2,32,256]{4,3,2,1,0:T(8,128)(2,1)S(1)}, u32[]{:S(2)}, u32[]{:S(2)}) collective-permute-start(bf16[2,2,2,32,256]{4,3,2,1,0:T(8,128)(2,1)S(1)} %get-tuple-element.37), channel_id=1, source_target_pairs={{0,17},{1,16},{2,19},{3,18},{4,21},{5,20},{6,23},{7,22},{8,25},{9,... | collective-permute-start | bytes 393224 | tf_op jit(solution)/shard_map/ppermute | solution.py:190
  69.9 20.5 %copy-start.3 = (f32[256,1024]{1,0:T(8,128)S(1)}, f32[256,1024]{1,0:T(8,128)}, u32[]{:S(2)}) copy-start(f32[256,1024]{1,0:T(8,128)} %get-tuple-element.25) | copy-start | bytes 3145732
  71.6 9.8 %collective-permute-start.22 = (bf16[2,2,2,32,256]{4,3,2,1,0:T(8,128)(2,1)S(1)}, bf16[2,2,2,32,256]{4,3,2,1,0:T(8,128)(2,1)S(1)}, u32[]{:S(2)}, u32[]{:S(2)}) collective-permute-start(bf16[2,2,2,32,256]{4,3,2,1,0:T(8,128)(2,1)S(1)} %get-tuple-element.34), channel_id=1, source_target_pairs={{0,17},{1,16},{2,19},{3,18},{4,21},{5,20},{6,23},{7,22},{8,25},{9,... | collective-permute-start | bytes 393224 | tf_op jit(solution)/shard_map/ppermute | solution.py:190
  74.9 9.4 %collective-permute-start.17 = (bf16[2,2,32,1024]{3,2,1,0:T(8,128)(2,1)S(1)}, bf16[2,2,32,1024]{3,2,1,0:T(8,128)(2,1)S(1)}, u32[]{:S(2)}, u32[]{:S(2)}) collective-permute-start(bf16[2,2,32,1024]{3,2,1,0:T(8,128)(2,1)S(1)} %get-tuple-element.30), channel_id=1, source_target_pairs={{0,16},{1,17},{2,18},{3,19},{4,20},{5,21},{6,22},{7,23},{8,24},{9,... | collective-permute-start | bytes 786440 | tf_op jit(solution)/shard_map/ppermute | solution.py:190
  78.7 11.3 %collective-permute-start.18 = (bf16[2,2,32,1024]{3,2,1,0:T(8,128)(2,1)S(1)}, bf16[2,2,32,1024]{3,2,1,0:T(8,128)(2,1)S(1)}, u32[]{:S(2)}, u32[]{:S(2)}) collective-permute-start(bf16[2,2,32,1024]{3,2,1,0:T(8,128)(2,1)S(1)} %get-tuple-element.32), channel_id=1, source_target_pairs={{0,1},{1,0},{2,3},{3,2},{4,5},{5,4},{6,7},{7,6},{8,9},{9,8},{10,11... | collective-permute-start | bytes 786440 | tf_op jit(solution)/shard_map/ppermute | solution.py:190
  79.8 10.3 %collective-permute-start.19 = (bf16[2,2,32,1024]{3,2,1,0:T(8,128)(2,1)S(1)}, bf16[2,2,32,1024]{3,2,1,0:T(8,128)(2,1)S(1)}, u32[]{:S(2)}, u32[]{:S(2)}) collective-permute-start(bf16[2,2,32,1024]{3,2,1,0:T(8,128)(2,1)S(1)} %get-tuple-element.31), channel_id=1, source_target_pairs={{0,17},{1,16},{2,19},{3,18},{4,21},{5,20},{6,23},{7,22},{8,25},{9,... | collective-permute-start | bytes 786440 | tf_op jit(solution)/shard_map/ppermute | solution.py:190
  81.3 9.1 %collective-permute-start.10 = (bf16[2,8,8,1024]{3,2,1,0:T(8,128)(2,1)S(1)}, bf16[2,8,8,1024]{3,2,1,0:T(8,128)(2,1)S(1)}, u32[]{:S(2)}, u32[]{:S(2)}) collective-permute-start(bf16[2,8,8,1024]{3,2,1,0:T(8,128)(2,1)S(1)} %fusion.4), channel_id=1, source_target_pairs={{0,8},{1,9},{2,10},{3,11},{4,12},{5,13},{6,14},{7,15},{8,0},{9,1},... | collective-permute-start | bytes 786440 | tf_op jit(solution)/shard_map/ppermute | solution.py:190
  81.4 29.4 %collective-permute-start.6 = (bf16[512,512]{1,0:T(8,128)(2,1)S(1)}, bf16[512,512]{1,0:T(8,128)(2,1)S(1)}, u32[]{:S(2)}, u32[]{:S(2)}) collective-permute-start(bf16[512,512]{1,0:T(8,128)(2,1)S(1)} %copy-done.5), channel_id=1, source_target_pairs={{0,8},{1,9},{2,10},{3,11},{4,12},{5,13},{6,14},{7,15},{8,0},{9,1},... | collective-permute-start | bytes 1572872 | tf_op jit(solution)/shard_map/ppermute | solution.py:190
  90.5 4.3 %collective-permute-start.11 = (bf16[2,2,8,1024]{3,2,1,0:T(8,128)(2,1)S(1)}, bf16[2,2,8,1024]{3,2,1,0:T(8,128)(2,1)S(1)}, u32[]{:S(2)}, u32[]{:S(2)}) collective-permute-start(bf16[2,2,8,1024]{3,2,1,0:T(8,128)(2,1)S(1)} %get-tuple-element.44), channel_id=1, source_target_pairs={{0,16},{1,17},{2,18},{3,19},{4,20},{5,21},{6,22},{7,23},{8,24},{9,... | collective-permute-start | bytes 196616 | tf_op jit(solution)/shard_map/ppermute | solution.py:190
  90.6 7.6 %collective-permute-start.12 = (bf16[2,2,8,1024]{3,2,1,0:T(8,128)(2,1)S(1)}, bf16[2,2,8,1024]{3,2,1,0:T(8,128)(2,1)S(1)}, u32[]{:S(2)}, u32[]{:S(2)}) collective-permute-start(bf16[2,2,8,1024]{3,2,1,0:T(8,128)(2,1)S(1)} %get-tuple-element.46), channel_id=1, source_target_pairs={{0,1},{1,0},{2,3},{3,2},{4,5},{5,4},{6,7},{7,6},{8,9},{9,8},{10,11... | collective-permute-start | bytes 196616 | tf_op jit(solution)/shard_map/ppermute | solution.py:190
  90.7 7.9 %collective-permute-start.13 = (bf16[2,2,8,1024]{3,2,1,0:T(8,128)(2,1)S(1)}, bf16[2,2,8,1024]{3,2,1,0:T(8,128)(2,1)S(1)}, u32[]{:S(2)}, u32[]{:S(2)}) collective-permute-start(bf16[2,2,8,1024]{3,2,1,0:T(8,128)(2,1)S(1)} %get-tuple-element.45), channel_id=1, source_target_pairs={{0,17},{1,16},{2,19},{3,18},{4,21},{5,20},{6,23},{7,22},{8,25},{9,... | collective-permute-start | bytes 196616 | tf_op jit(solution)/shard_map/ppermute | solution.py:190
  94.1 5.2 %collective-permute-start.23 = (bf16[192,256]{1,0:T(8,128)(2,1)S(1)}, bf16[192,256]{1,0:T(8,128)(2,1)S(1)}, u32[]{:S(2)}, u32[]{:S(2)}) collective-permute-start(bf16[192,256]{1,0:T(8,128)(2,1)S(1)} %get-tuple-element.41), channel_id=1, source_target_pairs={{0,2},{1,3},{2,0},{3,1},{4,6},{5,7},{6,4},{7,5},{8,10},{9,11},{10,... | collective-permute-start | bytes 294920 | tf_op jit(solution)/shard_map/ppermute | solution.py:190
  94.8 7.9 %collective-permute-start.24 = (bf16[192,256]{1,0:T(8,128)(2,1)S(1)}, bf16[192,256]{1,0:T(8,128)(2,1)S(1)}, u32[]{:S(2)}, u32[]{:S(2)}) collective-permute-start(bf16[192,256]{1,0:T(8,128)(2,1)S(1)} %get-tuple-element.43), channel_id=1, source_target_pairs={{0,4},{1,5},{2,6},{3,7},{4,0},{5,1},{6,2},{7,3},{8,12},{9,13},{10,... | collective-permute-start | bytes 294920 | tf_op jit(solution)/shard_map/ppermute | solution.py:190
  98.2 7.8 %collective-permute-start.25 = (bf16[192,256]{1,0:T(8,128)(2,1)S(1)}, bf16[192,256]{1,0:T(8,128)(2,1)S(1)}, u32[]{:S(2)}, u32[]{:S(2)}) collective-permute-start(bf16[192,256]{1,0:T(8,128)(2,1)S(1)} %get-tuple-element.42), channel_id=1, source_target_pairs={{0,6},{1,7},{2,4},{3,5},{4,2},{5,3},{6,0},{7,1},{8,14},{9,15},{10,... | collective-permute-start | bytes 294920 | tf_op jit(solution)/shard_map/ppermute | solution.py:190
  98.7 8.0 %collective-permute-start.14 = (bf16[96,256]{1,0:T(8,128)(2,1)S(1)}, bf16[96,256]{1,0:T(8,128)(2,1)S(1)}, u32[]{:S(2)}, u32[]{:S(2)}) collective-permute-start(bf16[96,256]{1,0:T(8,128)(2,1)S(1)} %get-tuple-element.53), channel_id=1, source_target_pairs={{0,2},{1,3},{2,0},{3,1},{4,6},{5,7},{6,4},{7,5},{8,10},{9,11},{10,... | collective-permute-start | bytes 147464 | tf_op jit(solution)/shard_map/ppermute | solution.py:190
  99.3 7.4 %collective-permute-start.15 = (bf16[96,256]{1,0:T(8,128)(2,1)S(1)}, bf16[96,256]{1,0:T(8,128)(2,1)S(1)}, u32[]{:S(2)}, u32[]{:S(2)}) collective-permute-start(bf16[96,256]{1,0:T(8,128)(2,1)S(1)} %get-tuple-element.55), channel_id=1, source_target_pairs={{0,4},{1,5},{2,6},{3,7},{4,0},{5,1},{6,2},{7,3},{8,12},{9,13},{10,... | collective-permute-start | bytes 147464 | tf_op jit(solution)/shard_map/ppermute | solution.py:190
  102.8 5.9 %collective-permute-start.16 = (bf16[96,256]{1,0:T(8,128)(2,1)S(1)}, bf16[96,256]{1,0:T(8,128)(2,1)S(1)}, u32[]{:S(2)}, u32[]{:S(2)}) collective-permute-start(bf16[96,256]{1,0:T(8,128)(2,1)S(1)} %get-tuple-element.54), channel_id=1, source_target_pairs={{0,6},{1,7},{2,4},{3,5},{4,2},{5,3},{6,0},{7,1},{8,14},{9,15},{10,... | collective-permute-start | bytes 147464 | tf_op jit(solution)/shard_map/ppermute | solution.py:190
  108.7 1.3 %collective-permute-start.26 = (f32[2,32,256]{2,1,0:T(8,128)S(1)}, f32[2,32,256]{2,1,0:T(8,128)S(1)}, u32[]{:S(2)}, u32[]{:S(2)}) collective-permute-start(f32[2,32,256]{2,1,0:T(8,128)S(1)} %get-tuple-element.60), channel_id=1, source_target_pairs={{0,8},{1,9},{2,10},{3,11},{4,12},{5,13},{6,14},{7,15},{8,0},{9,1},... | collective-permute-start | bytes 196616 | tf_op jit(solution)/shard_map/ppermute | solution.py:190
  (1 other events, 0.8 us)

commit v4 on v1

v4 whole, which is shorter than its diff:
```python
from functools import partial

import jax
import jax.numpy as jnp
from jax import lax
from jax.experimental import pallas as pl
from jax.experimental.pallas import tpu as pltpu
from jax.sharding import PartitionSpec as P


HEADS = 16
TVIEWS = 8
CVIEWS = 16
AXES = ("grp", "seq")
GROUP = 2

F32 = jnp.float32
BF16 = jnp.bfloat16


def dot(left, right, dims):
    return lax.dot_general(left, right, (dims, ((), ())), preferred_element_type=F32)


def owned(core_ref, at, size, block):
    return pl.ds(pl.multiple_of((2 * (at // block) + core_ref[0]) * block + at % block, size), size)


def query_kernel(block, core_ref, weight_ref, own_ref, partner_ref, out_ref):
    rows = own_ref.shape[0]
    for at in range(0, out_ref.shape[0], block):
        weight = weight_ref[:, owned(core_ref, at, block, block)]
        part = pl.ds(at, block)
        out_ref[part, :rows] = dot(own_ref[...], weight, ((1,), (0,))).astype(BF16).T
        out_ref[part, rows:] = dot(partner_ref[...], weight, ((1,), (0,))).astype(BF16).T


def grad_kernel(block, core_ref, weight_ref, own_ref, partner_ref, out_ref):
    rows = own_ref.shape[0]
    for at in range(0, out_ref.shape[0], block):
        weight = weight_ref[owned(core_ref, at, block, block), :]
        part = pl.ds(at, block)
        out_ref[part, :rows] = dot(weight, own_ref[...], ((1,), (1,))).astype(BF16)
        out_ref[part, rows:] = dot(weight, partner_ref[...], ((1,), (1,))).astype(BF16)


def attend_kernel(
    block,
    size,
    scale,
    core_ref,
    context_ref,
    wk_ref,
    wv_ref,
    q_ref,
    own_ref,
    partner_ref,
    bias_ref,
    kv_ref,
    probs_ref,
    att_ref,
    wo_ref,
):
    block_rows = own_ref.shape[0]
    rows = 2 * block_rows
    width = GROUP * size
    context = context_ref[...]
    bias = bias_ref[...]
    lane = lax.broadcasted_iota(jnp.int32, (16, rows), 1)
    line = lax.broadcasted_iota(jnp.int32, (16, rows), 0)
    marks = jnp.where(lane // block_rows == line, 1.0, 0.0).astype(BF16)

    def keys_values(at):
        cols = owned(core_ref, at, width, block)
        weight = jnp.concatenate([wk_ref[:, cols], wv_ref[:, cols]], axis=1)
        both = dot(context, weight, ((1,), (0,))).astype(BF16)
        key_part = (both[:, :width].astype(F32) * scale).astype(BF16)
        kv_ref[0, pl.ds(at, width), :] = key_part.T
        kv_ref[1, pl.ds(at, width), :] = both[:, width:].T

    def out_product(at, depth):
        part = pl.ds(at, depth)
        total = dot(att_ref[part, :block_rows], own_ref[...], ((1,), (0,)))
        total += dot(att_ref[part, block_rows:], partner_ref[...], ((1,), (0,)))
        wo_ref[part, :] = total.astype(BF16)

    half_width = q_ref.shape[0]
    keys_values(0)
    for at in range(0, half_width, width):
        if at + width < half_width:
            keys_values(at + width)
        for first in range(at, at + width, size):
            part = pl.ds(first, size)
            key_rows = jnp.concatenate([kv_ref[0, part, :], bias], axis=0)
            query_rows = jnp.concatenate([q_ref[part, :], marks], axis=0)
            scores = dot(key_rows.T, query_rows, ((1,), (0,)))
            row_max = jnp.max(scores, axis=0, keepdims=True)
            unnormed = jnp.exp(scores - row_max)
            row_sum = jnp.sum(unnormed, axis=0, keepdims=True)
            probs = (unnormed * (1.0 / row_sum)).astype(BF16)
            probs_ref[first // size] = probs
            att_ref[part, :] = dot(kv_ref[1, part, :], probs, ((1,), (0,))).astype(BF16)
        if (at // width) % 2 == 1:
            out_product(at - width, 2 * width)


def back_kernel(
    block,
    size,
    scale,
    core_ref,
    wk_ref,
    wv_ref,
    q_ref,
    g_ref,
    kv_ref,
    probs_ref,
    att_ref,
    qg_own_ref,
    qg_partner_ref,
    kept_ref,
    sent_ref,
    sum_ref,
):
    half_width = q_ref.shape[0]
    block_rows = qg_own_ref.shape[1]
    width = GROUP * size
    for at in range(0, half_width, width):
        key_parts, value_parts = [], []
        for first in range(at, at + width, size):
            part = pl.ds(first, size)
            grad = g_ref[part, :]
            probs = probs_ref[first // size]
            attended = att_ref[part, :].astype(F32)
            row_dot = jnp.sum(attended * grad.astype(F32), axis=0, keepdims=True)
            grad_scores = dot(kv_ref[1, part, :].T, grad, ((1,), (0,)))
            value_parts.append(dot(grad, probs, ((1,), (1,))))
            logits = (probs.astype(F32) * (grad_scores - row_dot)).astype(BF16)
            query_grad = dot(kv_ref[0, part, :], logits, ((1,), (0,))).astype(BF16)
            qg_own_ref[part, :] = query_grad[:, :block_rows]
            qg_partner_ref[part, :] = query_grad[:, block_rows:]
            key_parts.append(dot(q_ref[part, :], logits, ((1,), (1,))) * scale)
        cols = owned(core_ref, at, width, block)
        grads = jnp.concatenate(key_parts + value_parts, axis=0).astype(BF16).T
        weight = jnp.concatenate([wk_ref[:, cols], wv_ref[:, cols]], axis=1)
        term = dot(grads, weight, ((1,), (1,)))
        if at == 0:
            sum_ref[...] = term
        else:
            sum_ref[...] += term
    out_block = kept_ref.shape[1]
    for high in range(kept_ref.shape[0]):
        kept = pl.multiple_of((2 * high + core_ref[0]) * out_block, out_block)
        sent = pl.multiple_of((2 * high + 1 - core_ref[0]) * out_block, out_block)
        kept_ref[high] = sum_ref[pl.ds(kept, out_block), :]
        sent_ref[high] = sum_ref[pl.ds(sent, out_block), :].astype(BF16)


def weight_kernel(qg_own_ref, qg_partner_ref, own_ref, partner_ref, out_ref):
    step = min(256, qg_own_ref.shape[0])
    for at in range(0, qg_own_ref.shape[0], step):
        part = pl.ds(at, step)
        total = dot(qg_own_ref[part, :], own_ref[...], ((1,), (0,)))
        total += dot(qg_partner_ref[part, :], partner_ref[...], ((1,), (0,)))
        out_ref[:, part] = total.astype(BF16).T


def targets_kernel(block, core_ref, mine_ref, theirs_ref, weight_ref, out_ref):
    other_ref = [1 - core_ref[0]]
    total = None
    for at in range(0, mine_ref.shape[0], block):
        part = pl.ds(at, block)
        for source, core in ((mine_ref, core_ref), (theirs_ref, other_ref)):
            weight = weight_ref[:, owned(core, at, block, block)]
            term = dot(source[part, :].T, weight, ((1,), (1,)))
            total = term if total is None else total + term
    out_ref[...] = total.astype(BF16)


def on_device(targets, context, w_query, w_key, w_value, w_out, visible, grad_out):
    query_rows, width = targets.shape
    head_size = width // HEADS
    score_scale = head_size ** (-0.5)
    grp_count = lax.axis_size("grp")
    seq_count = lax.axis_size("seq")
    device_count = grp_count * seq_count
    grp = lax.axis_index("grp")
    seq = lax.axis_index("seq")
    me = grp * seq_count + seq
    core = grp % 2
    core_mask = seq_count
    high_count = grp_count // 2
    half_width = width // 2
    half_heads = HEADS // 2
    block = width // grp_count
    context_rows = context.shape[0] * seq_count
    rows = 2 * query_rows
    core_index = core.reshape(1).astype(jnp.int32)
    limit = (10 << 20) + 6 * 4 * context_rows * rows

    def swap(array, mask):
        return lax.ppermute(array, AXES, [(i, i ^ mask) for i in range(device_count)])

    def bit_of(mask):
        return (me // mask) % 2

    def call(kernel, operands, outs, flops, scratch=()):
        in_vmem = pl.BlockSpec(memory_space=pltpu.VMEM)
        scalar = pl.BlockSpec(memory_space=pltpu.SMEM)
        specs = [scalar if one is core_index else in_vmem for one in operands]
        return pl.pallas_call(
            kernel,
            in_specs=specs,
            out_specs=[in_vmem] * len(outs),
            out_shape=[jax.ShapeDtypeStruct(shape, kind) for shape, kind in outs],
            scratch_shapes=scratch,
            compiler_params=pltpu.CompilerParams(vmem_limit_bytes=limit),
            cost_estimate=pl.CostEstimate(flops=flops, bytes_accessed=1 << 20, transcendentals=0),
        )(*operands)

    own_half = context.shape[0] // 2
    held = lax.dynamic_slice_in_dim(context, core * own_half, own_half, 0)[None]
    targets_swapped = None
    mask = 1
    while mask < seq_count:
        other = swap(held, mask)
        if targets_swapped is None:
            targets_swapped = swap(targets, core_mask)
            grad_swapped = swap(grad_out, core_mask)
        upper = bit_of(mask) == 1
        held = jnp.concatenate(
            [jnp.where(upper, other, held), jnp.where(upper, held, other)], axis=0
        )
        mask *= 2
    other = swap(held, core_mask)
    held = jnp.stack(
        [jnp.where(core == 1, other, held), jnp.where(core == 1, held, other)], axis=1
    )
    context_all = held.reshape(context_rows, width)

    product = 2 * half_width * rows * width
    attention = 8 * half_width * rows * context_rows
    (queries,) = call(
        partial(query_kernel, block),
        [core_index, w_query, targets, targets_swapped],
        [((half_width, rows), BF16)],
        product,
    )
    (grads,) = call(
        partial(grad_kernel, block),
        [core_index, w_out, grad_out, grad_swapped],
        [((half_width, rows), BF16)],
        product,
    )

    view_rows = query_rows * device_count // TVIEWS
    context_view = context_rows // CVIEWS
    firsts = jnp.stack([me, me ^ core_mask]) * query_rows // view_rows
    view_hot = firsts[:, None] == jnp.arange(TVIEWS)
    seen = jnp.sum(jnp.where(view_hot[:, :, None], visible[None], 0), axis=1)
    key_hot = jnp.arange(context_rows)[:, None] // context_view == jnp.arange(CVIEWS)
    seen = jnp.sum(jnp.where(key_hot[None], seen[:, None, :], 0), axis=2)
    bias = jnp.where(seen == 1, 0.0, -1e30).astype(BF16)
    bias = jnp.concatenate([bias, jnp.zeros((14, context_rows), BF16)], axis=0)

    key_values, probs, attended, wo_term = call(
        partial(attend_kernel, block, head_size, score_scale),
        [core_index, context_all, w_key, w_value, queries, grad_out, grad_swapped, bias],
        [
            ((2, half_width, context_rows), BF16),
            ((half_heads, context_rows, rows), BF16),
            ((half_width, rows), BF16),
            ((half_width, width), BF16),
        ],
        product + attention,
    )

    high_masks = []
    mask = core_mask * high_count
    while mask > core_mask:
        high_masks.append(mask)
        mask //= 2
    seq_masks = []
    mask = seq_count // 2
    while mask >= 1:
        seq_masks.append(mask)
        mask //= 2
    all_masks = high_masks + seq_masks
    high_bits = [2] * len(high_masks)
    seq_bits = [2] * len(seq_masks)
    order = [high_masks[-1], seq_masks[-1]] + seq_masks[-2::-1] + high_masks[:-1]
    stages = [tuple(order[at : at + 2]) for at in range(0, len(order), 2)]

    def exchange(array, masks, stage, last=False):
        def piece(flips):
            part = array
            for mask, flip in sorted(zip(stage, flips), key=lambda one: -masks.index(one[0])):
                at = (bit_of(mask) + flip) % 2
                part = lax.dynamic_index_in_dim(part, at, masks.index(mask), keepdims=False)
            return part

        moved = []
        for way in range(1, 2 ** len(stage)):
            flips = [way >> at & 1 for at in range(len(stage))]
            target = sum(mask for mask, flip in zip(stage, flips) if flip)
            moved.append(swap(piece(flips), target))
        total = piece([0] * len(stage)).astype(F32)
        for one in moved:
            total = total + one.astype(F32)
        left = [mask for mask in masks if mask not in stage]
        return (total if last else total.astype(BF16)), left

    def exchange_rest(array, masks):
        for at, stage in enumerate(stages[1:]):
            array, masks = exchange(array, masks, stage, at == len(stages) - 2)
        return array

    out_rows = width // device_count
    ctx_out = context_rows // device_count

    wo_split = wo_term.reshape(*high_bits, *seq_bits, out_rows, width)
    wo_part, left_masks = exchange(wo_split, all_masks, stages[0])
    grad_wo = exchange_rest(wo_part, left_masks)

    query_own, query_partner, ctx_kept, ctx_sent = call(
        partial(back_kernel, block, head_size, score_scale),
        [core_index, w_key, w_value, queries, grads, key_values, probs, attended],
        [
            ((half_width, query_rows), BF16),
            ((half_width, query_rows), BF16),
            ((high_count, seq_count * ctx_out, width), F32),
            ((high_count, seq_count * ctx_out, width), BF16),
        ],
        product // 2 + attention,
        scratch=[pltpu.VMEM((context_rows, width), F32)],
    )
    ctx_moved = swap(ctx_sent, core_mask)
    (wq_term,) = call(
        weight_kernel,
        [query_own, query_partner, targets, targets_swapped],
        [((width, half_width), BF16)],
        product,
    )
    ctx_pair = (ctx_kept + ctx_moved.astype(F32)).astype(BF16)
    ctx_pair = ctx_pair.reshape(*high_bits, *seq_bits, ctx_out, width)
    wq_split = wq_term.reshape(high_count, 2, seq_count, out_rows, half_width)
    tail = [wq_split[:, which].reshape(*high_bits, *seq_bits, out_rows, half_width) for which in (0, 1)]
    tail += [ctx_pair[..., :half_width], ctx_pair[..., half_width:]]
    tail, _ = exchange(jnp.concatenate(tail, axis=-2), all_masks, stages[0])
    tail = exchange_rest(tail, left_masks)

    wq_sums = tail[: 2 * out_rows].reshape(2, out_rows, half_width)
    sent = lax.dynamic_index_in_dim(wq_sums, 1 - core, 0, keepdims=False)
    mine = lax.dynamic_index_in_dim(wq_sums, core, 0, keepdims=False)
    theirs = swap(sent, core_mask)
    pieces = []
    for at in range(0, half_width, block):
        pieces.append(jnp.where(core == 0, mine[:, at : at + block], theirs[:, at : at + block]))
        pieces.append(jnp.where(core == 0, theirs[:, at : at + block], mine[:, at : at + block]))
    grad_wq = jnp.concatenate(pieces, axis=1)
    ctx_sums = tail[2 * out_rows :]
    d_context = jnp.concatenate([ctx_sums[:ctx_out], ctx_sums[ctx_out:]], axis=1).astype(BF16)

    returned = swap(query_partner, core_mask)
    (d_targets,) = call(
        partial(targets_kernel, block),
        [core_index, query_own, returned, w_query],
        [((query_rows, width), BF16)],
        product,
    )
    return (d_targets, d_context, grad_wq, grad_wo)


def solution(mesh):
    in_specs = (
        P(AXES, None),
        P("seq", None),
        P(),
        P(),
        P(),
        P(),
        P(),
        P(AXES, None),
    )
    out_specs = (P(AXES, None), P(AXES, None), P(AXES, None), P(AXES, None))

    return jax.shard_map(
        on_device, mesh=mesh, in_specs=in_specs, out_specs=out_specs, check_vma=False
    )
```

time: 126 us -> 86.4 us (0.69)
  local copies, waits for them, and re-layouts: 29.5 us -> 3.85 us
  matrix products: 16.6 us -> 0 us
  waiting for transfers between devices: 29.6 us -> 20.9 us
  other arithmetic: 1.96 us -> 9.23 us
  starting transfers between devices: 21.1 us -> 26.6 us
    dot_general x7 -> x0, matrix products: 16.6 us -> none  [dot(): lax.dot_general(left, right, (dims, ((), ())), preferred_element_type=F32)]
    unnamed x40 -> x22, local copies, waits for them, and re-layouts: 17.4 us -> 1.17 us
    ppermute x21, waiting for transfers between devices: 29.6 us -> 20.9 us  [swap(): lax.ppermute(array, AXES, [(i, i ^ mask) for i in range(device_count)])]
    ppermute x21, starting transfers between devices: 21.1 us -> 26.6 us  [swap(): lax.ppermute(array, AXES, [(i, i ^ mask) for i in range(device_count)])]
    dynamic_slice x7 -> x0, local copies, waits for them, and re-layouts: 4.48 us -> none  [the longest x2 4.26 us: columns_of(): lax.dynamic_index_in_dim(split, which, 2, keepdims=False)]
    concatenate x2 -> x1, local copies, waits for them, and re-layouts: 2.59 us -> 0.01 us  [on_device(): bias = jnp.concatenate([bias, jnp.zeros((14, context_rows), BF16)], axis=0)]
    squeeze x7 -> x5, local copies, waits for them, and re-layouts: 0.13 us -> 1.79 us  [the longest x4 1.78 us: piece(): part = lax.dynamic_index_in_dim(part, at, masks.index(mask), keepdims=False)]
    select_n x3, other arithmetic: 0.05 us -> 1.71 us  [on_device(): jnp.where(upper, other, held)]
  transfers between devices with their start and end apart: 21 -> 21, of which waited for: 10 -> 11; matrix products, arithmetic and copies ran while one was open for 25% -> 12% of each run, Pallas kernels for 0% -> 19%
where the time goes in v4:
time: 86.4 us; the launch traced here: 85.9 us
  starting transfers between devices  26.6 us (31%)
  Pallas kernels  24.1 us (28%)
  waiting for transfers between devices  20.9 us (24%)
  other arithmetic  9.23 us (11%)
  local copies, waits for them, and re-layouts  3.85 us (4%)
  between operations  1.18 us (1%)
    ppermute x21, starting transfers between devices, swap(): lax.ppermute(array, AXES, [(i, i ^ mask) for i in range(device_count)])  26.6 us
    pallas_call x6, Pallas kernels, call(): pl.pallas_call(kernel, in_specs=specs, out_specs=[in_vmem] * len(outs), o...  24.1 us
    ppermute x21, waiting for transfers between devices, swap(): lax.ppermute(array, AXES, [(i, i ^ mask) for i in range(device_count)])  20.9 us
    squeeze x4, local copies, waits for them, and re-layouts, piece(): part = lax.dynamic_index_in_dim(part, at, masks.index(mask), keepdims=False)  1.78 us
  transfers between devices with their start and end apart: 21, of which 11 were waited for; matrix products, arithmetic and copies ran while one was open for 12% of the time, Pallas kernels for 19%

profile of v4, /device:TPU:0, one launch (start us, length us, event | category | flops | bytes accessed | tf_op | source)
XLA Modules:
  0.0 85.9 jit_solution(17455119453012889420)
XLA Ops:
  1.4 3.0 %collective-permute-start.2 = (bf16[1,16,1024]{2,1,0:T(8,128)(2,1)S(1)}, bf16[1,16,1024]{2,1,0:T(8,128)(2,1)S(1)}, u32[]{:S(2)}, u32[]{:S(2)}) collective-permute-start(bf16[1,16,1024]{2,1,0:T(8,128)(2,1)S(1)} %dynamic-slice_bitcast_fusion.14), channel_id=1, source_target_pairs={{0,1},{1,0},{2,3},{3,2},{4,5},{5,4},{6,7},{7,6},{8,9},{9,8},{10,11... | collective-permute-start | bytes 98312 | tf_op jit(solution)/shard_map/ppermute | solution.py:202
  5.0 1.3 %collective-permute-done.2 = bf16[1,16,1024]{2,1,0:T(8,128)(2,1)S(1)} collective-permute-done((bf16[1,16,1024]{2,1,0:T(8,128)(2,1)S(1)}, bf16[1,16,1024]{2,1,0:T(8,128)(2,1)S(1)}, u32[]{:S(2)}, u32[]{:S(2)}) %collective-permute-start.2) | collective-permute-done | bytes 32800 | tf_op jit(solution)/shard_map/ppermute | solution.py:202
  7.1 2.1 %collective-permute-start.3 = (bf16[2,16,1024]{2,1,0:T(8,128)(2,1)S(1)}, bf16[2,16,1024]{2,1,0:T(8,128)(2,1)S(1)}, u32[]{:S(2)}, u32[]{:S(2)}) collective-permute-start(bf16[2,16,1024]{2,1,0:T(8,128)(2,1)S(1)} %pad_maximum_fusion.5), channel_id=1, source_target_pairs={{0,2},{1,3},{2,0},{3,1},{4,6},{5,7},{6,4},{7,5},{8,10},{9,11},{10,... | collective-permute-start | bytes 196616 | tf_op jit(solution)/shard_map/ppermute | solution.py:202
  9.3 2.2 %collective-permute-done.3 = bf16[2,16,1024]{2,1,0:T(8,128)(2,1)S(1)} collective-permute-done((bf16[2,16,1024]{2,1,0:T(8,128)(2,1)S(1)}, bf16[2,16,1024]{2,1,0:T(8,128)(2,1)S(1)}, u32[]{:S(2)}, u32[]{:S(2)}) %collective-permute-start.3) | collective-permute-done | bytes 65568 | tf_op jit(solution)/shard_map/ppermute | solution.py:202
  11.6 3.1 %collective-permute-start.4 = (bf16[4,16,1024]{2,1,0:T(8,128)(2,1)S(1)}, bf16[4,16,1024]{2,1,0:T(8,128)(2,1)}, u32[]{:S(2)}, u32[]{:S(2)}) collective-permute-start(bf16[4,16,1024]{2,1,0:T(8,128)(2,1)S(1)} %pad_maximum_fusion.3), channel_id=1, source_target_pairs={{0,4},{1,5},{2,6},{3,7},{4,0},{5,1},{6,2},{7,3},{8,12},{9,13},{10,... | collective-permute-start | bytes 393224 | tf_op jit(solution)/shard_map/ppermute | solution.py:202
  15.5 2.2 %collective-permute-done.4 = bf16[4,16,1024]{2,1,0:T(8,128)(2,1)} collective-permute-done((bf16[4,16,1024]{2,1,0:T(8,128)(2,1)S(1)}, bf16[4,16,1024]{2,1,0:T(8,128)(2,1)}, u32[]{:S(2)}, u32[]{:S(2)}) %collective-permute-start.4) | collective-permute-done | bytes 131104 | tf_op jit(solution)/shard_map/ppermute | solution.py:202
  17.7 0.9 %broadcast_select_fusion.1 = (bf16[4,16,1024]{2,1,0:T(8,128)(2,1)S(1)}, bf16[4,16,1024]{2,1,0:T(8,128)(2,1)S(1)}) fusion(bf16[4,16,1024]{2,1,0:T(8,128)(2,1)} %collective-permute-done.4, pred[]{:T(512)S(6)} %eq.129, bf16[2,16,1024]{2,1,0:T(8,128)(2,1)S(1)} %get-tuple-element.49, bf16[2,16,1024]{2,1,0:T(8,128)(2,1)S(1)} %get-tuple-element.48), kind=kLoop, calls=%fused_computation.29 | loop fusion | flops 196608 | bytes 524289 | tf_op jit(solution)/shard_map/jit(_where)/select_n | solution.py:232
  19.6 1.6 %collective-permute-done.5 = bf16[8,16,1024]{2,1,0:T(8,128)(2,1)} collective-permute-done((bf16[8,16,1024]{2,1,0:T(8,128)(2,1)}, bf16[8,16,1024]{2,1,0:T(8,128)(2,1)}, u32[]{:S(2)}, u32[]{:S(2)}) %collective-permute-start.5) | collective-permute-done | bytes 262176 | tf_op jit(solution)/shard_map/ppermute | solution.py:202
  21.2 1.0 %select_bitcast_fusion.1 = (bf16[8,1,16,1024]{3,2,1,0:T(8,128)(2,1)S(1)}, bf16[8,1,16,1024]{3,2,1,0:T(8,128)(2,1)S(1)}) fusion(bf16[8,16,1024]{2,1,0:T(8,128)(2,1)} %collective-permute-done.5, pred[]{:T(512)S(6)} %eq.128, bf16[4,16,1024]{2,1,0:T(8,128)(2,1)S(1)} %get-tuple-element.41, bf16[4,16,1024]{2,1,0:T(8,128)(2,1)S(1)} %get-tuple-element.40), kind=kLoop, calls=%fused_computation.19 | loop fusion | flops 393216 | bytes 1048577 | tf_op jit(solution)/shard_map/stack | solution.py:236
  22.4 2.7 %shard_map.111.q_ref = bf16[512,1024]{1,0:T(8,128)(2,1)S(1)} custom-call(s32[1]{0:T(128)} %bitcast.core_ref, bf16[1024,1024]{1,0:T(8,128)(2,1)S(1)} %copy-done, bf16[512,1024]{1,0:T(8,128)(2,1)S(1)} %copy-done.1, bf16[512,1024]{1,0:T(8,128)(2,1)} %collective-permute-done.partner_ref), custom_call_target="tpu_custom_call" | custom-call | flops 1073741824 | bytes 1048576 | tf_op jit(solution)/shard_map/pallas_call | solution.py:211
  25.1 7.4 %shard_map.113 = (bf16[2,512,256]{2,1,0:T(8,128)(2,1)S(1)}, bf16[8,256,1024]{2,1,0:T(8,128)(2,1)S(1)}, bf16[512,1024]{1,0:T(8,128)(2,1)S(1)}, bf16[512,1024]{1,0:T(8,128)(2,1)S(1)}) custom-call(s32[1]{0:T(128)} %bitcast.core_ref, bf16[256,1024]{1,0:T(8,128)(2,1)S(1)} %bitcast.70, bf16[1024,1024]{1,0:T(8,128)(2,1)S(1)} %copy-done.3, ...), custom_call_target="tpu_custom_call" | custom-call | flops 2147483648 | bytes 1048576 | tf_op jit(solution)/shard_map/pallas_call | solution.py:211
  32.7 3.3 %collective-permute-start.15 = (bf16[2,2,32,1024]{3,2,1,0:T(8,128)(2,1)S(1)}, bf16[2,2,32,1024]{3,2,1,0:T(8,128)(2,1)S(1)}, u32[]{:S(2)}, u32[]{:S(2)}) collective-permute-start(bf16[2,2,32,1024]{3,2,1,0:T(8,128)(2,1)S(1)} %get-tuple-element.25), channel_id=1, source_target_pairs={{0,16},{1,17},{2,18},{3,19},{4,20},{5,21},{6,22},{7,23},{8,24},{9,... | collective-permute-start | bytes 786440 | tf_op jit(solution)/shard_map/ppermute | solution.py:202
  35.9 1.5 %collective-permute-start.16 = (bf16[2,2,32,1024]{3,2,1,0:T(8,128)(2,1)S(1)}, bf16[2,2,32,1024]{3,2,1,0:T(8,128)(2,1)S(1)}, u32[]{:S(2)}, u32[]{:S(2)}) collective-permute-start(bf16[2,2,32,1024]{3,2,1,0:T(8,128)(2,1)S(1)} %get-tuple-element.27), channel_id=1, source_target_pairs={{0,1},{1,0},{2,3},{3,2},{4,5},{5,4},{6,7},{7,6},{8,9},{9,8},{10,11... | collective-permute-start | bytes 786440 | tf_op jit(solution)/shard_map/ppermute | solution.py:202
  37.5 2.5 %shard_map.112.g_ref = bf16[512,1024]{1,0:T(8,128)(2,1)S(1)} custom-call(s32[1]{0:T(128)} %bitcast.core_ref, bf16[1024,1024]{1,0:T(8,128)(2,1)S(1)} %copy-done.2, bf16[512,1024]{1,0:T(8,128)(2,1)S(1)} %copy-done.7, bf16[512,1024]{1,0:T(8,128)(2,1)} %collective-permute-done.1.partner_ref), custom_call_target="tpu_custom_call" | custom-call | flops 1073741824 | bytes 1048576 | tf_op jit(solution)/shard_map/pallas_call | solution.py:211
  40.0 6.3 %shard_map.114 = (bf16[512,512]{1,0:T(8,128)(2,1)S(1)}, bf16[512,512]{1,0:T(8,128)(2,1)S(1)}, f32[2,64,1024]{2,1,0:T(8,128)S(1)}, bf16[2,64,1024]{2,1,0:T(8,128)(2,1)S(1)}) custom-call(s32[1]{0:T(128)} %bitcast.core_ref, bf16[1024,1024]{1,0:T(8,128)(2,1)S(1)} %copy-done.3, bf16[1024,1024]{1,0:T(8,128)(2,1)S(1)} %copy-done.4, ...), custom_call_target="tpu_custom_call" | custom-call | flops 1610612736 | bytes 1048576 | tf_op jit(solution)/shard_map/pallas_call | solution.py:211
  46.4 2.8 %shard_map.116 = bf16[1024,512]{1,0:T(8,128)(2,1)S(1)} custom-call(bf16[512,512]{1,0:T(8,128)(2,1)S(1)} %get-tuple-element.15.mine_ref.qg_own_ref, bf16[512,512]{1,0:T(8,128)(2,1)S(1)} %get-tuple-element.16.qg_partner_ref, bf16[512,1024]{1,0:T(8,128)(2,1)S(1)} %copy-done.1, bf16[512,1024]{1,0:T(8,128)(2,1)} %collective-permute-done.partner_ref), custom_call_target="tpu_custom_call" | custom-call | flops 1073741824 | bytes 1048576 | tf_op jit(solution)/shard_map/pallas_call | solution.py:211
  50.5 0.9 %collective-permute-start.18 = (bf16[32,1024]{1,0:T(8,128)(2,1)S(1)}, bf16[32,1024]{1,0:T(8,128)(2,1)S(1)}, u32[]{:S(2)}, u32[]{:S(2)}) collective-permute-start(bf16[32,1024]{1,0:T(8,128)(2,1)S(1)} %get-tuple-element.35), channel_id=1, source_target_pairs={{0,2},{1,3},{2,0},{3,1},{4,6},{5,7},{6,4},{7,5},{8,10},{9,11},{10,... | collective-permute-start | bytes 196616 | tf_op jit(solution)/shard_map/ppermute | solution.py:202
  51.6 1.1 %copy-done.10 = bf16[2,2,2,2,80,512]{5,4,3,2,1,0:T(8,128)(2,1)} copy-done((bf16[2,2,2,2,80,512]{5,4,3,2,1,0:T(8,128)(2,1)}, bf16[2,2,2,2,80,512]{5,4,3,2,1,0:T(8,128)(2,1)S(1)}, u32[]{:S(2)}) %copy-start.10) | copy-done | bytes 1310744
  52.7 1.0 %dynamic-slice_bitcast_fusion.2 = (bf16[2,2,80,512]{3,2,1,0:T(8,128)(2,1)}, bf16[2,2,80,512]{3,2,1,0:T(8,128)(2,1)}, bf16[2,2,80,512]{3,2,1,0:T(8,128)(2,1)}) fusion(bf16[2,2,2,2,80,512]{5,4,3,2,1,0:T(8,128)(2,1)S(1)} %pad_maximum_fusion, s32[]{:T(128)S(6)} %select_n.422, s32[]{:T(128)S(6)} %select_n.419, s32[]{:T(128)S(6)} %select_n.425, s32[]{:T(128)S(6)} %select_n.416), kind=kLoop, calls=%fused_computation.13 | loop fusion | bytes 1966096 | tf_op jit(solution)/shard_map/jit(dynamic_index_in_dim)/squeeze | solution.py:299
  53.7 2.4 %collective-permute-start.10 = (bf16[2,2,80,512]{3,2,1,0:T(8,128)(2,1)}, bf16[2,2,80,512]{3,2,1,0:T(8,128)(2,1)}, u32[]{:S(2)}, u32[]{:S(2)}) collective-permute-start(bf16[2,2,80,512]{3,2,1,0:T(8,128)(2,1)} %get-tuple-element.23), channel_id=1, source_target_pairs={{0,17},{1,16},{2,19},{3,18},{4,21},{5,20},{6,23},{7,22},{8,25},{9,... | collective-permute-start | bytes 983048 | tf_op jit(solution)/shard_map/ppermute | solution.py:202
  57.2 3.5 %collective-permute-start.19 = (bf16[32,1024]{1,0:T(8,128)(2,1)}, bf16[32,1024]{1,0:T(8,128)(2,1)}, u32[]{:S(2)}, u32[]{:S(2)}) collective-permute-start(bf16[32,1024]{1,0:T(8,128)(2,1)} %get-tuple-element.37), channel_id=1, source_target_pairs={{0,4},{1,5},{2,6},{3,7},{4,0},{5,1},{6,2},{7,3},{8,12},{9,13},{10,... | collective-permute-start | bytes 196616 | tf_op jit(solution)/shard_map/ppermute | solution.py:202
  60.7 4.3 %collective-permute-done.19 = bf16[32,1024]{1,0:T(8,128)(2,1)} collective-permute-done((bf16[32,1024]{1,0:T(8,128)(2,1)}, bf16[32,1024]{1,0:T(8,128)(2,1)}, u32[]{:S(2)}, u32[]{:S(2)}) %collective-permute-start.19) | collective-permute-done | bytes 65568 | tf_op jit(solution)/shard_map/ppermute | solution.py:202
  65.0 1.9 %collective-permute-done.20 = bf16[32,1024]{1,0:T(8,128)(2,1)} collective-permute-done((bf16[32,1024]{1,0:T(8,128)(2,1)S(1)}, bf16[32,1024]{1,0:T(8,128)(2,1)}, u32[]{:S(2)}, u32[]{:S(2)}) %collective-permute-start.20) | collective-permute-done | bytes 65568 | tf_op jit(solution)/shard_map/ppermute | solution.py:202
  66.8 1.6 %fusion.9 = f32[32,1024]{1,0:T(8,128)} fusion(bf16[32,1024]{1,0:T(8,128)(2,1)} %collective-permute-done.20, bf16[32,1024]{1,0:T(8,128)(2,1)} %collective-permute-done.19, bf16[32,1024]{1,0:T(8,128)(2,1)S(1)} %collective-permute-done.18, bf16[2,2,32,1024]{3,2,1,0:T(8,128)(2,1)S(1)} %fusion.5, s32[]{:T(128)S(6)} %select_n.428, s32[]{:T(128)S(6)} %select_n.431), kind=kLoop, calls=%fused_computation.27 | loop fusion | flops 229376 | bytes 393224 | tf_op jit(solution)/shard_map/add | solution.py:309
  68.4 3.2 %collective-permute-done.8 = bf16[2,2,80,512]{3,2,1,0:T(8,128)(2,1)} collective-permute-done((bf16[2,2,80,512]{3,2,1,0:T(8,128)(2,1)}, bf16[2,2,80,512]{3,2,1,0:T(8,128)(2,1)}, u32[]{:S(2)}, u32[]{:S(2)}) %collective-permute-start.8) | collective-permute-done | bytes 327712 | tf_op jit(solution)/shard_map/ppermute | solution.py:202
  71.6 1.4 %fusion.2 = bf16[2,2,80,512]{3,2,1,0:T(8,128)(2,1)S(1)} fusion(bf16[2,2,80,512]{3,2,1,0:T(8,128)(2,1)} %collective-permute-done.10, bf16[2,2,80,512]{3,2,1,0:T(8,128)(2,1)} %collective-permute-done.9, bf16[2,2,80,512]{3,2,1,0:T(8,128)(2,1)} %collective-permute-done.8, bf16[2,2,2,2,80,512]{5,4,3,2,1,0:T(8,128)(2,1)} %copy-done.10, s32[]{:T(128)S(6)} %select_n.416, ...), kind=kLoop, calls=%fused_computation.4 | loop fusion | flops 1310720 | bytes 1638408 | tf_op jit(solution)/shard_map/convert_element_type | solution.py:311
  73.0 1.5 %collective-permute-start.11 = (bf16[80,512]{1,0:T(8,128)(2,1)S(1)}, bf16[80,512]{1,0:T(8,128)(2,1)S(1)}, u32[]{:S(2)}, u32[]{:S(2)}) collective-permute-start(bf16[80,512]{1,0:T(8,128)(2,1)S(1)} %get-tuple-element.32), channel_id=1, source_target_pairs={{0,2},{1,3},{2,0},{3,1},{4,6},{5,7},{6,4},{7,5},{8,10},{9,11},{10,... | collective-permute-start | bytes 245768 | tf_op jit(solution)/shard_map/ppermute | solution.py:202
  74.6 2.3 %collective-permute-start.12 = (bf16[80,512]{1,0:T(8,128)(2,1)S(1)}, bf16[80,512]{1,0:T(8,128)(2,1)S(1)}, u32[]{:S(2)}, u32[]{:S(2)}) collective-permute-start(bf16[80,512]{1,0:T(8,128)(2,1)S(1)} %get-tuple-element.34), channel_id=1, source_target_pairs={{0,4},{1,5},{2,6},{3,7},{4,0},{5,1},{6,2},{7,3},{8,12},{9,13},{10,... | collective-permute-start | bytes 245768 | tf_op jit(solution)/shard_map/ppermute | solution.py:202
  76.9 1.2 %collective-permute-start.13 = (bf16[80,512]{1,0:T(8,128)(2,1)S(1)}, bf16[80,512]{1,0:T(8,128)(2,1)S(1)}, u32[]{:S(2)}, u32[]{:S(2)}) collective-permute-start(bf16[80,512]{1,0:T(8,128)(2,1)S(1)} %get-tuple-element.33), channel_id=1, source_target_pairs={{0,6},{1,7},{2,4},{3,5},{4,2},{5,3},{6,0},{7,1},{8,14},{9,15},{10,... | collective-permute-start | bytes 245768 | tf_op jit(solution)/shard_map/ppermute | solution.py:202
  78.1 2.3 %shard_map.115 = bf16[512,1024]{1,0:T(8,128)(2,1)} custom-call(s32[1]{0:T(128)} %bitcast.core_ref, bf16[512,512]{1,0:T(8,128)(2,1)S(1)} %copy-done.6, bf16[512,512]{1,0:T(8,128)(2,1)S(1)} %collective-permute-done.6.theirs_ref, bf16[1024,1024]{1,0:T(8,128)(2,1)S(1)} %copy-done), custom_call_target="tpu_custom_call" | custom-call | flops 1073741824 | bytes 1048576 | tf_op jit(solution)/shard_map/pallas_call | solution.py:211
  80.3 0.8 collective-permute-done.12
  81.1 2.7 %collective-permute-done.13 = bf16[80,512]{1,0:T(8,128)(2,1)S(1)} collective-permute-done((bf16[80,512]{1,0:T(8,128)(2,1)S(1)}, bf16[80,512]{1,0:T(8,128)(2,1)S(1)}, u32[]{:S(2)}, u32[]{:S(2)}) %collective-permute-start.13) | collective-permute-done | bytes 81952 | tf_op jit(solution)/shard_map/ppermute | solution.py:202
  (73 shorter events, 8.6 us)
Async XLA Ops:
  1.4 4.9 %collective-permute-start.2 = (bf16[1,16,1024]{2,1,0:T(8,128)(2,1)S(1)}, bf16[1,16,1024]{2,1,0:T(8,128)(2,1)S(1)}, u32[]{:S(2)}, u32[]{:S(2)}) collective-permute-start(bf16[1,16,1024]{2,1,0:T(8,128)(2,1)S(1)} %dynamic-slice_bitcast_fusion.14), channel_id=1, source_target_pairs={{0,1},{1,0},{2,3},{3,2},{4,5},{5,4},{6,7},{7,6},{8,9},{9,8},{10,11... | collective-permute-start | bytes 98312 | tf_op jit(solution)/shard_map/ppermute | solution.py:202
  4.4 17.9 %collective-permute-start = (bf16[512,1024]{1,0:T(8,128)(2,1)}, bf16[512,1024]{1,0:T(8,128)(2,1)}, u32[]{:S(2)}, u32[]{:S(2)}) collective-permute-start(bf16[512,1024]{1,0:T(8,128)(2,1)} %own_ref.7), channel_id=1, source_target_pairs={{0,8},{1,9},{2,10},{3,11},{4,12},{5,13},{6,14},{7,15},{8,0},{9,1},... | collective-permute-start | bytes 3145736 | tf_op jit(solution)/shard_map/ppermute | solution.py:202
  4.4 20.7 %collective-permute-start.1 = (bf16[512,1024]{1,0:T(8,128)(2,1)}, bf16[512,1024]{1,0:T(8,128)(2,1)}, u32[]{:S(2)}, u32[]{:S(2)}) collective-permute-start(bf16[512,1024]{1,0:T(8,128)(2,1)} %own_ref.6), channel_id=1, source_target_pairs={{0,8},{1,9},{2,10},{3,11},{4,12},{5,13},{6,14},{7,15},{8,0},{9,1},... | collective-permute-start | bytes 3145736 | tf_op jit(solution)/shard_map/ppermute | solution.py:202
  7.1 15.2 %copy-start = (bf16[1024,1024]{1,0:T(8,128)(2,1)S(1)}, bf16[1024,1024]{1,0:T(8,128)(2,1)}, u32[]{:S(2)}) copy-start(bf16[1024,1024]{1,0:T(8,128)(2,1)} %weight_ref.5) | copy-start | bytes 6291460
  7.1 15.2 %copy-start.1 = (bf16[512,1024]{1,0:T(8,128)(2,1)S(1)}, bf16[512,1024]{1,0:T(8,128)(2,1)}, u32[]{:S(2)}) copy-start(bf16[512,1024]{1,0:T(8,128)(2,1)} %own_ref.7) | copy-start | bytes 3145732
  7.1 4.4 %collective-permute-start.3 = (bf16[2,16,1024]{2,1,0:T(8,128)(2,1)S(1)}, bf16[2,16,1024]{2,1,0:T(8,128)(2,1)S(1)}, u32[]{:S(2)}, u32[]{:S(2)}) collective-permute-start(bf16[2,16,1024]{2,1,0:T(8,128)(2,1)S(1)} %pad_maximum_fusion.5), channel_id=1, source_target_pairs={{0,2},{1,3},{2,0},{3,1},{4,6},{5,7},{6,4},{7,5},{8,10},{9,11},{10,... | collective-permute-start | bytes 196616 | tf_op jit(solution)/shard_map/ppermute | solution.py:202
  11.6 6.2 %collective-permute-start.4 = (bf16[4,16,1024]{2,1,0:T(8,128)(2,1)S(1)}, bf16[4,16,1024]{2,1,0:T(8,128)(2,1)}, u32[]{:S(2)}, u32[]{:S(2)}) collective-permute-start(bf16[4,16,1024]{2,1,0:T(8,128)(2,1)S(1)} %pad_maximum_fusion.3), channel_id=1, source_target_pairs={{0,4},{1,5},{2,6},{3,7},{4,0},{5,1},{6,2},{7,3},{8,12},{9,13},{10,... | collective-permute-start | bytes 393224 | tf_op jit(solution)/shard_map/ppermute | solution.py:202
  19.4 1.9 %collective-permute-start.5 = (bf16[8,16,1024]{2,1,0:T(8,128)(2,1)}, bf16[8,16,1024]{2,1,0:T(8,128)(2,1)}, u32[]{:S(2)}, u32[]{:S(2)}) collective-permute-start(bf16[8,16,1024]{2,1,0:T(8,128)(2,1)} %pad_maximum_fusion.2), channel_id=1, source_target_pairs={{0,8},{1,9},{2,10},{3,11},{4,12},{5,13},{6,14},{7,15},{8,0},{9,1},... | collective-permute-start | bytes 786440 | tf_op jit(solution)/shard_map/ppermute | solution.py:202
  22.3 2.8 %copy-start.3 = (bf16[1024,1024]{1,0:T(8,128)(2,1)S(1)}, bf16[1024,1024]{1,0:T(8,128)(2,1)}, u32[]{:S(2)}) copy-start(bf16[1024,1024]{1,0:T(8,128)(2,1)} %wk_ref.3) | copy-start | bytes 6291460
  22.3 2.8 %copy-start.4 = (bf16[1024,1024]{1,0:T(8,128)(2,1)S(1)}, bf16[1024,1024]{1,0:T(8,128)(2,1)}, u32[]{:S(2)}) copy-start(bf16[1024,1024]{1,0:T(8,128)(2,1)} %wv_ref.3) | copy-start | bytes 6291460
  22.4 2.8 %copy-start.7 = (bf16[512,1024]{1,0:T(8,128)(2,1)S(1)}, bf16[512,1024]{1,0:T(8,128)(2,1)}, u32[]{:S(2)}) copy-start(bf16[512,1024]{1,0:T(8,128)(2,1)} %own_ref.6) | copy-start | bytes 3145732
  25.1 12.3 %copy-start.2 = (bf16[1024,1024]{1,0:T(8,128)(2,1)S(1)}, bf16[1024,1024]{1,0:T(8,128)(2,1)}, u32[]{:S(2)}) copy-start(bf16[1024,1024]{1,0:T(8,128)(2,1)} %weight_ref.4) | copy-start | bytes 6291460
  32.7 16.7 %collective-permute-start.15 = (bf16[2,2,32,1024]{3,2,1,0:T(8,128)(2,1)S(1)}, bf16[2,2,32,1024]{3,2,1,0:T(8,128)(2,1)S(1)}, u32[]{:S(2)}, u32[]{:S(2)}) collective-permute-start(bf16[2,2,32,1024]{3,2,1,0:T(8,128)(2,1)S(1)} %get-tuple-element.25), channel_id=1, source_target_pairs={{0,16},{1,17},{2,18},{3,19},{4,20},{5,21},{6,22},{7,23},{8,24},{9,... | collective-permute-start | bytes 786440 | tf_op jit(solution)/shard_map/ppermute | solution.py:202
  35.9 13.7 %collective-permute-start.16 = (bf16[2,2,32,1024]{3,2,1,0:T(8,128)(2,1)S(1)}, bf16[2,2,32,1024]{3,2,1,0:T(8,128)(2,1)S(1)}, u32[]{:S(2)}, u32[]{:S(2)}) collective-permute-start(bf16[2,2,32,1024]{3,2,1,0:T(8,128)(2,1)S(1)} %get-tuple-element.27), channel_id=1, source_target_pairs={{0,1},{1,0},{2,3},{3,2},{4,5},{5,4},{6,7},{7,6},{8,9},{9,8},{10,11... | collective-permute-start | bytes 786440 | tf_op jit(solution)/shard_map/ppermute | solution.py:202
  37.5 12.1 %collective-permute-start.17 = (bf16[2,2,32,1024]{3,2,1,0:T(8,128)(2,1)S(1)}, bf16[2,2,32,1024]{3,2,1,0:T(8,128)(2,1)S(1)}, u32[]{:S(2)}, u32[]{:S(2)}) collective-permute-start(bf16[2,2,32,1024]{3,2,1,0:T(8,128)(2,1)S(1)} %get-tuple-element.26), channel_id=1, source_target_pairs={{0,17},{1,16},{2,19},{3,18},{4,21},{5,20},{6,23},{7,22},{8,25},{9,... | collective-permute-start | bytes 786440 | tf_op jit(solution)/shard_map/ppermute | solution.py:202
  46.3 3.0 %copy-start.5 = (bf16[512,512]{1,0:T(8,128)(2,1)}, bf16[512,512]{1,0:T(8,128)(2,1)S(1)}, u32[]{:S(2)}) copy-start(bf16[512,512]{1,0:T(8,128)(2,1)S(1)} %get-tuple-element.15.mine_ref.qg_own_ref) | copy-start | bytes 1572868
  46.4 2.9 %copy-start.8 = (bf16[512,512]{1,0:T(8,128)(2,1)}, bf16[512,512]{1,0:T(8,128)(2,1)S(1)}, u32[]{:S(2)}) copy-start(bf16[512,512]{1,0:T(8,128)(2,1)S(1)} %get-tuple-element.16.qg_partner_ref) | copy-start | bytes 1572868
  46.4 5.0 %collective-permute-start.7 = (bf16[2,64,1024]{2,1,0:T(8,128)(2,1)S(1)}, bf16[2,64,1024]{2,1,0:T(8,128)(2,1)S(1)}, u32[]{:S(2)}, u32[]{:S(2)}) collective-permute-start(bf16[2,64,1024]{2,1,0:T(8,128)(2,1)S(1)} %get-tuple-element.18), channel_id=1, source_target_pairs={{0,8},{1,9},{2,10},{3,11},{4,12},{5,13},{6,14},{7,15},{8,0},{9,1},... | collective-permute-start | bytes 786440 | tf_op jit(solution)/shard_map/ppermute | solution.py:202
  50.5 10.2 %collective-permute-start.18 = (bf16[32,1024]{1,0:T(8,128)(2,1)S(1)}, bf16[32,1024]{1,0:T(8,128)(2,1)S(1)}, u32[]{:S(2)}, u32[]{:S(2)}) collective-permute-start(bf16[32,1024]{1,0:T(8,128)(2,1)S(1)} %get-tuple-element.35), channel_id=1, source_target_pairs={{0,2},{1,3},{2,0},{3,1},{4,6},{5,7},{6,4},{7,5},{8,10},{9,11},{10,... | collective-permute-start | bytes 196616 | tf_op jit(solution)/shard_map/ppermute | solution.py:202
  51.4 13.6 %copy-start.9 = (bf16[512,512]{1,0:T(8,128)(2,1)S(1)}, bf16[512,512]{1,0:T(8,128)(2,1)}, u32[]{:S(2)}) copy-start(bf16[512,512]{1,0:T(8,128)(2,1)} %copy-done.8) | copy-start | bytes 1572868
  51.5 1.1 %copy-start.10 = (bf16[2,2,2,2,80,512]{5,4,3,2,1,0:T(8,128)(2,1)}, bf16[2,2,2,2,80,512]{5,4,3,2,1,0:T(8,128)(2,1)S(1)}, u32[]{:S(2)}) copy-start(bf16[2,2,2,2,80,512]{5,4,3,2,1,0:T(8,128)(2,1)S(1)} %pad_maximum_fusion) | copy-start | bytes 3932164
  52.7 25.4 %copy-start.6 = (bf16[512,512]{1,0:T(8,128)(2,1)S(1)}, bf16[512,512]{1,0:T(8,128)(2,1)}, u32[]{:S(2)}) copy-start(bf16[512,512]{1,0:T(8,128)(2,1)} %copy-done.5) | copy-start | bytes 1572868
  53.7 14.7 %collective-permute-start.10 = (bf16[2,2,80,512]{3,2,1,0:T(8,128)(2,1)}, bf16[2,2,80,512]{3,2,1,0:T(8,128)(2,1)}, u32[]{:S(2)}, u32[]{:S(2)}) collective-permute-start(bf16[2,2,80,512]{3,2,1,0:T(8,128)(2,1)} %get-tuple-element.23), channel_id=1, source_target_pairs={{0,17},{1,16},{2,19},{3,18},{4,21},{5,20},{6,23},{7,22},{8,25},{9,... | collective-permute-start | bytes 983048 | tf_op jit(solution)/shard_map/ppermute | solution.py:202
  56.1 15.4 %collective-permute-start.8 = (bf16[2,2,80,512]{3,2,1,0:T(8,128)(2,1)}, bf16[2,2,80,512]{3,2,1,0:T(8,128)(2,1)}, u32[]{:S(2)}, u32[]{:S(2)}) collective-permute-start(bf16[2,2,80,512]{3,2,1,0:T(8,128)(2,1)} %get-tuple-element.22), channel_id=1, source_target_pairs={{0,16},{1,17},{2,18},{3,19},{4,20},{5,21},{6,22},{7,23},{8,24},{9,... | collective-permute-start | bytes 983048 | tf_op jit(solution)/shard_map/ppermute | solution.py:202
  56.7 14.9 %collective-permute-start.9 = (bf16[2,2,80,512]{3,2,1,0:T(8,128)(2,1)}, bf16[2,2,80,512]{3,2,1,0:T(8,128)(2,1)}, u32[]{:S(2)}, u32[]{:S(2)}) collective-permute-start(bf16[2,2,80,512]{3,2,1,0:T(8,128)(2,1)} %get-tuple-element.24), channel_id=1, source_target_pairs={{0,1},{1,0},{2,3},{3,2},{4,5},{5,4},{6,7},{7,6},{8,9},{9,8},{10,11... | collective-permute-start | bytes 983048 | tf_op jit(solution)/shard_map/ppermute | solution.py:202
  57.2 7.8 %collective-permute-start.19 = (bf16[32,1024]{1,0:T(8,128)(2,1)}, bf16[32,1024]{1,0:T(8,128)(2,1)}, u32[]{:S(2)}, u32[]{:S(2)}) collective-permute-start(bf16[32,1024]{1,0:T(8,128)(2,1)} %get-tuple-element.37), channel_id=1, source_target_pairs={{0,4},{1,5},{2,6},{3,7},{4,0},{5,1},{6,2},{7,3},{8,12},{9,13},{10,... | collective-permute-start | bytes 196616 | tf_op jit(solution)/shard_map/ppermute | solution.py:202
  60.7 6.2 %collective-permute-start.20 = (bf16[32,1024]{1,0:T(8,128)(2,1)S(1)}, bf16[32,1024]{1,0:T(8,128)(2,1)}, u32[]{:S(2)}, u32[]{:S(2)}) collective-permute-start(bf16[32,1024]{1,0:T(8,128)(2,1)S(1)} %get-tuple-element.36), channel_id=1, source_target_pairs={{0,6},{1,7},{2,4},{3,5},{4,2},{5,3},{6,0},{7,1},{8,14},{9,15},{10,... | collective-permute-start | bytes 196616 | tf_op jit(solution)/shard_map/ppermute | solution.py:202
  65.0 13.1 %collective-permute-start.6 = (bf16[512,512]{1,0:T(8,128)(2,1)S(1)}, bf16[512,512]{1,0:T(8,128)(2,1)S(1)}, u32[]{:S(2)}, u32[]{:S(2)}) collective-permute-start(bf16[512,512]{1,0:T(8,128)(2,1)S(1)} %copy-done.9), channel_id=1, source_target_pairs={{0,8},{1,9},{2,10},{3,11},{4,12},{5,13},{6,14},{7,15},{8,0},{9,1},... | collective-permute-start | bytes 1572872 | tf_op jit(solution)/shard_map/ppermute | solution.py:202
  73.0 7.3 %collective-permute-start.11 = (bf16[80,512]{1,0:T(8,128)(2,1)S(1)}, bf16[80,512]{1,0:T(8,128)(2,1)S(1)}, u32[]{:S(2)}, u32[]{:S(2)}) collective-permute-start(bf16[80,512]{1,0:T(8,128)(2,1)S(1)} %get-tuple-element.32), channel_id=1, source_target_pairs={{0,2},{1,3},{2,0},{3,1},{4,6},{5,7},{6,4},{7,5},{8,10},{9,11},{10,... | collective-permute-start | bytes 245768 | tf_op jit(solution)/shard_map/ppermute | solution.py:202
  74.6 6.6 %collective-permute-start.12 = (bf16[80,512]{1,0:T(8,128)(2,1)S(1)}, bf16[80,512]{1,0:T(8,128)(2,1)S(1)}, u32[]{:S(2)}, u32[]{:S(2)}) collective-permute-start(bf16[80,512]{1,0:T(8,128)(2,1)S(1)} %get-tuple-element.34), channel_id=1, source_target_pairs={{0,4},{1,5},{2,6},{3,7},{4,0},{5,1},{6,2},{7,3},{8,12},{9,13},{10,... | collective-permute-start | bytes 245768 | tf_op jit(solution)/shard_map/ppermute | solution.py:202
  76.9 6.9 %collective-permute-start.13 = (bf16[80,512]{1,0:T(8,128)(2,1)S(1)}, bf16[80,512]{1,0:T(8,128)(2,1)S(1)}, u32[]{:S(2)}, u32[]{:S(2)}) collective-permute-start(bf16[80,512]{1,0:T(8,128)(2,1)S(1)} %get-tuple-element.33), channel_id=1, source_target_pairs={{0,6},{1,7},{2,4},{3,5},{4,2},{5,3},{6,0},{7,1},{8,14},{9,15},{10,... | collective-permute-start | bytes 245768 | tf_op jit(solution)/shard_map/ppermute | solution.py:202
  83.9 1.3 %collective-permute-start.14 = (f32[32,512]{1,0:T(8,128)S(1)}, f32[32,512]{1,0:T(8,128)S(1)}, u32[]{:S(2)}, u32[]{:S(2)}) collective-permute-start(f32[32,512]{1,0:T(8,128)S(1)} %get-tuple-element.47), channel_id=1, source_target_pairs={{0,8},{1,9},{2,10},{3,11},{4,12},{5,13},{6,14},{7,15},{8,0},{9,1},... | collective-permute-start | bytes 196616 | tf_op jit(solution)/shard_map/ppermute | solution.py:202

commit v5 on v4

--- a/solution.py
+++ b/solution.py
@@ -22,48 +22,99 @@
     return lax.dot_general(left, right, (dims, ((), ())), preferred_element_type=F32)
 
 
-def owned(core_ref, at, size, block):
-    return pl.ds(pl.multiple_of((2 * (at // block) + core_ref[0]) * block + at % block, size), size)
-
-
-def query_kernel(block, core_ref, weight_ref, own_ref, partner_ref, out_ref):
-    rows = own_ref.shape[0]
-    for at in range(0, out_ref.shape[0], block):
-        weight = weight_ref[:, owned(core_ref, at, block, block)]
-        part = pl.ds(at, block)
-        out_ref[part, :rows] = dot(own_ref[...], weight, ((1,), (0,))).astype(BF16).T
-        out_ref[part, rows:] = dot(partner_ref[...], weight, ((1,), (0,))).astype(BF16).T
-
-
-def grad_kernel(block, core_ref, weight_ref, own_ref, partner_ref, out_ref):
-    rows = own_ref.shape[0]
-    for at in range(0, out_ref.shape[0], block):
-        weight = weight_ref[owned(core_ref, at, block, block), :]
-        part = pl.ds(at, block)
-        out_ref[part, :rows] = dot(weight, own_ref[...], ((1,), (1,))).astype(BF16)
-        out_ref[part, rows:] = dot(weight, partner_ref[...], ((1,), (1,))).astype(BF16)
+def owned(place_ref, at, size, block):
+    return pl.ds(pl.multiple_of((2 * (at // block) + place_ref[0]) * block + at % block, size), size)
+
+
+def query_kernel(block, place_ref, weight_ref, own_ref, partner_ref, out_ref, tokens, weights, sems):
+    rows = partner_ref.shape[0]
+    count = weights.shape[0]
+    copies = []
+    for at in range(count):
+        part = owned(place_ref, at * block, block, block)
+        copies.append(pltpu.make_async_copy(weight_ref.at[:, part], weights.at[at], sems.at[at]))
+    copies.append(pltpu.make_async_copy(own_ref, tokens, sems.at[count]))
+    for one in copies:
+        one.start()
+    for side, source in enumerate((partner_ref, tokens)):
+        if side == 1:
+            copies[count].wait()
+        for at in range(count):
+            if side == 0:
+                copies[at].wait()
+            term = dot(source[...], weights[at], ((1,), (0,))).astype(BF16).T
+            out_ref[pl.ds(at * block, block), pl.ds((1 - side) * rows, rows)] = term
+
+
+def grad_kernel(block, place_ref, weight_ref, own_ref, partner_ref, out_ref, tokens, weights, sems):
+    rows = partner_ref.shape[0]
+    count = weights.shape[0]
+    copies = []
+    for at in range(count):
+        part = owned(place_ref, at * block, block, block)
+        copies.append(pltpu.make_async_copy(weight_ref.at[part, :], weights.at[at], sems.at[at]))
+    copies.append(pltpu.make_async_copy(own_ref, tokens, sems.at[count]))
+    for one in copies:
+        one.start()
+    for side, source in enumerate((partner_ref, tokens)):
+        if side == 1:
+            copies[count].wait()
+        for at in range(count):
+            if side == 0:
+                copies[at].wait()
+            term = dot(weights[at], source[...], ((1,), (1,))).astype(BF16)
+            out_ref[pl.ds(at * block, block), pl.ds((1 - side) * rows, rows)] = term
+
+
+def fetch_kernel(block, group, place_ref, wk_ref, wv_ref, wkv_ref, sems):
+    copies = []
+    for at in range(wkv_ref.shape[0]):
+        part = owned(place_ref, at * group, group, block)
+        for which, source in enumerate((wk_ref, wv_ref)):
+            target = wkv_ref.at[at, :, pl.ds(which * group, group)]
+            copies.append(
+                pltpu.make_async_copy(source.at[:, part], target, sems.at[2 * at + which])
+            )
+            copies[-1].start()
+    for one in copies:
+        one.wait()
 
 
 def attend_kernel(
-    block,
     size,
     scale,
-    core_ref,
-    context_ref,
-    wk_ref,
-    wv_ref,
+    place_ref,
+    mine_ref,
+    other_ref,
+    wkv_ref,
     q_ref,
+    g_ref,
+    bias_ref,
     own_ref,
     partner_ref,
-    bias_ref,
     kv_ref,
     probs_ref,
+    row_dot_ref,
+    wo_ref,
+    context_ref,
     att_ref,
-    wo_ref,
+    tokens,
+    sems,
 ):
-    block_rows = own_ref.shape[0]
-    rows = 2 * block_rows
+    half_width, rows = q_ref.shape
+    block_rows = rows // 2
     width = GROUP * size
+    moves = []
+    for side, source in enumerate((own_ref, partner_ref)):
+        moves.append(pltpu.make_async_copy(source, tokens.at[side], sems.at[side]))
+        moves[-1].start()
+    shards, half_rows = mine_ref.shape[:2]
+    for at in range(shards):
+        first = lax.bitwise_xor(place_ref[1], at) * 2 * half_rows
+        mine = pl.multiple_of(first + place_ref[0] * half_rows, half_rows)
+        other = pl.multiple_of(first + (1 - place_ref[0]) * half_rows, half_rows)
+        context_ref[pl.ds(mine, half_rows), :] = mine_ref[at]
+        context_ref[pl.ds(other, half_rows), :] = other_ref[at]
     context = context_ref[...]
     bias = bias_ref[...]
     lane = lax.broadcasted_iota(jnp.int32, (16, rows), 1)
@@ -71,20 +122,12 @@
     marks = jnp.where(lane // block_rows == line, 1.0, 0.0).astype(BF16)
 
     def keys_values(at):
-        cols = owned(core_ref, at, width, block)
-        weight = jnp.concatenate([wk_ref[:, cols], wv_ref[:, cols]], axis=1)
-        both = dot(context, weight, ((1,), (0,))).astype(BF16)
+        step = at // width
+        both = dot(context, wkv_ref[step], ((1,), (0,))).astype(BF16)
         key_part = (both[:, :width].astype(F32) * scale).astype(BF16)
         kv_ref[0, pl.ds(at, width), :] = key_part.T
         kv_ref[1, pl.ds(at, width), :] = both[:, width:].T
 
-    def out_product(at, depth):
-        part = pl.ds(at, depth)
-        total = dot(att_ref[part, :block_rows], own_ref[...], ((1,), (0,)))
-        total += dot(att_ref[part, block_rows:], partner_ref[...], ((1,), (0,)))
-        wo_ref[part, :] = total.astype(BF16)
-
-    half_width = q_ref.shape[0]
     keys_values(0)
     for at in range(0, half_width, width):
         if at + width < half_width:
@@ -99,23 +142,30 @@
             row_sum = jnp.sum(unnormed, axis=0, keepdims=True)
             probs = (unnormed * (1.0 / row_sum)).astype(BF16)
             probs_ref[first // size] = probs
-            att_ref[part, :] = dot(kv_ref[1, part, :], probs, ((1,), (0,))).astype(BF16)
+            attended = dot(kv_ref[1, part, :], probs, ((1,), (0,))).astype(BF16)
+            att_ref[part, :] = attended
+            row_dot = attended.astype(F32) * g_ref[part, :].astype(F32)
+            row_dot_ref[pl.ds(first // size, 1), :] = jnp.sum(row_dot, axis=0, keepdims=True)
         if (at // width) % 2 == 1:
-            out_product(at - width, 2 * width)
+            if at == width:
+                for move in moves:
+                    move.wait()
+            part = pl.ds(at - width, 2 * width)
+            total = dot(att_ref[part, :block_rows], tokens[0], ((1,), (0,)))
+            total += dot(att_ref[part, block_rows:], tokens[1], ((1,), (0,)))
+            wo_ref[part, :] = total.astype(BF16)
 
 
 def back_kernel(
-    block,
     size,
     scale,
-    core_ref,
-    wk_ref,
-    wv_ref,
+    place_ref,
+    wkv_ref,
     q_ref,
     g_ref,
     kv_ref,
     probs_ref,
-    att_ref,
+    row_dot_ref,
     qg_own_ref,
     qg_partner_ref,
     kept_ref,
@@ -131,8 +181,7 @@
             part = pl.ds(first, size)
             grad = g_ref[part, :]
             probs = probs_ref[first // size]
-            attended = att_ref[part, :].astype(F32)
-            row_dot = jnp.sum(attended * grad.astype(F32), axis=0, keepdims=True)
+            row_dot = row_dot_ref[pl.ds(first // size, 1), :]
             grad_scores = dot(kv_ref[1, part, :].T, grad, ((1,), (0,)))
             value_parts.append(dot(grad, probs, ((1,), (1,))))
             logits = (probs.astype(F32) * (grad_scores - row_dot)).astype(BF16)
@@ -140,18 +189,16 @@
             qg_own_ref[part, :] = query_grad[:, :block_rows]
             qg_partner_ref[part, :] = query_grad[:, block_rows:]
             key_parts.append(dot(q_ref[part, :], logits, ((1,), (1,))) * scale)
-        cols = owned(core_ref, at, width, block)
         grads = jnp.concatenate(key_parts + value_parts, axis=0).astype(BF16).T
-        weight = jnp.concatenate([wk_ref[:, cols], wv_ref[:, cols]], axis=1)
-        term = dot(grads, weight, ((1,), (1,)))
+        term = dot(grads, wkv_ref[at // width], ((1,), (1,)))
         if at == 0:
             sum_ref[...] = term
         else:
             sum_ref[...] += term
     out_block = kept_ref.shape[1]
     for high in range(kept_ref.shape[0]):
-        kept = pl.multiple_of((2 * high + core_ref[0]) * out_block, out_block)
-        sent = pl.multiple_of((2 * high + 1 - core_ref[0]) * out_block, out_block)
+        kept = pl.multiple_of((2 * high + place_ref[0]) * out_block, out_block)
+        sent = pl.multiple_of((2 * high + 1 - place_ref[0]) * out_block, out_block)
         kept_ref[high] = sum_ref[pl.ds(kept, out_block), :]
         sent_ref[high] = sum_ref[pl.ds(sent, out_block), :].astype(BF16)
 
@@ -165,12 +212,12 @@
         out_ref[:, part] = total.astype(BF16).T
 
 
-def targets_kernel(block, core_ref, mine_ref, theirs_ref, weight_ref, out_ref):
-    other_ref = [1 - core_ref[0]]
+def targets_kernel(block, place_ref, mine_ref, theirs_ref, weight_ref, out_ref):
+    other_ref = [1 - place_ref[0]]
     total = None
     for at in range(0, mine_ref.shape[0], block):
         part = pl.ds(at, block)
-        for source, core in ((mine_ref, core_ref), (theirs_ref, other_ref)):
+        for source, core in ((mine_ref, place_ref), (theirs_ref, other_ref)):
             weight = weight_ref[:, owned(core, at, block, block)]
             term = dot(source[part, :].T, weight, ((1,), (1,)))
             total = term if total is None else total + term
@@ -195,8 +242,8 @@
     block = width // grp_count
     context_rows = context.shape[0] * seq_count
     rows = 2 * query_rows
-    core_index = core.reshape(1).astype(jnp.int32)
-    limit = (10 << 20) + 6 * 4 * context_rows * rows
+    place = jnp.stack([core, seq]).astype(jnp.int32)
+    limit = (14 << 20) + 6 * 4 * context_rows * rows
 
     def swap(array, mask):
         return lax.ppermute(array, AXES, [(i, i ^ mask) for i in range(device_count)])
@@ -204,10 +251,15 @@
     def bit_of(mask):
         return (me // mask) % 2
 
-    def call(kernel, operands, outs, flops, scratch=()):
+    def call(kernel, operands, outs, flops, scratch=(), fetched=()):
         in_vmem = pl.BlockSpec(memory_space=pltpu.VMEM)
         scalar = pl.BlockSpec(memory_space=pltpu.SMEM)
-        specs = [scalar if one is core_index else in_vmem for one in operands]
+        anywhere = pl.BlockSpec(memory_space=pltpu.HBM)
+        specs = [scalar if one is place else in_vmem for one in operands]
+        operands = list(operands)
+        for at in fetched:
+            specs[at] = anywhere
+            operands[at] = pltpu.with_memory_space_constraint(operands[at], pltpu.HBM)
         return pl.pallas_call(
             kernel,
             in_specs=specs,
@@ -227,30 +279,45 @@
         if targets_swapped is None:
             targets_swapped = swap(targets, core_mask)
             grad_swapped = swap(grad_out, core_mask)
-        upper = bit_of(mask) == 1
-        held = jnp.concatenate(
-            [jnp.where(upper, other, held), jnp.where(upper, held, other)], axis=0
-        )
+        held = jnp.concatenate([held, other], axis=0)
         mask *= 2
     other = swap(held, core_mask)
-    held = jnp.stack(
-        [jnp.where(core == 1, other, held), jnp.where(core == 1, held, other)], axis=1
-    )
-    context_all = held.reshape(context_rows, width)
 
     product = 2 * half_width * rows * width
     attention = 8 * half_width * rows * context_rows
+    group_width = GROUP * head_size
+    groups = half_width // group_width
     (queries,) = call(
         partial(query_kernel, block),
-        [core_index, w_query, targets, targets_swapped],
+        [place, w_query, targets, targets_swapped],
         [((half_width, rows), BF16)],
         product,
+        [
+            pltpu.VMEM((query_rows, width), BF16),
+            pltpu.VMEM((high_count, width, block), BF16),
+            pltpu.SemaphoreType.DMA((high_count + 1,)),
+        ],
+        (1, 2),
     )
     (grads,) = call(
         partial(grad_kernel, block),
-        [core_index, w_out, grad_out, grad_swapped],
+        [place, w_out, grad_out, grad_swapped],
         [((half_width, rows), BF16)],
         product,
+        [
+            pltpu.VMEM((query_rows, width), BF16),
+            pltpu.VMEM((high_count, block, width), BF16),
+            pltpu.SemaphoreType.DMA((high_count + 1,)),
+        ],
+        (1, 2),
+    )
+    (wkv,) = call(
+        partial(fetch_kernel, block, group_width),
+        [place, w_key, w_value],
+        [((groups, width, 2 * group_width), BF16)],
+        product,
+        [pltpu.SemaphoreType.DMA((2 * groups,))],
+        (1, 2),
     )
 
     view_rows = query_rows * device_count // TVIEWS
@@ -263,16 +330,23 @@
     bias = jnp.where(seen == 1, 0.0, -1e30).astype(BF16)
     bias = jnp.concatenate([bias, jnp.zeros((14, context_rows), BF16)], axis=0)
 
-    key_values, probs, attended, wo_term = call(
-        partial(attend_kernel, block, head_size, score_scale),
-        [core_index, context_all, w_key, w_value, queries, grad_out, grad_swapped, bias],
+    key_values, probs, row_dots, wo_term = call(
+        partial(attend_kernel, head_size, score_scale),
+        [place, held, other, wkv, queries, grads, bias, grad_out, grad_swapped],
         [
             ((2, half_width, context_rows), BF16),
             ((half_heads, context_rows, rows), BF16),
-            ((half_width, rows), BF16),
+            ((half_heads, rows), F32),
             ((half_width, width), BF16),
         ],
         product + attention,
+        [
+            pltpu.VMEM((context_rows, width), BF16),
+            pltpu.VMEM((half_width, rows), BF16),
+            pltpu.VMEM((2, query_rows, width), BF16),
+            pltpu.SemaphoreType.DMA((2,)),
+        ],
+        (7, 8),
     )
 
     high_masks = []
@@ -323,8 +397,8 @@
     grad_wo = exchange_rest(wo_part, left_masks)
 
     query_own, query_partner, ctx_kept, ctx_sent = call(
-        partial(back_kernel, block, head_size, score_scale),
-        [core_index, w_key, w_value, queries, grads, key_values, probs, attended],
+        partial(back_kernel, head_size, score_scale),
+        [place, wkv, queries, grads, key_values, probs, row_dots],
         [
             ((half_width, query_rows), BF16),
             ((half_width, query_rows), BF16),
@@ -364,7 +438,7 @@
     returned = swap(query_partner, core_mask)
     (d_targets,) = call(
         partial(targets_kernel, block),
-        [core_index, query_own, returned, w_query],
+        [place, query_own, returned, w_query],
         [((query_rows, width), BF16)],
         product,
     )

time: 86.4 us -> 87.7 us (1.015)
  Pallas kernels: 24.1 us -> 27.4 us
  other arithmetic: 9.23 us -> 6.94 us
  waiting for transfers between devices: 20.9 us -> 22.7 us
  starting transfers between devices: 26.6 us -> 25.3 us
    pallas_call x6 -> x7, Pallas kernels: 24.1 us -> 27.4 us  [call(): pl.pallas_call(kernel, in_specs=specs, out_specs=[in_vmem] * len(outs), o...]
    ppermute x21, waiting for transfers between devices: 20.9 us -> 22.7 us  [swap(): lax.ppermute(array, AXES, [(i, i ^ mask) for i in range(device_count)])]
    select_n x3 -> x0, other arithmetic: 1.71 us -> none  [on_device(): jnp.where(upper, other, held)]
    ppermute x21, starting transfers between devices: 26.6 us -> 25.3 us  [swap(): lax.ppermute(array, AXES, [(i, i ^ mask) for i in range(device_count)])]
    squeeze x4, local copies, waits for them, and re-layouts: 1.78 us -> 3.06 us  [piece(): part = lax.dynamic_index_in_dim(part, at, masks.index(mask), keepdims=False)]
    concatenate x1, other arithmetic: 0.12 us -> 1.19 us  [on_device(): tail, _ = exchange(jnp.concatenate(tail, axis=-2), all_masks, stages[0])]
    another operation x3 -> x2, other arithmetic: 1.09 us -> 0.12 us  [the longest x1 0.08 us: on_device(): place = jnp.stack([core, seq]).astype(jnp.int32)]
  transfers between devices with their start and end apart: 21 -> 21, of which waited for: 11 -> 9; matrix products, arithmetic and copies ran while one was open for 12% -> 11% of each run, Pallas kernels for 19% -> 23%
where the time goes in v5:
time: 87.7 us; the launch traced here: 87.3 us
  Pallas kernels  27.4 us (31%)
  starting transfers between devices  25.3 us (29%)
  waiting for transfers between devices  22.7 us (26%)
  other arithmetic  6.94 us (8%)
  local copies, waits for them, and re-layouts  4.02 us (5%)
  between operations  0.9 us (1%)
    pallas_call x7, Pallas kernels, call(): pl.pallas_call(kernel, in_specs=specs, out_specs=[in_vmem] * len(outs), o...  27.4 us
    ppermute x21, starting transfers between devices, swap(): lax.ppermute(array, AXES, [(i, i ^ mask) for i in range(device_count)])  25.3 us
    ppermute x21, waiting for transfers between devices, swap(): lax.ppermute(array, AXES, [(i, i ^ mask) for i in range(device_count)])  22.7 us
    squeeze x4, local copies, waits for them, and re-layouts, piece(): part = lax.dynamic_index_in_dim(part, at, masks.index(mask), keepdims=False)  3.06 us
  transfers between devices with their start and end apart: 21, of which 9 were waited for; matrix products, arithmetic and copies ran while one was open for 11% of the time, Pallas kernels for 23%

profile of v5, /device:TPU:0, one launch (start us, length us, event | category | flops | bytes accessed | tf_op | source)
XLA Modules:
  0.0 87.3 jit_solution(17310498359119059641)
XLA Ops:
  0.7 0.8 copy-done
  1.5 3.0 %collective-permute-start.2 = (bf16[1,16,1024]{2,1,0:T(8,128)(2,1)S(1)}, bf16[1,16,1024]{2,1,0:T(8,128)(2,1)S(1)}, u32[]{:S(2)}, u32[]{:S(2)}) collective-permute-start(bf16[1,16,1024]{2,1,0:T(8,128)(2,1)S(1)} %dynamic-slice_bitcast_fusion.14), channel_id=1, source_target_pairs={{0,1},{1,0},{2,3},{3,2},{4,5},{5,4},{6,7},{7,6},{8,9},{9,8},{10,11... | collective-permute-start | bytes 98312 | tf_op jit(solution)/shard_map/ppermute | solution.py:249
  5.2 0.8 select_reduce_fusion.1
  6.4 2.1 %collective-permute-start.3 = (bf16[2,16,1024]{2,1,0:T(8,128)(2,1)S(1)}, bf16[2,16,1024]{2,1,0:T(8,128)(2,1)S(1)}, u32[]{:S(2)}, u32[]{:S(2)}) collective-permute-start(bf16[2,16,1024]{2,1,0:T(8,128)(2,1)S(1)} %pad_maximum_fusion.4), channel_id=1, source_target_pairs={{0,2},{1,3},{2,0},{3,1},{4,6},{5,7},{6,4},{7,5},{8,10},{9,11},{10,... | collective-permute-start | bytes 196616 | tf_op jit(solution)/shard_map/ppermute | solution.py:249
  8.6 2.2 %collective-permute-done.3 = bf16[2,16,1024]{2,1,0:T(8,128)(2,1)S(1)} collective-permute-done((bf16[2,16,1024]{2,1,0:T(8,128)(2,1)S(1)}, bf16[2,16,1024]{2,1,0:T(8,128)(2,1)S(1)}, u32[]{:S(2)}, u32[]{:S(2)}) %collective-permute-start.3) | collective-permute-done | bytes 65568 | tf_op jit(solution)/shard_map/ppermute | solution.py:249
  10.8 3.1 %collective-permute-start.4 = (bf16[4,16,1024]{2,1,0:T(8,128)(2,1)S(1)}, bf16[4,16,1024]{2,1,0:T(8,128)(2,1)S(1)}, u32[]{:S(2)}, u32[]{:S(2)}) collective-permute-start(bf16[4,16,1024]{2,1,0:T(8,128)(2,1)S(1)} %pad_maximum_fusion.2), channel_id=1, source_target_pairs={{0,4},{1,5},{2,6},{3,7},{4,0},{5,1},{6,2},{7,3},{8,12},{9,13},{10,... | collective-permute-start | bytes 393224 | tf_op jit(solution)/shard_map/ppermute | solution.py:249
  14.0 4.4 %collective-permute-done.4 = bf16[4,16,1024]{2,1,0:T(8,128)(2,1)S(1)} collective-permute-done((bf16[4,16,1024]{2,1,0:T(8,128)(2,1)S(1)}, bf16[4,16,1024]{2,1,0:T(8,128)(2,1)S(1)}, u32[]{:S(2)}, u32[]{:S(2)}) %collective-permute-start.4) | collective-permute-done | bytes 131104 | tf_op jit(solution)/shard_map/ppermute | solution.py:249
  18.4 2.2 %shard_map.111.wkv_ref = bf16[4,1024,256]{2,1,0:T(8,128)(2,1)S(1)} custom-call(s32[2]{0:T(128)S(1)} %pad_add_fusion.place_ref, bf16[1024,1024]{1,0:T(8,128)(2,1)} %wk_ref.1, bf16[1024,1024]{1,0:T(8,128)(2,1)} %wv_ref.1), custom_call_target="tpu_custom_call" | custom-call | flops 1073741824 | bytes 1048576 | tf_op jit(solution)/shard_map/pallas_call | solution.py:263
  20.6 3.9 %shard_map.112.q_ref = bf16[512,1024]{1,0:T(8,128)(2,1)S(1)} custom-call(s32[2]{0:T(128)S(1)} %pad_add_fusion.place_ref, bf16[1024,1024]{1,0:T(8,128)(2,1)} %weight_ref.5, bf16[512,1024]{1,0:T(8,128)(2,1)} %own_ref.7, bf16[512,1024]{1,0:T(8,128)(2,1)S(1)} %collective-permute-done.partner_ref), custom_call_target="tpu_custom_call" | custom-call | flops 1073741824 | bytes 1048576 | tf_op jit(solution)/shard_map/pallas_call | solution.py:263
  24.6 3.3 %shard_map.113.g_ref = bf16[512,1024]{1,0:T(8,128)(2,1)S(1)} custom-call(s32[2]{0:T(128)S(1)} %pad_add_fusion.place_ref, bf16[1024,1024]{1,0:T(8,128)(2,1)} %weight_ref.4, bf16[512,1024]{1,0:T(8,128)(2,1)} %own_ref.6, bf16[512,1024]{1,0:T(8,128)(2,1)S(1)} %collective-permute-done.1.partner_ref), custom_call_target="tpu_custom_call" | custom-call | flops 1073741824 | bytes 1048576 | tf_op jit(solution)/shard_map/pallas_call | solution.py:263
  27.9 7.0 %shard_map.114 = (bf16[2,512,256]{2,1,0:T(8,128)(2,1)S(1)}, bf16[8,256,1024]{2,1,0:T(8,128)(2,1)S(1)}, f32[8,1024]{1,0:T(8,128)S(1)}, bf16[512,1024]{1,0:T(8,128)(2,1)S(1)}) custom-call(s32[2]{0:T(128)S(1)} %pad_add_fusion.place_ref, bf16[8,16,1024]{2,1,0:T(8,128)(2,1)S(1)} %pad_maximum_fusion.1.mine_ref, ...), custom_call_target="tpu_custom_call" | custom-call | flops 2147483648 | bytes 1048576 | tf_op jit(solution)/shard_map/pallas_call | solution.py:263
  35.0 1.8 %collective-permute-start.15 = (bf16[2,2,32,1024]{3,2,1,0:T(8,128)(2,1)S(1)}, bf16[2,2,32,1024]{3,2,1,0:T(8,128)(2,1)S(1)}, u32[]{:S(2)}, u32[]{:S(2)}) collective-permute-start(bf16[2,2,32,1024]{3,2,1,0:T(8,128)(2,1)S(1)} %get-tuple-element.25), channel_id=1, source_target_pairs={{0,16},{1,17},{2,18},{3,19},{4,20},{5,21},{6,22},{7,23},{8,24},{9,... | collective-permute-start | bytes 786440 | tf_op jit(solution)/shard_map/ppermute | solution.py:249
  36.8 1.5 %collective-permute-start.16 = (bf16[2,2,32,1024]{3,2,1,0:T(8,128)(2,1)S(1)}, bf16[2,2,32,1024]{3,2,1,0:T(8,128)(2,1)S(1)}, u32[]{:S(2)}, u32[]{:S(2)}) collective-permute-start(bf16[2,2,32,1024]{3,2,1,0:T(8,128)(2,1)S(1)} %get-tuple-element.27), channel_id=1, source_target_pairs={{0,1},{1,0},{2,3},{3,2},{4,5},{5,4},{6,7},{7,6},{8,9},{9,8},{10,11... | collective-permute-start | bytes 786440 | tf_op jit(solution)/shard_map/ppermute | solution.py:249
  38.5 6.9 %shard_map.115 = (bf16[512,512]{1,0:T(8,128)(2,1)S(1)}, bf16[512,512]{1,0:T(8,128)(2,1)S(1)}, f32[2,64,1024]{2,1,0:T(8,128)S(1)}, bf16[2,64,1024]{2,1,0:T(8,128)(2,1)S(1)}) custom-call(s32[2]{0:T(128)S(1)} %pad_add_fusion.place_ref, bf16[4,1024,256]{2,1,0:T(8,128)(2,1)S(1)} %shard_map.111.wkv_ref, bf16[512,1024]{1,0:T(8,128)(2,1)S(1)} %shard_map.112.q_ref, ...), custom_call_target="tpu_custom_call" | custom-call | flops 1610612736 | bytes 1048576 | tf_op jit(solution)/shard_map/pallas_call | solution.py:263
  45.5 1.4 %shard_map.117 = bf16[1024,512]{1,0:T(8,128)(2,1)S(1)} custom-call(bf16[512,512]{1,0:T(8,128)(2,1)S(1)} %get-tuple-element.15.mine_ref.qg_own_ref, bf16[512,512]{1,0:T(8,128)(2,1)S(1)} %get-tuple-element.16.qg_partner_ref, bf16[512,1024]{1,0:T(8,128)(2,1)S(1)} %copy-done.2, bf16[512,1024]{1,0:T(8,128)(2,1)S(1)} %collective-permute-done.partner_ref), custom_call_target="tpu_custom_call" | custom-call | flops 1073741824 | bytes 1048576 | tf_op jit(solution)/shard_map/pallas_call | solution.py:263
  46.9 3.9 %collective-permute-done.16 = bf16[2,2,32,1024]{3,2,1,0:T(8,128)(2,1)S(1)} collective-permute-done((bf16[2,2,32,1024]{3,2,1,0:T(8,128)(2,1)S(1)}, bf16[2,2,32,1024]{3,2,1,0:T(8,128)(2,1)S(1)}, u32[]{:S(2)}, u32[]{:S(2)}) %collective-permute-start.16) | collective-permute-done | bytes 262176 | tf_op jit(solution)/shard_map/ppermute | solution.py:249
  51.0 0.7 dynamic-slice_bitcast_fusion.11
  52.5 1.2 %pad_maximum_fusion = bf16[2,2,2,2,80,512]{5,4,3,2,1,0:T(8,128)(2,1)} fusion(bf16[2,2,2,2,8,512]{5,4,3,2,1,0:T(8,128)(2,1)S(1)} %get-tuple-element.37, bf16[2,2,2,2,8,512]{5,4,3,2,1,0:T(8,128)(2,1)S(1)} %get-tuple-element.36, bf16[2,2,2,2,32,512]{5,4,3,2,1,0:T(8,128)(2,1)S(1)} %bitcast.63, bf16[2,2,2,2,32,512]{5,4,3,2,1,0:T(8,128)(2,1)S(1)} %bitcast.62), kind=kLoop, calls=%fused_computation | loop fusion | flops 5242880 | bytes 2621440 | tf_op jit(solution)/shard_map/concatenate | solution.py:423
  53.6 2.3 %dynamic-slice_bitcast_fusion.2 = (bf16[2,2,80,512]{3,2,1,0:T(8,128)(2,1)}, bf16[2,2,80,512]{3,2,1,0:T(8,128)(2,1)}, bf16[2,2,80,512]{3,2,1,0:T(8,128)(2,1)}) fusion(bf16[2,2,2,2,80,512]{5,4,3,2,1,0:T(8,128)(2,1)} %pad_maximum_fusion, s32[]{:T(128)S(6)} %select_n.349, s32[]{:T(128)S(6)} %select_n.346, s32[]{:T(128)S(6)} %select_n.352, s32[]{:T(128)S(6)} %select_n.342), kind=kLoop, calls=%fused_computation.12 | loop fusion | bytes 1966096 | tf_op jit(solution)/shard_map/jit(dynamic_index_in_dim)/squeeze | solution.py:373
  55.9 1.5 %collective-permute-start.10 = (bf16[2,2,80,512]{3,2,1,0:T(8,128)(2,1)}, bf16[2,2,80,512]{3,2,1,0:T(8,128)(2,1)}, u32[]{:S(2)}, u32[]{:S(2)}) collective-permute-start(bf16[2,2,80,512]{3,2,1,0:T(8,128)(2,1)} %get-tuple-element.23), channel_id=1, source_target_pairs={{0,17},{1,16},{2,19},{3,18},{4,21},{5,20},{6,23},{7,22},{8,25},{9,... | collective-permute-start | bytes 983048 | tf_op jit(solution)/shard_map/ppermute | solution.py:249
  57.4 1.5 %collective-permute-start.8 = (bf16[2,2,80,512]{3,2,1,0:T(8,128)(2,1)}, bf16[2,2,80,512]{3,2,1,0:T(8,128)(2,1)}, u32[]{:S(2)}, u32[]{:S(2)}) collective-permute-start(bf16[2,2,80,512]{3,2,1,0:T(8,128)(2,1)} %get-tuple-element.22), channel_id=1, source_target_pairs={{0,16},{1,17},{2,18},{3,19},{4,20},{5,21},{6,22},{7,23},{8,24},{9,... | collective-permute-start | bytes 983048 | tf_op jit(solution)/shard_map/ppermute | solution.py:249
  59.4 3.4 %collective-permute-start.19 = (bf16[32,1024]{1,0:T(8,128)(2,1)}, bf16[32,1024]{1,0:T(8,128)(2,1)}, u32[]{:S(2)}, u32[]{:S(2)}) collective-permute-start(bf16[32,1024]{1,0:T(8,128)(2,1)} %get-tuple-element.35), channel_id=1, source_target_pairs={{0,4},{1,5},{2,6},{3,7},{4,0},{5,1},{6,2},{7,3},{8,12},{9,13},{10,... | collective-permute-start | bytes 196616 | tf_op jit(solution)/shard_map/ppermute | solution.py:249
  63.1 3.6 %collective-permute-done.19 = bf16[32,1024]{1,0:T(8,128)(2,1)} collective-permute-done((bf16[32,1024]{1,0:T(8,128)(2,1)}, bf16[32,1024]{1,0:T(8,128)(2,1)}, u32[]{:S(2)}, u32[]{:S(2)}) %collective-permute-start.19) | collective-permute-done | bytes 65568 | tf_op jit(solution)/shard_map/ppermute | solution.py:249
  66.8 2.4 %collective-permute-done.20 = bf16[32,1024]{1,0:T(8,128)(2,1)} collective-permute-done((bf16[32,1024]{1,0:T(8,128)(2,1)}, bf16[32,1024]{1,0:T(8,128)(2,1)}, u32[]{:S(2)}, u32[]{:S(2)}) %collective-permute-start.20) | collective-permute-done | bytes 65568 | tf_op jit(solution)/shard_map/ppermute | solution.py:249
  69.2 1.6 %fusion.9 = f32[32,1024]{1,0:T(8,128)} fusion(bf16[32,1024]{1,0:T(8,128)(2,1)} %collective-permute-done.20, bf16[32,1024]{1,0:T(8,128)(2,1)} %collective-permute-done.19, bf16[32,1024]{1,0:T(8,128)(2,1)S(1)} %collective-permute-done.18, bf16[2,2,32,1024]{3,2,1,0:T(8,128)(2,1)S(1)} %fusion.5, s32[]{:T(128)S(6)} %select_n.357, s32[]{:T(128)S(6)} %select_n.362), kind=kLoop, calls=%fused_computation.24 | loop fusion | flops 229376 | bytes 393224 | tf_op jit(solution)/shard_map/add | solution.py:383
  70.7 2.2 %collective-permute-done.8 = bf16[2,2,80,512]{3,2,1,0:T(8,128)(2,1)} collective-permute-done((bf16[2,2,80,512]{3,2,1,0:T(8,128)(2,1)}, bf16[2,2,80,512]{3,2,1,0:T(8,128)(2,1)}, u32[]{:S(2)}, u32[]{:S(2)}) %collective-permute-start.8) | collective-permute-done | bytes 327712 | tf_op jit(solution)/shard_map/ppermute | solution.py:249
  73.0 1.4 %fusion.2 = bf16[2,2,80,512]{3,2,1,0:T(8,128)(2,1)S(1)} fusion(bf16[2,2,80,512]{3,2,1,0:T(8,128)(2,1)} %collective-permute-done.10, bf16[2,2,80,512]{3,2,1,0:T(8,128)(2,1)} %collective-permute-done.9, bf16[2,2,80,512]{3,2,1,0:T(8,128)(2,1)} %collective-permute-done.8, bf16[2,2,2,2,80,512]{5,4,3,2,1,0:T(8,128)(2,1)} %pad_maximum_fusion, s32[]{:T(128)S(6)} %select_n.342, ...), kind=kLoop, calls=%fused_computation.4 | loop fusion | flops 1310720 | bytes 1638408 | tf_op jit(solution)/shard_map/convert_element_type | solution.py:385
  74.4 1.4 %collective-permute-start.11 = (bf16[80,512]{1,0:T(8,128)(2,1)S(1)}, bf16[80,512]{1,0:T(8,128)(2,1)S(1)}, u32[]{:S(2)}, u32[]{:S(2)}) collective-permute-start(bf16[80,512]{1,0:T(8,128)(2,1)S(1)} %get-tuple-element.30), channel_id=1, source_target_pairs={{0,2},{1,3},{2,0},{3,1},{4,6},{5,7},{6,4},{7,5},{8,10},{9,11},{10,... | collective-permute-start | bytes 245768 | tf_op jit(solution)/shard_map/ppermute | solution.py:249
  75.9 2.3 %collective-permute-start.12 = (bf16[80,512]{1,0:T(8,128)(2,1)S(1)}, bf16[80,512]{1,0:T(8,128)(2,1)S(1)}, u32[]{:S(2)}, u32[]{:S(2)}) collective-permute-start(bf16[80,512]{1,0:T(8,128)(2,1)S(1)} %get-tuple-element.32), channel_id=1, source_target_pairs={{0,4},{1,5},{2,6},{3,7},{4,0},{5,1},{6,2},{7,3},{8,12},{9,13},{10,... | collective-permute-start | bytes 245768 | tf_op jit(solution)/shard_map/ppermute | solution.py:249
  78.2 1.2 %collective-permute-start.13 = (bf16[80,512]{1,0:T(8,128)(2,1)S(1)}, bf16[80,512]{1,0:T(8,128)(2,1)S(1)}, u32[]{:S(2)}, u32[]{:S(2)}) collective-permute-start(bf16[80,512]{1,0:T(8,128)(2,1)S(1)} %get-tuple-element.31), channel_id=1, source_target_pairs={{0,6},{1,7},{2,4},{3,5},{4,2},{5,3},{6,0},{7,1},{8,14},{9,15},{10,... | collective-permute-start | bytes 245768 | tf_op jit(solution)/shard_map/ppermute | solution.py:249
  79.4 2.8 %shard_map.116 = bf16[512,1024]{1,0:T(8,128)(2,1)} custom-call(s32[2]{0:T(128)S(1)} %pad_add_fusion.place_ref, bf16[512,512]{1,0:T(8,128)(2,1)S(1)} %get-tuple-element.15.mine_ref.qg_own_ref, bf16[512,512]{1,0:T(8,128)(2,1)S(1)} %collective-permute-done.6.theirs_ref, bf16[1024,1024]{1,0:T(8,128)(2,1)S(1)} %copy-done.1), custom_call_target="tpu_custom_call" | custom-call | flops 1073741824 | bytes 1048576 | tf_op jit(solution)/shard_map/pallas_call | solution.py:263
  82.2 3.0 %collective-permute-done.13 = bf16[80,512]{1,0:T(8,128)(2,1)S(1)} collective-permute-done((bf16[80,512]{1,0:T(8,128)(2,1)S(1)}, bf16[80,512]{1,0:T(8,128)(2,1)S(1)}, u32[]{:S(2)}, u32[]{:S(2)}) %collective-permute-start.13) | collective-permute-done | bytes 81952 | tf_op jit(solution)/shard_map/ppermute | solution.py:249
  (56 shorter events, 5.8 us)
Async XLA Ops:
  0.6 0.8 copy-start
  1.5 4.9 %collective-permute-start.2 = (bf16[1,16,1024]{2,1,0:T(8,128)(2,1)S(1)}, bf16[1,16,1024]{2,1,0:T(8,128)(2,1)S(1)}, u32[]{:S(2)}, u32[]{:S(2)}) collective-permute-start(bf16[1,16,1024]{2,1,0:T(8,128)(2,1)S(1)} %dynamic-slice_bitcast_fusion.14), channel_id=1, source_target_pairs={{0,1},{1,0},{2,3},{3,2},{4,5},{5,4},{6,7},{7,6},{8,9},{9,8},{10,11... | collective-permute-start | bytes 98312 | tf_op jit(solution)/shard_map/ppermute | solution.py:249
  4.5 16.2 %collective-permute-start = (bf16[512,1024]{1,0:T(8,128)(2,1)}, bf16[512,1024]{1,0:T(8,128)(2,1)S(1)}, u32[]{:S(2)}, u32[]{:S(2)}) collective-permute-start(bf16[512,1024]{1,0:T(8,128)(2,1)} %own_ref.7), channel_id=1, source_target_pairs={{0,8},{1,9},{2,10},{3,11},{4,12},{5,13},{6,14},{7,15},{8,0},{9,1},... | collective-permute-start | bytes 3145736 | tf_op jit(solution)/shard_map/ppermute | solution.py:249
  4.5 20.1 %collective-permute-start.1 = (bf16[512,1024]{1,0:T(8,128)(2,1)}, bf16[512,1024]{1,0:T(8,128)(2,1)S(1)}, u32[]{:S(2)}, u32[]{:S(2)}) collective-permute-start(bf16[512,1024]{1,0:T(8,128)(2,1)} %own_ref.6), channel_id=1, source_target_pairs={{0,8},{1,9},{2,10},{3,11},{4,12},{5,13},{6,14},{7,15},{8,0},{9,1},... | collective-permute-start | bytes 3145736 | tf_op jit(solution)/shard_map/ppermute | solution.py:249
  6.4 4.4 %collective-permute-start.3 = (bf16[2,16,1024]{2,1,0:T(8,128)(2,1)S(1)}, bf16[2,16,1024]{2,1,0:T(8,128)(2,1)S(1)}, u32[]{:S(2)}, u32[]{:S(2)}) collective-permute-start(bf16[2,16,1024]{2,1,0:T(8,128)(2,1)S(1)} %pad_maximum_fusion.4), channel_id=1, source_target_pairs={{0,2},{1,3},{2,0},{3,1},{4,6},{5,7},{6,4},{7,5},{8,10},{9,11},{10,... | collective-permute-start | bytes 196616 | tf_op jit(solution)/shard_map/ppermute | solution.py:249
  10.8 7.5 %collective-permute-start.4 = (bf16[4,16,1024]{2,1,0:T(8,128)(2,1)S(1)}, bf16[4,16,1024]{2,1,0:T(8,128)(2,1)S(1)}, u32[]{:S(2)}, u32[]{:S(2)}) collective-permute-start(bf16[4,16,1024]{2,1,0:T(8,128)(2,1)S(1)} %pad_maximum_fusion.2), channel_id=1, source_target_pairs={{0,4},{1,5},{2,6},{3,7},{4,0},{5,1},{6,2},{7,3},{8,12},{9,13},{10,... | collective-permute-start | bytes 393224 | tf_op jit(solution)/shard_map/ppermute | solution.py:249
  18.4 9.5 %collective-permute-start.5 = (bf16[8,16,1024]{2,1,0:T(8,128)(2,1)S(1)}, bf16[8,16,1024]{2,1,0:T(8,128)(2,1)S(1)}, u32[]{:S(2)}, u32[]{:S(2)}) collective-permute-start(bf16[8,16,1024]{2,1,0:T(8,128)(2,1)S(1)} %pad_maximum_fusion.1.mine_ref), channel_id=1, source_target_pairs={{0,8},{1,9},{2,10},{3,11},{4,12},{5,13},{6,14},{7,15},{8,0},{9,1},... | collective-permute-start | bytes 786440 | tf_op jit(solution)/shard_map/ppermute | solution.py:249
  24.6 3.3 %copy-start.3 = (bf16[512,1024]{1,0:T(8,128)(2,1)}, bf16[512,1024]{1,0:T(8,128)(2,1)S(1)}, u32[]{:S(2)}) copy-start(bf16[512,1024]{1,0:T(8,128)(2,1)S(1)} %collective-permute-done.1.partner_ref) | copy-start | bytes 3145732
  35.0 11.9 %collective-permute-start.15 = (bf16[2,2,32,1024]{3,2,1,0:T(8,128)(2,1)S(1)}, bf16[2,2,32,1024]{3,2,1,0:T(8,128)(2,1)S(1)}, u32[]{:S(2)}, u32[]{:S(2)}) collective-permute-start(bf16[2,2,32,1024]{3,2,1,0:T(8,128)(2,1)S(1)} %get-tuple-element.25), channel_id=1, source_target_pairs={{0,16},{1,17},{2,18},{3,19},{4,20},{5,21},{6,22},{7,23},{8,24},{9,... | collective-permute-start | bytes 786440 | tf_op jit(solution)/shard_map/ppermute | solution.py:249
  36.8 14.0 %collective-permute-start.16 = (bf16[2,2,32,1024]{3,2,1,0:T(8,128)(2,1)S(1)}, bf16[2,2,32,1024]{3,2,1,0:T(8,128)(2,1)S(1)}, u32[]{:S(2)}, u32[]{:S(2)}) collective-permute-start(bf16[2,2,32,1024]{3,2,1,0:T(8,128)(2,1)S(1)} %get-tuple-element.27), channel_id=1, source_target_pairs={{0,1},{1,0},{2,3},{3,2},{4,5},{5,4},{6,7},{7,6},{8,9},{9,8},{10,11... | collective-permute-start | bytes 786440 | tf_op jit(solution)/shard_map/ppermute | solution.py:249
  38.3 12.5 %collective-permute-start.17 = (bf16[2,2,32,1024]{3,2,1,0:T(8,128)(2,1)S(1)}, bf16[2,2,32,1024]{3,2,1,0:T(8,128)(2,1)S(1)}, u32[]{:S(2)}, u32[]{:S(2)}) collective-permute-start(bf16[2,2,32,1024]{3,2,1,0:T(8,128)(2,1)S(1)} %get-tuple-element.26), channel_id=1, source_target_pairs={{0,17},{1,16},{2,19},{3,18},{4,21},{5,20},{6,23},{7,22},{8,25},{9,... | collective-permute-start | bytes 786440 | tf_op jit(solution)/shard_map/ppermute | solution.py:249
  38.5 6.9 %copy-start.2 = (bf16[512,1024]{1,0:T(8,128)(2,1)S(1)}, bf16[512,1024]{1,0:T(8,128)(2,1)}, u32[]{:S(2)}) copy-start(bf16[512,1024]{1,0:T(8,128)(2,1)} %own_ref.7) | copy-start | bytes 3145732
  45.4 7.0 %collective-permute-start.7 = (bf16[2,64,1024]{2,1,0:T(8,128)(2,1)S(1)}, bf16[2,64,1024]{2,1,0:T(8,128)(2,1)S(1)}, u32[]{:S(2)}, u32[]{:S(2)}) collective-permute-start(bf16[2,64,1024]{2,1,0:T(8,128)(2,1)S(1)} %get-tuple-element.18), channel_id=1, source_target_pairs={{0,8},{1,9},{2,10},{3,11},{4,12},{5,13},{6,14},{7,15},{8,0},{9,1},... | collective-permute-start | bytes 786440 | tf_op jit(solution)/shard_map/ppermute | solution.py:249
  51.7 11.1 %collective-permute-start.18 = (bf16[32,1024]{1,0:T(8,128)(2,1)S(1)}, bf16[32,1024]{1,0:T(8,128)(2,1)S(1)}, u32[]{:S(2)}, u32[]{:S(2)}) collective-permute-start(bf16[32,1024]{1,0:T(8,128)(2,1)S(1)} %get-tuple-element.33), channel_id=1, source_target_pairs={{0,2},{1,3},{2,0},{3,1},{4,6},{5,7},{6,4},{7,5},{8,10},{9,11},{10,... | collective-permute-start | bytes 196616 | tf_op jit(solution)/shard_map/ppermute | solution.py:249
  53.6 25.7 %copy-start.1 = (bf16[1024,1024]{1,0:T(8,128)(2,1)S(1)}, bf16[1024,1024]{1,0:T(8,128)(2,1)}, u32[]{:S(2)}) copy-start(bf16[1024,1024]{1,0:T(8,128)(2,1)} %weight_ref.5) | copy-start | bytes 6291460
  55.9 14.8 %collective-permute-start.10 = (bf16[2,2,80,512]{3,2,1,0:T(8,128)(2,1)}, bf16[2,2,80,512]{3,2,1,0:T(8,128)(2,1)}, u32[]{:S(2)}, u32[]{:S(2)}) collective-permute-start(bf16[2,2,80,512]{3,2,1,0:T(8,128)(2,1)} %get-tuple-element.23), channel_id=1, source_target_pairs={{0,17},{1,16},{2,19},{3,18},{4,21},{5,20},{6,23},{7,22},{8,25},{9,... | collective-permute-start | bytes 983048 | tf_op jit(solution)/shard_map/ppermute | solution.py:249
  57.4 15.5 %collective-permute-start.8 = (bf16[2,2,80,512]{3,2,1,0:T(8,128)(2,1)}, bf16[2,2,80,512]{3,2,1,0:T(8,128)(2,1)}, u32[]{:S(2)}, u32[]{:S(2)}) collective-permute-start(bf16[2,2,80,512]{3,2,1,0:T(8,128)(2,1)} %get-tuple-element.22), channel_id=1, source_target_pairs={{0,16},{1,17},{2,18},{3,19},{4,20},{5,21},{6,22},{7,23},{8,24},{9,... | collective-permute-start | bytes 983048 | tf_op jit(solution)/shard_map/ppermute | solution.py:249
  58.9 14.1 %collective-permute-start.9 = (bf16[2,2,80,512]{3,2,1,0:T(8,128)(2,1)}, bf16[2,2,80,512]{3,2,1,0:T(8,128)(2,1)}, u32[]{:S(2)}, u32[]{:S(2)}) collective-permute-start(bf16[2,2,80,512]{3,2,1,0:T(8,128)(2,1)} %get-tuple-element.24), channel_id=1, source_target_pairs={{0,1},{1,0},{2,3},{3,2},{4,5},{5,4},{6,7},{7,6},{8,9},{9,8},{10,11... | collective-permute-start | bytes 983048 | tf_op jit(solution)/shard_map/ppermute | solution.py:249
  59.4 7.3 %collective-permute-start.19 = (bf16[32,1024]{1,0:T(8,128)(2,1)}, bf16[32,1024]{1,0:T(8,128)(2,1)}, u32[]{:S(2)}, u32[]{:S(2)}) collective-permute-start(bf16[32,1024]{1,0:T(8,128)(2,1)} %get-tuple-element.35), channel_id=1, source_target_pairs={{0,4},{1,5},{2,6},{3,7},{4,0},{5,1},{6,2},{7,3},{8,12},{9,13},{10,... | collective-permute-start | bytes 196616 | tf_op jit(solution)/shard_map/ppermute | solution.py:249
  62.8 6.4 %collective-permute-start.20 = (bf16[32,1024]{1,0:T(8,128)(2,1)}, bf16[32,1024]{1,0:T(8,128)(2,1)}, u32[]{:S(2)}, u32[]{:S(2)}) collective-permute-start(bf16[32,1024]{1,0:T(8,128)(2,1)} %get-tuple-element.34), channel_id=1, source_target_pairs={{0,6},{1,7},{2,4},{3,5},{4,2},{5,3},{6,0},{7,1},{8,14},{9,15},{10,... | collective-permute-start | bytes 196616 | tf_op jit(solution)/shard_map/ppermute | solution.py:249
  66.8 12.6 %collective-permute-start.6 = (bf16[512,512]{1,0:T(8,128)(2,1)S(1)}, bf16[512,512]{1,0:T(8,128)(2,1)S(1)}, u32[]{:S(2)}, u32[]{:S(2)}) collective-permute-start(bf16[512,512]{1,0:T(8,128)(2,1)S(1)} %get-tuple-element.16.qg_partner_ref), channel_id=1, source_target_pairs={{0,8},{1,9},{2,10},{3,11},{4,12},{5,13},{6,14},{7,15},{8,0},{9,1},... | collective-permute-start | bytes 1572872 | tf_op jit(solution)/shard_map/ppermute | solution.py:249
  74.4 7.7 %collective-permute-start.11 = (bf16[80,512]{1,0:T(8,128)(2,1)S(1)}, bf16[80,512]{1,0:T(8,128)(2,1)S(1)}, u32[]{:S(2)}, u32[]{:S(2)}) collective-permute-start(bf16[80,512]{1,0:T(8,128)(2,1)S(1)} %get-tuple-element.30), channel_id=1, source_target_pairs={{0,2},{1,3},{2,0},{3,1},{4,6},{5,7},{6,4},{7,5},{8,10},{9,11},{10,... | collective-permute-start | bytes 245768 | tf_op jit(solution)/shard_map/ppermute | solution.py:249
  75.9 6.3 %collective-permute-start.12 = (bf16[80,512]{1,0:T(8,128)(2,1)S(1)}, bf16[80,512]{1,0:T(8,128)(2,1)S(1)}, u32[]{:S(2)}, u32[]{:S(2)}) collective-permute-start(bf16[80,512]{1,0:T(8,128)(2,1)S(1)} %get-tuple-element.32), channel_id=1, source_target_pairs={{0,4},{1,5},{2,6},{3,7},{4,0},{5,1},{6,2},{7,3},{8,12},{9,13},{10,... | collective-permute-start | bytes 245768 | tf_op jit(solution)/shard_map/ppermute | solution.py:249
  78.2 7.0 %collective-permute-start.13 = (bf16[80,512]{1,0:T(8,128)(2,1)S(1)}, bf16[80,512]{1,0:T(8,128)(2,1)S(1)}, u32[]{:S(2)}, u32[]{:S(2)}) collective-permute-start(bf16[80,512]{1,0:T(8,128)(2,1)S(1)} %get-tuple-element.31), channel_id=1, source_target_pairs={{0,6},{1,7},{2,4},{3,5},{4,2},{5,3},{6,0},{7,1},{8,14},{9,15},{10,... | collective-permute-start | bytes 245768 | tf_op jit(solution)/shard_map/ppermute | solution.py:249
  85.3 1.3 %collective-permute-start.14 = (f32[32,512]{1,0:T(8,128)S(1)}, f32[32,512]{1,0:T(8,128)S(1)}, u32[]{:S(2)}, u32[]{:S(2)}) collective-permute-start(f32[32,512]{1,0:T(8,128)S(1)} %get-tuple-element.43), channel_id=1, source_target_pairs={{0,8},{1,9},{2,10},{3,11},{4,12},{5,13},{6,14},{7,15},{8,0},{9,1},... | collective-permute-start | bytes 196616 | tf_op jit(solution)/shard_map/ppermute | solution.py:249

commit v6 on v5

--- a/solution.py
+++ b/solution.py
@@ -128,15 +128,22 @@
         kv_ref[0, pl.ds(at, width), :] = key_part.T
         kv_ref[1, pl.ds(at, width), :] = both[:, width:].T
 
+    def score(first):
+        part = pl.ds(first, size)
+        key_rows = jnp.concatenate([kv_ref[0, part, :], bias], axis=0)
+        query_rows = jnp.concatenate([q_ref[part, :], marks], axis=0)
+        return dot(key_rows.T, query_rows, ((1,), (0,)))
+
     keys_values(0)
+    following = score(0)
     for at in range(0, half_width, width):
         if at + width < half_width:
             keys_values(at + width)
         for first in range(at, at + width, size):
             part = pl.ds(first, size)
-            key_rows = jnp.concatenate([kv_ref[0, part, :], bias], axis=0)
-            query_rows = jnp.concatenate([q_ref[part, :], marks], axis=0)
-            scores = dot(key_rows.T, query_rows, ((1,), (0,)))
+            scores = following
+            if first + size < half_width:
+                following = score(first + size)
             row_max = jnp.max(scores, axis=0, keepdims=True)
             unnormed = jnp.exp(scores - row_max)
             row_sum = jnp.sum(unnormed, axis=0, keepdims=True)
@@ -175,15 +182,22 @@
     half_width = q_ref.shape[0]
     block_rows = qg_own_ref.shape[1]
     width = GROUP * size
+
+    def score_grads(first):
+        part = pl.ds(first, size)
+        return dot(kv_ref[1, part, :].T, g_ref[part, :], ((1,), (0,)))
+
+    following = score_grads(0)
     for at in range(0, half_width, width):
         key_parts, value_parts = [], []
         for first in range(at, at + width, size):
             part = pl.ds(first, size)
-            grad = g_ref[part, :]
+            grad_scores = following
+            if first + size < half_width:
+                following = score_grads(first + size)
             probs = probs_ref[first // size]
+            value_parts.append(dot(g_ref[part, :], probs, ((1,), (1,))))
             row_dot = row_dot_ref[pl.ds(first // size, 1), :]
-            grad_scores = dot(kv_ref[1, part, :].T, grad, ((1,), (0,)))
-            value_parts.append(dot(grad, probs, ((1,), (1,))))
             logits = (probs.astype(F32) * (grad_scores - row_dot)).astype(BF16)
             query_grad = dot(kv_ref[0, part, :], logits, ((1,), (0,))).astype(BF16)
             qg_own_ref[part, :] = query_grad[:, :block_rows]
@@ -203,24 +217,28 @@
         sent_ref[high] = sum_ref[pl.ds(sent, out_block), :].astype(BF16)
 
 
-def weight_kernel(qg_own_ref, qg_partner_ref, own_ref, partner_ref, out_ref):
-    step = min(256, qg_own_ref.shape[0])
-    for at in range(0, qg_own_ref.shape[0], step):
-        part = pl.ds(at, step)
-        total = dot(qg_own_ref[part, :], own_ref[...], ((1,), (0,)))
-        total += dot(qg_partner_ref[part, :], partner_ref[...], ((1,), (0,)))
-        out_ref[:, part] = total.astype(BF16).T
-
-
-def targets_kernel(block, place_ref, mine_ref, theirs_ref, weight_ref, out_ref):
+def weight_kernel(at, qg_own_ref, qg_partner_ref, own_ref, partner_ref, out_ref):
+    part = pl.ds(at, out_ref.shape[1])
+    total = dot(qg_own_ref[part, :], own_ref[...], ((1,), (0,)))
+    total += dot(qg_partner_ref[part, :], partner_ref[...], ((1,), (0,)))
+    out_ref[...] = total.astype(BF16).T
+
+
+def targets_kernel(block, place_ref, mine_ref, theirs_ref, weight_ref, out_ref, weights, sems):
     other_ref = [1 - place_ref[0]]
+    copies, sources = [], []
+    for at in range(0, mine_ref.shape[0], block):
+        for source, core in ((mine_ref, place_ref), (theirs_ref, other_ref)):
+            index = len(copies)
+            columns = weight_ref.at[:, owned(core, at, block, block)]
+            copies.append(pltpu.make_async_copy(columns, weights.at[index], sems.at[index]))
+            copies[-1].start()
+            sources.append(source[pl.ds(at, block), :])
     total = None
-    for at in range(0, mine_ref.shape[0], block):
-        part = pl.ds(at, block)
-        for source, core in ((mine_ref, place_ref), (theirs_ref, other_ref)):
-            weight = weight_ref[:, owned(core, at, block, block)]
-            term = dot(source[part, :].T, weight, ((1,), (1,)))
-            total = term if total is None else total + term
+    for index, source in enumerate(sources):
+        copies[index].wait()
+        term = dot(source.T, weights[index], ((1,), (1,)))
+        total = term if total is None else total + term
     out_ref[...] = total.astype(BF16)
 
 
@@ -381,8 +399,9 @@
         total = piece([0] * len(stage)).astype(F32)
         for one in moved:
             total = total + one.astype(F32)
+        total = total if last else total.astype(BF16)
         left = [mask for mask in masks if mask not in stage]
-        return (total if last else total.astype(BF16)), left
+        return total, left
 
     def exchange_rest(array, masks):
         for at, stage in enumerate(stages[1:]):
@@ -394,7 +413,6 @@
 
     wo_split = wo_term.reshape(*high_bits, *seq_bits, out_rows, width)
     wo_part, left_masks = exchange(wo_split, all_masks, stages[0])
-    grad_wo = exchange_rest(wo_part, left_masks)
 
     query_own, query_partner, ctx_kept, ctx_sent = call(
         partial(back_kernel, head_size, score_scale),
@@ -409,31 +427,42 @@
         scratch=[pltpu.VMEM((context_rows, width), F32)],
     )
     ctx_moved = swap(ctx_sent, core_mask)
-    (wq_term,) = call(
-        weight_kernel,
-        [query_own, query_partner, targets, targets_swapped],
-        [((width, half_width), BF16)],
-        product,
-    )
-    ctx_pair = (ctx_kept + ctx_moved.astype(F32)).astype(BF16)
-    ctx_pair = ctx_pair.reshape(*high_bits, *seq_bits, ctx_out, width)
-    wq_split = wq_term.reshape(high_count, 2, seq_count, out_rows, half_width)
-    tail = [wq_split[:, which].reshape(*high_bits, *seq_bits, out_rows, half_width) for which in (0, 1)]
-    tail += [ctx_pair[..., :half_width], ctx_pair[..., half_width:]]
-    tail, _ = exchange(jnp.concatenate(tail, axis=-2), all_masks, stages[0])
-    tail = exchange_rest(tail, left_masks)
-
-    wq_sums = tail[: 2 * out_rows].reshape(2, out_rows, half_width)
-    sent = lax.dynamic_index_in_dim(wq_sums, 1 - core, 0, keepdims=False)
-    mine = lax.dynamic_index_in_dim(wq_sums, core, 0, keepdims=False)
+
+    def stacked(array):
+        return [array[..., at : at + block] for at in range(0, array.shape[-1], block)]
+
+    parts = []
+    for part in range(high_count):
+        (wq_term,) = call(
+            partial(weight_kernel, part * block),
+            [query_own, query_partner, targets, targets_swapped],
+            [((width, block), BF16)],
+            product // high_count,
+        )
+        wq_split = wq_term.reshape(high_count, 2, seq_count, out_rows, block)
+        pieces = [
+            wq_split[:, which].reshape(*high_bits, *seq_bits, out_rows, block) for which in (0, 1)
+        ]
+        if part == 0:
+            ctx_pair = (ctx_kept + ctx_moved.astype(F32)).astype(BF16)
+            pieces += stacked(ctx_pair.reshape(*high_bits, *seq_bits, ctx_out, width))
+        moved, _ = exchange(jnp.concatenate(pieces, axis=-2), all_masks, stages[0])
+        parts.append(exchange_rest(moved, left_masks))
+
+    first = parts[0]
+    edges = [2 * out_rows, 2 * out_rows + grp_count * ctx_out]
+    wq_sums = jnp.stack([one[: edges[0]].reshape(2, out_rows, block) for one in parts])
+    ctx_sums = first[edges[0] : edges[1]].reshape(grp_count, ctx_out, block)
+    d_context = jnp.concatenate(list(ctx_sums), axis=1).astype(BF16)
+    grad_wo = exchange_rest(wo_part, left_masks)
+    sent = lax.dynamic_index_in_dim(wq_sums, 1 - core, 1, keepdims=False)
+    mine = lax.dynamic_index_in_dim(wq_sums, core, 1, keepdims=False)
     theirs = swap(sent, core_mask)
     pieces = []
-    for at in range(0, half_width, block):
-        pieces.append(jnp.where(core == 0, mine[:, at : at + block], theirs[:, at : at + block]))
-        pieces.append(jnp.where(core == 0, theirs[:, at : at + block], mine[:, at : at + block]))
+    for part in range(high_count):
+        pieces.append(jnp.where(core == 0, mine[part], theirs[part]))
+        pieces.append(jnp.where(core == 0, theirs[part], mine[part]))
     grad_wq = jnp.concatenate(pieces, axis=1)
-    ctx_sums = tail[2 * out_rows :]
-    d_context = jnp.concatenate([ctx_sums[:ctx_out], ctx_sums[ctx_out:]], axis=1).astype(BF16)
 
     returned = swap(query_partner, core_mask)
     (d_targets,) = call(
@@ -441,6 +470,8 @@
         [place, query_own, returned, w_query],
         [((query_rows, width), BF16)],
         product,
+        [pltpu.VMEM((grp_count, width, block), BF16), pltpu.SemaphoreType.DMA((grp_count,))],
+        (3,),
     )
     return (d_targets, d_context, grad_wq, grad_wo)
 

time: 87.7 us -> 97.3 us (1.11)
  starting transfers between devices: 25.3 us -> 36.5 us
  waiting for transfers between devices: 22.7 us -> 26.2 us
  other arithmetic: 6.94 us -> 3.69 us
  local copies, waits for them, and re-layouts: 4.02 us -> 1.2 us
    ppermute x21 -> x27, starting transfers between devices: 25.3 us -> 36.5 us  [swap(): lax.ppermute(array, AXES, [(i, i ^ mask) for i in range(device_count)])]
    ppermute x21 -> x27, waiting for transfers between devices: 22.7 us -> 26.2 us  [swap(): lax.ppermute(array, AXES, [(i, i ^ mask) for i in range(device_count)])]
    squeeze x4 -> x5, local copies, waits for them, and re-layouts: 3.06 us -> 0.19 us  [piece(): part = lax.dynamic_index_in_dim(part, at, masks.index(mask), keepdims=False)]
    convert_element_type x2 -> x3, other arithmetic: 1.63 us -> 0.38 us  [exchange(): total = total if last else total.astype(BF16)]
    concatenate x2 -> x1, other arithmetic: 1.8 us -> 0.61 us  [on_device(): d_context = jnp.concatenate(list(ctx_sums), axis=1).astype(BF16)]
    pallas_call x7 -> x8, Pallas kernels: 27.4 us -> 28.3 us  [call(): pl.pallas_call(kernel, in_specs=specs, out_specs=[in_vmem] * len(outs), o...]
  transfers between devices with their start and end apart: 21 -> 27, of which waited for: 9 -> 9; matrix products, arithmetic and copies ran while one was open for 11% -> 3% of each run, Pallas kernels for 23% -> 16%
where the time goes in v6:
time: 97.3 us; the launch traced here: 97 us
  starting transfers between devices  36.5 us (38%)
  Pallas kernels  28.3 us (29%)
  waiting for transfers between devices  26.2 us (27%)
  other arithmetic  3.69 us (4%)
  local copies, waits for them, and re-layouts  1.2 us (1%)
  between operations  1.05 us (1%)
    ppermute x27, starting transfers between devices, swap(): lax.ppermute(array, AXES, [(i, i ^ mask) for i in range(device_count)])  36.5 us
    pallas_call x8, Pallas kernels, call(): pl.pallas_call(kernel, in_specs=specs, out_specs=[in_vmem] * len(outs), o...  28.3 us
    ppermute x27, waiting for transfers between devices, swap(): lax.ppermute(array, AXES, [(i, i ^ mask) for i in range(device_count)])  26.2 us
  transfers between devices with their start and end apart: 27, of which 9 were waited for; matrix products, arithmetic and copies ran while one was open for 3% of the time, Pallas kernels for 16%

profile of v6, /device:TPU:0, one launch (start us, length us, event | category | flops | bytes accessed | tf_op | source)
XLA Modules:
  0.0 97.0 jit_solution(11514716588881072578)
XLA Ops:
  0.7 0.8 copy-done
  1.5 3.0 %collective-permute-start.2 = (bf16[1,16,1024]{2,1,0:T(8,128)(2,1)S(1)}, bf16[1,16,1024]{2,1,0:T(8,128)(2,1)S(1)}, u32[]{:S(2)}, u32[]{:S(2)}) collective-permute-start(bf16[1,16,1024]{2,1,0:T(8,128)(2,1)S(1)} %dynamic-slice_bitcast_fusion.15), channel_id=1, source_target_pairs={{0,1},{1,0},{2,3},{3,2},{4,5},{5,4},{6,7},{7,6},{8,9},{9,8},{10,11... | collective-permute-start | bytes 98312 | tf_op jit(solution)/shard_map/ppermute | solution.py:267
  6.4 2.1 %collective-permute-start.3 = (bf16[2,16,1024]{2,1,0:T(8,128)(2,1)S(1)}, bf16[2,16,1024]{2,1,0:T(8,128)(2,1)S(1)}, u32[]{:S(2)}, u32[]{:S(2)}) collective-permute-start(bf16[2,16,1024]{2,1,0:T(8,128)(2,1)S(1)} %pad_maximum_fusion.3), channel_id=1, source_target_pairs={{0,2},{1,3},{2,0},{3,1},{4,6},{5,7},{6,4},{7,5},{8,10},{9,11},{10,... | collective-permute-start | bytes 196616 | tf_op jit(solution)/shard_map/ppermute | solution.py:267
  8.6 2.2 %collective-permute-done.3 = bf16[2,16,1024]{2,1,0:T(8,128)(2,1)S(1)} collective-permute-done((bf16[2,16,1024]{2,1,0:T(8,128)(2,1)S(1)}, bf16[2,16,1024]{2,1,0:T(8,128)(2,1)S(1)}, u32[]{:S(2)}, u32[]{:S(2)}) %collective-permute-start.3) | collective-permute-done | bytes 65568 | tf_op jit(solution)/shard_map/ppermute | solution.py:267
  10.8 3.1 %collective-permute-start.4 = (bf16[4,16,1024]{2,1,0:T(8,128)(2,1)S(1)}, bf16[4,16,1024]{2,1,0:T(8,128)(2,1)S(1)}, u32[]{:S(2)}, u32[]{:S(2)}) collective-permute-start(bf16[4,16,1024]{2,1,0:T(8,128)(2,1)S(1)} %pad_maximum_fusion.1), channel_id=1, source_target_pairs={{0,4},{1,5},{2,6},{3,7},{4,0},{5,1},{6,2},{7,3},{8,12},{9,13},{10,... | collective-permute-start | bytes 393224 | tf_op jit(solution)/shard_map/ppermute | solution.py:267
  14.0 4.3 %collective-permute-done.4 = bf16[4,16,1024]{2,1,0:T(8,128)(2,1)S(1)} collective-permute-done((bf16[4,16,1024]{2,1,0:T(8,128)(2,1)S(1)}, bf16[4,16,1024]{2,1,0:T(8,128)(2,1)S(1)}, u32[]{:S(2)}, u32[]{:S(2)}) %collective-permute-start.4) | collective-permute-done | bytes 131104 | tf_op jit(solution)/shard_map/ppermute | solution.py:267
  18.4 2.2 %shard_map.111.wkv_ref = bf16[4,1024,256]{2,1,0:T(8,128)(2,1)S(1)} custom-call(s32[2]{0:T(128)S(1)} %pad_add_fusion.place_ref, bf16[1024,1024]{1,0:T(8,128)(2,1)} %wk_ref.1, bf16[1024,1024]{1,0:T(8,128)(2,1)} %wv_ref.1), custom_call_target="tpu_custom_call" | custom-call | flops 1073741824 | bytes 1048576 | tf_op jit(solution)/shard_map/pallas_call | solution.py:281
  20.6 3.9 %shard_map.112.q_ref = bf16[512,1024]{1,0:T(8,128)(2,1)S(1)} custom-call(s32[2]{0:T(128)S(1)} %pad_add_fusion.place_ref, bf16[1024,1024]{1,0:T(8,128)(2,1)} %weight_ref.5, bf16[512,1024]{1,0:T(8,128)(2,1)} %own_ref.9, bf16[512,1024]{1,0:T(8,128)(2,1)S(1)} %collective-permute-done.partner_ref), custom_call_target="tpu_custom_call" | custom-call | flops 1073741824 | bytes 1048576 | tf_op jit(solution)/shard_map/pallas_call | solution.py:281
  24.6 3.3 %shard_map.113.g_ref = bf16[512,1024]{1,0:T(8,128)(2,1)S(1)} custom-call(s32[2]{0:T(128)S(1)} %pad_add_fusion.place_ref, bf16[1024,1024]{1,0:T(8,128)(2,1)} %weight_ref.4, bf16[512,1024]{1,0:T(8,128)(2,1)} %own_ref.7, bf16[512,1024]{1,0:T(8,128)(2,1)S(1)} %collective-permute-done.1.partner_ref), custom_call_target="tpu_custom_call" | custom-call | flops 1073741824 | bytes 1048576 | tf_op jit(solution)/shard_map/pallas_call | solution.py:281
  27.9 6.4 %shard_map.114 = (bf16[2,512,256]{2,1,0:T(8,128)(2,1)S(1)}, bf16[8,256,1024]{2,1,0:T(8,128)(2,1)S(1)}, f32[8,1024]{1,0:T(8,128)S(1)}, bf16[512,1024]{1,0:T(8,128)(2,1)S(1)}) custom-call(s32[2]{0:T(128)S(1)} %pad_add_fusion.place_ref, bf16[8,16,1024]{2,1,0:T(8,128)(2,1)S(1)} %pad_maximum_fusion.mine_ref, ...), custom_call_target="tpu_custom_call" | custom-call | flops 2147483648 | bytes 1048576 | tf_op jit(solution)/shard_map/pallas_call | solution.py:281
  34.3 6.7 %shard_map.115 = (bf16[512,512]{1,0:T(8,128)(2,1)S(1)}, bf16[512,512]{1,0:T(8,128)(2,1)S(1)}, f32[2,64,1024]{2,1,0:T(8,128)S(1)}, bf16[2,64,1024]{2,1,0:T(8,128)(2,1)S(1)}) custom-call(s32[2]{0:T(128)S(1)} %pad_add_fusion.place_ref, bf16[4,1024,256]{2,1,0:T(8,128)(2,1)S(1)} %shard_map.111.wkv_ref, bf16[512,1024]{1,0:T(8,128)(2,1)S(1)} %shard_map.112.q_ref, ...), custom_call_target="tpu_custom_call" | custom-call | flops 1610612736 | bytes 1048576 | tf_op jit(solution)/shard_map/pallas_call | solution.py:281
  41.6 0.8 shard_map.118
  42.5 1.8 %collective-permute-start.14 = (bf16[2,2,64,256]{3,2,1,0:T(8,128)(2,1)S(1)}, bf16[2,2,64,256]{3,2,1,0:T(8,128)(2,1)S(1)}, u32[]{:S(2)}, u32[]{:S(2)}) collective-permute-start(bf16[2,2,64,256]{3,2,1,0:T(8,128)(2,1)S(1)} %get-tuple-element.28), channel_id=1, source_target_pairs={{0,16},{1,17},{2,18},{3,19},{4,20},{5,21},{6,22},{7,23},{8,24},{9,... | collective-permute-start | bytes 393224 | tf_op jit(solution)/shard_map/ppermute | solution.py:267
  44.3 1.5 %collective-permute-start.15 = (bf16[2,2,64,256]{3,2,1,0:T(8,128)(2,1)S(1)}, bf16[2,2,64,256]{3,2,1,0:T(8,128)(2,1)S(1)}, u32[]{:S(2)}, u32[]{:S(2)}) collective-permute-start(bf16[2,2,64,256]{3,2,1,0:T(8,128)(2,1)S(1)} %get-tuple-element.29), channel_id=1, source_target_pairs={{0,1},{1,0},{2,3},{3,2},{4,5},{5,4},{6,7},{7,6},{8,9},{9,8},{10,11... | collective-permute-start | bytes 393224 | tf_op jit(solution)/shard_map/ppermute | solution.py:267
  46.1 0.8 shard_map.117
  47.0 1.2 %collective-permute-done.14 = bf16[2,2,64,256]{3,2,1,0:T(8,128)(2,1)S(1)} collective-permute-done((bf16[2,2,64,256]{3,2,1,0:T(8,128)(2,1)S(1)}, bf16[2,2,64,256]{3,2,1,0:T(8,128)(2,1)S(1)}, u32[]{:S(2)}, u32[]{:S(2)}) %collective-permute-start.14) | collective-permute-done | bytes 131104 | tf_op jit(solution)/shard_map/ppermute | solution.py:267
  48.2 4.1 %collective-permute-done.15 = bf16[2,2,64,256]{3,2,1,0:T(8,128)(2,1)S(1)} collective-permute-done((bf16[2,2,64,256]{3,2,1,0:T(8,128)(2,1)S(1)}, bf16[2,2,64,256]{3,2,1,0:T(8,128)(2,1)S(1)}, u32[]{:S(2)}, u32[]{:S(2)}) %collective-permute-start.15) | collective-permute-done | bytes 131104 | tf_op jit(solution)/shard_map/ppermute | solution.py:267
  53.1 3.4 %collective-permute-start.18 = (bf16[64,256]{1,0:T(8,128)(2,1)S(1)}, bf16[64,256]{1,0:T(8,128)(2,1)S(1)}, u32[]{:S(2)}, u32[]{:S(2)}) collective-permute-start(bf16[64,256]{1,0:T(8,128)(2,1)S(1)} %get-tuple-element.49), channel_id=1, source_target_pairs={{0,4},{1,5},{2,6},{3,7},{4,0},{5,1},{6,2},{7,3},{8,12},{9,13},{10,... | collective-permute-start | bytes 98312 | tf_op jit(solution)/shard_map/ppermute | solution.py:267
  56.9 1.3 %collective-permute-start.21 = (bf16[2,2,32,1024]{3,2,1,0:T(8,128)(2,1)S(1)}, bf16[2,2,32,1024]{3,2,1,0:T(8,128)(2,1)S(1)}, u32[]{:S(2)}, u32[]{:S(2)}) collective-permute-start(bf16[2,2,32,1024]{3,2,1,0:T(8,128)(2,1)S(1)} %get-tuple-element.22), channel_id=1, source_target_pairs={{0,16},{1,17},{2,18},{3,19},{4,20},{5,21},{6,22},{7,23},{8,24},{9,... | collective-permute-start | bytes 786440 | tf_op jit(solution)/shard_map/ppermute | solution.py:267
  58.4 2.2 %collective-permute-start.22 = (bf16[2,2,32,1024]{3,2,1,0:T(8,128)(2,1)S(1)}, bf16[2,2,32,1024]{3,2,1,0:T(8,128)(2,1)S(1)}, u32[]{:S(2)}, u32[]{:S(2)}) collective-permute-start(bf16[2,2,32,1024]{3,2,1,0:T(8,128)(2,1)S(1)} %get-tuple-element.24), channel_id=1, source_target_pairs={{0,1},{1,0},{2,3},{3,2},{4,5},{5,4},{6,7},{7,6},{8,9},{9,8},{10,11... | collective-permute-start | bytes 786440 | tf_op jit(solution)/shard_map/ppermute | solution.py:267
  60.6 1.6 %collective-permute-done.19 = bf16[64,256]{1,0:T(8,128)(2,1)S(1)} collective-permute-done((bf16[64,256]{1,0:T(8,128)(2,1)S(1)}, bf16[64,256]{1,0:T(8,128)(2,1)S(1)}, u32[]{:S(2)}, u32[]{:S(2)}) %collective-permute-start.19) | collective-permute-done | bytes 32800 | tf_op jit(solution)/shard_map/ppermute | solution.py:267
  62.2 1.5 %collective-permute-start.23 = (bf16[2,2,32,1024]{3,2,1,0:T(8,128)(2,1)S(1)}, bf16[2,2,32,1024]{3,2,1,0:T(8,128)(2,1)S(1)}, u32[]{:S(2)}, u32[]{:S(2)}) collective-permute-start(bf16[2,2,32,1024]{3,2,1,0:T(8,128)(2,1)S(1)} %get-tuple-element.23), channel_id=1, source_target_pairs={{0,17},{1,16},{2,19},{3,18},{4,21},{5,20},{6,23},{7,22},{8,25},{9,... | collective-permute-start | bytes 786440 | tf_op jit(solution)/shard_map/ppermute | solution.py:267
  63.9 1.5 %collective-permute-start.10 = (bf16[2,2,96,256]{3,2,1,0:T(8,128)(2,1)S(1)}, bf16[2,2,96,256]{3,2,1,0:T(8,128)(2,1)S(1)}, u32[]{:S(2)}, u32[]{:S(2)}) collective-permute-start(bf16[2,2,96,256]{3,2,1,0:T(8,128)(2,1)S(1)} %get-tuple-element.26), channel_id=1, source_target_pairs={{0,17},{1,16},{2,19},{3,18},{4,21},{5,20},{6,23},{7,22},{8,25},{9,... | collective-permute-start | bytes 589832 | tf_op jit(solution)/shard_map/ppermute | solution.py:267
  65.4 1.2 %collective-permute-start.8 = (bf16[2,2,96,256]{3,2,1,0:T(8,128)(2,1)S(1)}, bf16[2,2,96,256]{3,2,1,0:T(8,128)(2,1)S(1)}, u32[]{:S(2)}, u32[]{:S(2)}) collective-permute-start(bf16[2,2,96,256]{3,2,1,0:T(8,128)(2,1)S(1)} %get-tuple-element.25), channel_id=1, source_target_pairs={{0,16},{1,17},{2,18},{3,19},{4,20},{5,21},{6,22},{7,23},{8,24},{9,... | collective-permute-start | bytes 589832 | tf_op jit(solution)/shard_map/ppermute | solution.py:267
  66.7 9.1 %collective-permute-done.22 = bf16[2,2,32,1024]{3,2,1,0:T(8,128)(2,1)S(1)} collective-permute-done((bf16[2,2,32,1024]{3,2,1,0:T(8,128)(2,1)S(1)}, bf16[2,2,32,1024]{3,2,1,0:T(8,128)(2,1)S(1)}, u32[]{:S(2)}, u32[]{:S(2)}) %collective-permute-start.22) | collective-permute-done | bytes 262176 | tf_op jit(solution)/shard_map/ppermute | solution.py:267
  75.8 2.5 %collective-permute-start.9 = (bf16[2,2,96,256]{3,2,1,0:T(8,128)(2,1)S(1)}, bf16[2,2,96,256]{3,2,1,0:T(8,128)(2,1)S(1)}, u32[]{:S(2)}, u32[]{:S(2)}) collective-permute-start(bf16[2,2,96,256]{3,2,1,0:T(8,128)(2,1)S(1)} %get-tuple-element.27), channel_id=1, source_target_pairs={{0,1},{1,0},{2,3},{3,2},{4,5},{5,4},{6,7},{7,6},{8,9},{9,8},{10,11... | collective-permute-start | bytes 589832 | tf_op jit(solution)/shard_map/ppermute | solution.py:267
  78.6 1.2 %collective-permute-start.25 = (bf16[32,1024]{1,0:T(8,128)(2,1)S(1)}, bf16[32,1024]{1,0:T(8,128)(2,1)S(1)}, u32[]{:S(2)}, u32[]{:S(2)}) collective-permute-start(bf16[32,1024]{1,0:T(8,128)(2,1)S(1)} %get-tuple-element.37), channel_id=1, source_target_pairs={{0,4},{1,5},{2,6},{3,7},{4,0},{5,1},{6,2},{7,3},{8,12},{9,13},{10,... | collective-permute-start | bytes 196616 | tf_op jit(solution)/shard_map/ppermute | solution.py:267
  79.9 3.1 %collective-permute-start.26 = (bf16[32,1024]{1,0:T(8,128)(2,1)S(1)}, bf16[32,1024]{1,0:T(8,128)(2,1)S(1)}, u32[]{:S(2)}, u32[]{:S(2)}) collective-permute-start(bf16[32,1024]{1,0:T(8,128)(2,1)S(1)} %get-tuple-element.36), channel_id=1, source_target_pairs={{0,6},{1,7},{2,4},{3,5},{4,2},{5,3},{6,0},{7,1},{8,14},{9,15},{10,... | collective-permute-start | bytes 196616 | tf_op jit(solution)/shard_map/ppermute | solution.py:267
  83.2 2.2 %collective-permute-start.12 = (bf16[96,256]{1,0:T(8,128)(2,1)S(1)}, bf16[96,256]{1,0:T(8,128)(2,1)S(1)}, u32[]{:S(2)}, u32[]{:S(2)}) collective-permute-start(bf16[96,256]{1,0:T(8,128)(2,1)S(1)} %get-tuple-element.40), channel_id=1, source_target_pairs={{0,4},{1,5},{2,6},{3,7},{4,0},{5,1},{6,2},{7,3},{8,12},{9,13},{10,... | collective-permute-start | bytes 147464 | tf_op jit(solution)/shard_map/ppermute | solution.py:267
  85.4 2.2 %collective-permute-start.13 = (bf16[96,256]{1,0:T(8,128)(2,1)S(1)}, bf16[96,256]{1,0:T(8,128)(2,1)S(1)}, u32[]{:S(2)}, u32[]{:S(2)}) collective-permute-start(bf16[96,256]{1,0:T(8,128)(2,1)S(1)} %get-tuple-element.39), channel_id=1, source_target_pairs={{0,6},{1,7},{2,4},{3,5},{4,2},{5,3},{6,0},{7,1},{8,14},{9,15},{10,... | collective-permute-start | bytes 147464 | tf_op jit(solution)/shard_map/ppermute | solution.py:267
  88.3 3.0 %collective-permute-done.13 = bf16[96,256]{1,0:T(8,128)(2,1)S(1)} collective-permute-done((bf16[96,256]{1,0:T(8,128)(2,1)S(1)}, bf16[96,256]{1,0:T(8,128)(2,1)S(1)}, u32[]{:S(2)}, u32[]{:S(2)}) %collective-permute-start.13) | collective-permute-done | bytes 49184 | tf_op jit(solution)/shard_map/ppermute | solution.py:267
  92.1 4.2 %shard_map.116 = bf16[512,1024]{1,0:T(8,128)(2,1)} custom-call(s32[2]{0:T(128)S(1)} %pad_add_fusion.place_ref, bf16[512,512]{1,0:T(8,128)(2,1)S(1)} %get-tuple-element.15.mine_ref.qg_own_ref, bf16[512,512]{1,0:T(8,128)(2,1)S(1)} %collective-permute-done.6.theirs_ref, bf16[1024,1024]{1,0:T(8,128)(2,1)} %weight_ref.5), custom_call_target="tpu_custom_call" | custom-call | flops 1073741824 | bytes 1048576 | tf_op jit(solution)/shard_map/pallas_call | solution.py:281
  (76 shorter events, 7.5 us)
Async XLA Ops:
  0.6 0.8 copy-start
  1.5 4.9 %collective-permute-start.2 = (bf16[1,16,1024]{2,1,0:T(8,128)(2,1)S(1)}, bf16[1,16,1024]{2,1,0:T(8,128)(2,1)S(1)}, u32[]{:S(2)}, u32[]{:S(2)}) collective-permute-start(bf16[1,16,1024]{2,1,0:T(8,128)(2,1)S(1)} %dynamic-slice_bitcast_fusion.15), channel_id=1, source_target_pairs={{0,1},{1,0},{2,3},{3,2},{4,5},{5,4},{6,7},{7,6},{8,9},{9,8},{10,11... | collective-permute-start | bytes 98312 | tf_op jit(solution)/shard_map/ppermute | solution.py:267
  4.5 16.2 %collective-permute-start = (bf16[512,1024]{1,0:T(8,128)(2,1)}, bf16[512,1024]{1,0:T(8,128)(2,1)S(1)}, u32[]{:S(2)}, u32[]{:S(2)}) collective-permute-start(bf16[512,1024]{1,0:T(8,128)(2,1)} %own_ref.9), channel_id=1, source_target_pairs={{0,8},{1,9},{2,10},{3,11},{4,12},{5,13},{6,14},{7,15},{8,0},{9,1},... | collective-permute-start | bytes 3145736 | tf_op jit(solution)/shard_map/ppermute | solution.py:267
  4.5 20.1 %collective-permute-start.1 = (bf16[512,1024]{1,0:T(8,128)(2,1)}, bf16[512,1024]{1,0:T(8,128)(2,1)S(1)}, u32[]{:S(2)}, u32[]{:S(2)}) collective-permute-start(bf16[512,1024]{1,0:T(8,128)(2,1)} %own_ref.7), channel_id=1, source_target_pairs={{0,8},{1,9},{2,10},{3,11},{4,12},{5,13},{6,14},{7,15},{8,0},{9,1},... | collective-permute-start | bytes 3145736 | tf_op jit(solution)/shard_map/ppermute | solution.py:267
  6.4 4.4 %collective-permute-start.3 = (bf16[2,16,1024]{2,1,0:T(8,128)(2,1)S(1)}, bf16[2,16,1024]{2,1,0:T(8,128)(2,1)S(1)}, u32[]{:S(2)}, u32[]{:S(2)}) collective-permute-start(bf16[2,16,1024]{2,1,0:T(8,128)(2,1)S(1)} %pad_maximum_fusion.3), channel_id=1, source_target_pairs={{0,2},{1,3},{2,0},{3,1},{4,6},{5,7},{6,4},{7,5},{8,10},{9,11},{10,... | collective-permute-start | bytes 196616 | tf_op jit(solution)/shard_map/ppermute | solution.py:267
  10.8 7.5 %collective-permute-start.4 = (bf16[4,16,1024]{2,1,0:T(8,128)(2,1)S(1)}, bf16[4,16,1024]{2,1,0:T(8,128)(2,1)S(1)}, u32[]{:S(2)}, u32[]{:S(2)}) collective-permute-start(bf16[4,16,1024]{2,1,0:T(8,128)(2,1)S(1)} %pad_maximum_fusion.1), channel_id=1, source_target_pairs={{0,4},{1,5},{2,6},{3,7},{4,0},{5,1},{6,2},{7,3},{8,12},{9,13},{10,... | collective-permute-start | bytes 393224 | tf_op jit(solution)/shard_map/ppermute | solution.py:267
  18.4 9.5 %collective-permute-start.5 = (bf16[8,16,1024]{2,1,0:T(8,128)(2,1)S(1)}, bf16[8,16,1024]{2,1,0:T(8,128)(2,1)S(1)}, u32[]{:S(2)}, u32[]{:S(2)}) collective-permute-start(bf16[8,16,1024]{2,1,0:T(8,128)(2,1)S(1)} %pad_maximum_fusion.mine_ref), channel_id=1, source_target_pairs={{0,8},{1,9},{2,10},{3,11},{4,12},{5,13},{6,14},{7,15},{8,0},{9,1},... | collective-permute-start | bytes 786440 | tf_op jit(solution)/shard_map/ppermute | solution.py:267
  24.6 3.3 %copy-start.2 = (bf16[512,1024]{1,0:T(8,128)(2,1)}, bf16[512,1024]{1,0:T(8,128)(2,1)S(1)}, u32[]{:S(2)}) copy-start(bf16[512,1024]{1,0:T(8,128)(2,1)S(1)} %collective-permute-done.1.partner_ref) | copy-start | bytes 3145732
  34.3 7.3 %copy-start.1 = (bf16[512,1024]{1,0:T(8,128)(2,1)S(1)}, bf16[512,1024]{1,0:T(8,128)(2,1)}, u32[]{:S(2)}) copy-start(bf16[512,1024]{1,0:T(8,128)(2,1)} %own_ref.9) | copy-start | bytes 3145732
  41.1 51.0 %collective-permute-start.6 = (bf16[512,512]{1,0:T(8,128)(2,1)S(1)}, bf16[512,512]{1,0:T(8,128)(2,1)S(1)}, u32[]{:S(2)}, u32[]{:S(2)}) collective-permute-start(bf16[512,512]{1,0:T(8,128)(2,1)S(1)} %get-tuple-element.16.qg_partner_ref), channel_id=1, source_target_pairs={{0,8},{1,9},{2,10},{3,11},{4,12},{5,13},{6,14},{7,15},{8,0},{9,1},... | collective-permute-start | bytes 1572872 | tf_op jit(solution)/shard_map/ppermute | solution.py:267
  42.5 5.7 %collective-permute-start.14 = (bf16[2,2,64,256]{3,2,1,0:T(8,128)(2,1)S(1)}, bf16[2,2,64,256]{3,2,1,0:T(8,128)(2,1)S(1)}, u32[]{:S(2)}, u32[]{:S(2)}) collective-permute-start(bf16[2,2,64,256]{3,2,1,0:T(8,128)(2,1)S(1)} %get-tuple-element.28), channel_id=1, source_target_pairs={{0,16},{1,17},{2,18},{3,19},{4,20},{5,21},{6,22},{7,23},{8,24},{9,... | collective-permute-start | bytes 393224 | tf_op jit(solution)/shard_map/ppermute | solution.py:267
  44.3 8.0 %collective-permute-start.15 = (bf16[2,2,64,256]{3,2,1,0:T(8,128)(2,1)S(1)}, bf16[2,2,64,256]{3,2,1,0:T(8,128)(2,1)S(1)}, u32[]{:S(2)}, u32[]{:S(2)}) collective-permute-start(bf16[2,2,64,256]{3,2,1,0:T(8,128)(2,1)S(1)} %get-tuple-element.29), channel_id=1, source_target_pairs={{0,1},{1,0},{2,3},{3,2},{4,5},{5,4},{6,7},{7,6},{8,9},{9,8},{10,11... | collective-permute-start | bytes 393224 | tf_op jit(solution)/shard_map/ppermute | solution.py:267
  45.8 6.4 %collective-permute-start.16 = (bf16[2,2,64,256]{3,2,1,0:T(8,128)(2,1)S(1)}, bf16[2,2,64,256]{3,2,1,0:T(8,128)(2,1)S(1)}, u32[]{:S(2)}, u32[]{:S(2)}) collective-permute-start(bf16[2,2,64,256]{3,2,1,0:T(8,128)(2,1)S(1)} %get-tuple-element.30), channel_id=1, source_target_pairs={{0,17},{1,16},{2,19},{3,18},{4,21},{5,20},{6,23},{7,22},{8,25},{9,... | collective-permute-start | bytes 393224 | tf_op jit(solution)/shard_map/ppermute | solution.py:267
  46.1 17.6 %collective-permute-start.7 = (bf16[2,64,1024]{2,1,0:T(8,128)(2,1)S(1)}, bf16[2,64,1024]{2,1,0:T(8,128)(2,1)S(1)}, u32[]{:S(2)}, u32[]{:S(2)}) collective-permute-start(bf16[2,64,1024]{2,1,0:T(8,128)(2,1)S(1)} %get-tuple-element.18), channel_id=1, source_target_pairs={{0,8},{1,9},{2,10},{3,11},{4,12},{5,13},{6,14},{7,15},{8,0},{9,1},... | collective-permute-start | bytes 786440 | tf_op jit(solution)/shard_map/ppermute | solution.py:267
  52.4 4.5 %collective-permute-start.17 = (bf16[64,256]{1,0:T(8,128)(2,1)S(1)}, bf16[64,256]{1,0:T(8,128)(2,1)S(1)}, u32[]{:S(2)}, u32[]{:S(2)}) collective-permute-start(bf16[64,256]{1,0:T(8,128)(2,1)S(1)} %get-tuple-element.47), channel_id=1, source_target_pairs={{0,2},{1,3},{2,0},{3,1},{4,6},{5,7},{6,4},{7,5},{8,10},{9,11},{10,... | collective-permute-start | bytes 98312 | tf_op jit(solution)/shard_map/ppermute | solution.py:267
  53.1 5.3 %collective-permute-start.18 = (bf16[64,256]{1,0:T(8,128)(2,1)S(1)}, bf16[64,256]{1,0:T(8,128)(2,1)S(1)}, u32[]{:S(2)}, u32[]{:S(2)}) collective-permute-start(bf16[64,256]{1,0:T(8,128)(2,1)S(1)} %get-tuple-element.49), channel_id=1, source_target_pairs={{0,4},{1,5},{2,6},{3,7},{4,0},{5,1},{6,2},{7,3},{8,12},{9,13},{10,... | collective-permute-start | bytes 98312 | tf_op jit(solution)/shard_map/ppermute | solution.py:267
  56.5 5.7 %collective-permute-start.19 = (bf16[64,256]{1,0:T(8,128)(2,1)S(1)}, bf16[64,256]{1,0:T(8,128)(2,1)S(1)}, u32[]{:S(2)}, u32[]{:S(2)}) collective-permute-start(bf16[64,256]{1,0:T(8,128)(2,1)S(1)} %get-tuple-element.48), channel_id=1, source_target_pairs={{0,6},{1,7},{2,4},{3,5},{4,2},{5,3},{6,0},{7,1},{8,14},{9,15},{10,... | collective-permute-start | bytes 98312 | tf_op jit(solution)/shard_map/ppermute | solution.py:267
  56.9 8.6 %collective-permute-start.21 = (bf16[2,2,32,1024]{3,2,1,0:T(8,128)(2,1)S(1)}, bf16[2,2,32,1024]{3,2,1,0:T(8,128)(2,1)S(1)}, u32[]{:S(2)}, u32[]{:S(2)}) collective-permute-start(bf16[2,2,32,1024]{3,2,1,0:T(8,128)(2,1)S(1)} %get-tuple-element.22), channel_id=1, source_target_pairs={{0,16},{1,17},{2,18},{3,19},{4,20},{5,21},{6,22},{7,23},{8,24},{9,... | collective-permute-start | bytes 786440 | tf_op jit(solution)/shard_map/ppermute | solution.py:267
  58.4 17.4 %collective-permute-start.22 = (bf16[2,2,32,1024]{3,2,1,0:T(8,128)(2,1)S(1)}, bf16[2,2,32,1024]{3,2,1,0:T(8,128)(2,1)S(1)}, u32[]{:S(2)}, u32[]{:S(2)}) collective-permute-start(bf16[2,2,32,1024]{3,2,1,0:T(8,128)(2,1)S(1)} %get-tuple-element.24), channel_id=1, source_target_pairs={{0,1},{1,0},{2,3},{3,2},{4,5},{5,4},{6,7},{7,6},{8,9},{9,8},{10,11... | collective-permute-start | bytes 786440 | tf_op jit(solution)/shard_map/ppermute | solution.py:267
  62.2 16.1 %collective-permute-start.23 = (bf16[2,2,32,1024]{3,2,1,0:T(8,128)(2,1)S(1)}, bf16[2,2,32,1024]{3,2,1,0:T(8,128)(2,1)S(1)}, u32[]{:S(2)}, u32[]{:S(2)}) collective-permute-start(bf16[2,2,32,1024]{3,2,1,0:T(8,128)(2,1)S(1)} %get-tuple-element.23), channel_id=1, source_target_pairs={{0,17},{1,16},{2,19},{3,18},{4,21},{5,20},{6,23},{7,22},{8,25},{9,... | collective-permute-start | bytes 786440 | tf_op jit(solution)/shard_map/ppermute | solution.py:267
  63.9 14.6 %collective-permute-start.10 = (bf16[2,2,96,256]{3,2,1,0:T(8,128)(2,1)S(1)}, bf16[2,2,96,256]{3,2,1,0:T(8,128)(2,1)S(1)}, u32[]{:S(2)}, u32[]{:S(2)}) collective-permute-start(bf16[2,2,96,256]{3,2,1,0:T(8,128)(2,1)S(1)} %get-tuple-element.26), channel_id=1, source_target_pairs={{0,17},{1,16},{2,19},{3,18},{4,21},{5,20},{6,23},{7,22},{8,25},{9,... | collective-permute-start | bytes 589832 | tf_op jit(solution)/shard_map/ppermute | solution.py:267
  65.4 14.4 %collective-permute-start.8 = (bf16[2,2,96,256]{3,2,1,0:T(8,128)(2,1)S(1)}, bf16[2,2,96,256]{3,2,1,0:T(8,128)(2,1)S(1)}, u32[]{:S(2)}, u32[]{:S(2)}) collective-permute-start(bf16[2,2,96,256]{3,2,1,0:T(8,128)(2,1)S(1)} %get-tuple-element.25), channel_id=1, source_target_pairs={{0,16},{1,17},{2,18},{3,19},{4,20},{5,21},{6,22},{7,23},{8,24},{9,... | collective-permute-start | bytes 589832 | tf_op jit(solution)/shard_map/ppermute | solution.py:267
  75.8 7.2 %collective-permute-start.9 = (bf16[2,2,96,256]{3,2,1,0:T(8,128)(2,1)S(1)}, bf16[2,2,96,256]{3,2,1,0:T(8,128)(2,1)S(1)}, u32[]{:S(2)}, u32[]{:S(2)}) collective-permute-start(bf16[2,2,96,256]{3,2,1,0:T(8,128)(2,1)S(1)} %get-tuple-element.27), channel_id=1, source_target_pairs={{0,1},{1,0},{2,3},{3,2},{4,5},{5,4},{6,7},{7,6},{8,9},{9,8},{10,11... | collective-permute-start | bytes 589832 | tf_op jit(solution)/shard_map/ppermute | solution.py:267
  78.5 4.7 %collective-permute-start.24 = (bf16[32,1024]{1,0:T(8,128)(2,1)S(1)}, bf16[32,1024]{1,0:T(8,128)(2,1)S(1)}, u32[]{:S(2)}, u32[]{:S(2)}) collective-permute-start(bf16[32,1024]{1,0:T(8,128)(2,1)S(1)} %get-tuple-element.35), channel_id=1, source_target_pairs={{0,2},{1,3},{2,0},{3,1},{4,6},{5,7},{6,4},{7,5},{8,10},{9,11},{10,... | collective-permute-start | bytes 196616 | tf_op jit(solution)/shard_map/ppermute | solution.py:267
  78.6 6.8 %collective-permute-start.25 = (bf16[32,1024]{1,0:T(8,128)(2,1)S(1)}, bf16[32,1024]{1,0:T(8,128)(2,1)S(1)}, u32[]{:S(2)}, u32[]{:S(2)}) collective-permute-start(bf16[32,1024]{1,0:T(8,128)(2,1)S(1)} %get-tuple-element.37), channel_id=1, source_target_pairs={{0,4},{1,5},{2,6},{3,7},{4,0},{5,1},{6,2},{7,3},{8,12},{9,13},{10,... | collective-permute-start | bytes 196616 | tf_op jit(solution)/shard_map/ppermute | solution.py:267
  79.9 7.7 %collective-permute-start.26 = (bf16[32,1024]{1,0:T(8,128)(2,1)S(1)}, bf16[32,1024]{1,0:T(8,128)(2,1)S(1)}, u32[]{:S(2)}, u32[]{:S(2)}) collective-permute-start(bf16[32,1024]{1,0:T(8,128)(2,1)S(1)} %get-tuple-element.36), channel_id=1, source_target_pairs={{0,6},{1,7},{2,4},{3,5},{4,2},{5,3},{6,0},{7,1},{8,14},{9,15},{10,... | collective-permute-start | bytes 196616 | tf_op jit(solution)/shard_map/ppermute | solution.py:267
  83.1 5.2 %collective-permute-start.11 = (bf16[96,256]{1,0:T(8,128)(2,1)S(1)}, bf16[96,256]{1,0:T(8,128)(2,1)S(1)}, u32[]{:S(2)}, u32[]{:S(2)}) collective-permute-start(bf16[96,256]{1,0:T(8,128)(2,1)S(1)} %get-tuple-element.38), channel_id=1, source_target_pairs={{0,2},{1,3},{2,0},{3,1},{4,6},{5,7},{6,4},{7,5},{8,10},{9,11},{10,... | collective-permute-start | bytes 147464 | tf_op jit(solution)/shard_map/ppermute | solution.py:267
  83.2 5.1 %collective-permute-start.12 = (bf16[96,256]{1,0:T(8,128)(2,1)S(1)}, bf16[96,256]{1,0:T(8,128)(2,1)S(1)}, u32[]{:S(2)}, u32[]{:S(2)}) collective-permute-start(bf16[96,256]{1,0:T(8,128)(2,1)S(1)} %get-tuple-element.40), channel_id=1, source_target_pairs={{0,4},{1,5},{2,6},{3,7},{4,0},{5,1},{6,2},{7,3},{8,12},{9,13},{10,... | collective-permute-start | bytes 147464 | tf_op jit(solution)/shard_map/ppermute | solution.py:267
  85.4 5.9 %collective-permute-start.13 = (bf16[96,256]{1,0:T(8,128)(2,1)S(1)}, bf16[96,256]{1,0:T(8,128)(2,1)S(1)}, u32[]{:S(2)}, u32[]{:S(2)}) collective-permute-start(bf16[96,256]{1,0:T(8,128)(2,1)S(1)} %get-tuple-element.39), channel_id=1, source_target_pairs={{0,6},{1,7},{2,4},{3,5},{4,2},{5,3},{6,0},{7,1},{8,14},{9,15},{10,... | collective-permute-start | bytes 147464 | tf_op jit(solution)/shard_map/ppermute | solution.py:267
  91.4 4.9 %collective-permute-start.20 = (f32[2,32,256]{2,1,0:T(8,128)S(1)}, f32[2,32,256]{2,1,0:T(8,128)S(1)}, u32[]{:S(2)}, u32[]{:S(2)}) collective-permute-start(f32[2,32,256]{2,1,0:T(8,128)S(1)} %get-tuple-element.45), channel_id=1, source_target_pairs={{0,8},{1,9},{2,10},{3,11},{4,12},{5,13},{6,14},{7,15},{8,0},{9,1},... | collective-permute-start | bytes 196616 | tf_op jit(solution)/shard_map/ppermute | solution.py:267

commit v7 on v6

--- a/solution.py
+++ b/solution.py
@@ -224,21 +224,15 @@
     out_ref[...] = total.astype(BF16).T
 
 
-def targets_kernel(block, place_ref, mine_ref, theirs_ref, weight_ref, out_ref, weights, sems):
+def targets_kernel(block, place_ref, mine_ref, theirs_ref, weight_ref, out_ref):
     other_ref = [1 - place_ref[0]]
-    copies, sources = [], []
+    total = None
     for at in range(0, mine_ref.shape[0], block):
+        part = pl.ds(at, block)
         for source, core in ((mine_ref, place_ref), (theirs_ref, other_ref)):
-            index = len(copies)
-            columns = weight_ref.at[:, owned(core, at, block, block)]
-            copies.append(pltpu.make_async_copy(columns, weights.at[index], sems.at[index]))
-            copies[-1].start()
-            sources.append(source[pl.ds(at, block), :])
-    total = None
-    for index, source in enumerate(sources):
-        copies[index].wait()
-        term = dot(source.T, weights[index], ((1,), (1,)))
-        total = term if total is None else total + term
+            weight = weight_ref[:, owned(core, at, block, block)]
+            term = dot(source[part, :].T, weight, ((1,), (1,)))
+            total = term if total is None else total + term
     out_ref[...] = total.astype(BF16)
 
 
@@ -381,7 +375,7 @@
     high_bits = [2] * len(high_masks)
     seq_bits = [2] * len(seq_masks)
     order = [high_masks[-1], seq_masks[-1]] + seq_masks[-2::-1] + high_masks[:-1]
-    stages = [tuple(order[at : at + 2]) for at in range(0, len(order), 2)]
+    stages = [tuple(order[:2])]
 
     def exchange(array, masks, stage, last=False):
         def piece(flips):
@@ -403,10 +397,16 @@
         left = [mask for mask in masks if mask not in stage]
         return total, left
 
-    def exchange_rest(array, masks):
-        for at, stage in enumerate(stages[1:]):
-            array, masks = exchange(array, masks, stage, at == len(stages) - 2)
+    def exchange_rest(array, masks, steps):
+        for at, stage in enumerate(steps):
+            array, masks = exchange(array, masks, stage, at == len(steps) - 1)
         return array
+
+    def paired(masks):
+        return [tuple(masks[at : at + 2]) for at in range(0, len(masks), 2)]
+
+    late_steps = paired(order[2:])
+    early_steps = [tuple(order[3:4])] + paired(order[4:])
 
     out_rows = width // device_count
     ctx_out = context_rows // device_count
@@ -447,14 +447,21 @@
             ctx_pair = (ctx_kept + ctx_moved.astype(F32)).astype(BF16)
             pieces += stacked(ctx_pair.reshape(*high_bits, *seq_bits, ctx_out, width))
         moved, _ = exchange(jnp.concatenate(pieces, axis=-2), all_masks, stages[0])
-        parts.append(exchange_rest(moved, left_masks))
+        if part == 0:
+            moved, early_masks = exchange(moved, left_masks, order[2:3])
+            wo_half, _ = exchange(wo_part, left_masks, order[2:3])
+            moved = jnp.concatenate([moved] + stacked(wo_half), axis=-2)
+            parts.append(exchange_rest(moved, early_masks, early_steps))
+        else:
+            parts.append(exchange_rest(moved, left_masks, late_steps))
 
     first = parts[0]
     edges = [2 * out_rows, 2 * out_rows + grp_count * ctx_out]
     wq_sums = jnp.stack([one[: edges[0]].reshape(2, out_rows, block) for one in parts])
     ctx_sums = first[edges[0] : edges[1]].reshape(grp_count, ctx_out, block)
     d_context = jnp.concatenate(list(ctx_sums), axis=1).astype(BF16)
-    grad_wo = exchange_rest(wo_part, left_masks)
+    wo_sums = first[edges[1] :].reshape(grp_count, out_rows, block)
+    grad_wo = jnp.concatenate(list(wo_sums), axis=1)
     sent = lax.dynamic_index_in_dim(wq_sums, 1 - core, 1, keepdims=False)
     mine = lax.dynamic_index_in_dim(wq_sums, core, 1, keepdims=False)
     theirs = swap(sent, core_mask)
@@ -470,8 +477,6 @@
         [place, query_own, returned, w_query],
         [((query_rows, width), BF16)],
         product,
-        [pltpu.VMEM((grp_count, width, block), BF16), pltpu.SemaphoreType.DMA((grp_count,))],
-        (3,),
     )
     return (d_targets, d_context, grad_wq, grad_wo)
 

time: 97.3 us -> 99.1 us (1.018)
  waiting for transfers between devices: 26.2 us -> 37.1 us
  starting transfers between devices: 36.5 us -> 28.6 us
  Pallas kernels: 28.3 us -> 27 us
    ppermute x27 -> x24, waiting for transfers between devices: 26.2 us -> 37.1 us  [swap(): lax.ppermute(array, AXES, [(i, i ^ mask) for i in range(device_count)])]
    ppermute x27 -> x24, starting transfers between devices: 36.5 us -> 28.6 us  [swap(): lax.ppermute(array, AXES, [(i, i ^ mask) for i in range(device_count)])]
    pallas_call x8, Pallas kernels: 28.3 us -> 27 us  [call(): pl.pallas_call(kernel, in_specs=specs, out_specs=[in_vmem] * len(outs), o...]
  transfers between devices with their start and end apart: 27 -> 24, of which waited for: 9 -> 10; matrix products, arithmetic and copies ran while one was open for 3% -> 3% of each run, Pallas kernels for 16% -> 21%
where the time goes in v7:
time: 99.1 us; the launch traced here: 98.8 us
  waiting for transfers between devices  37.1 us (37%)
  starting transfers between devices  28.6 us (29%)
  Pallas kernels  27 us (27%)
  other arithmetic  3.71 us (4%)
  local copies, waits for them, and re-layouts  1.34 us (1%)
  between operations  1.13 us (1%)
    ppermute x24, waiting for transfers between devices, swap(): lax.ppermute(array, AXES, [(i, i ^ mask) for i in range(device_count)])  37.1 us
    ppermute x24, starting transfers between devices, swap(): lax.ppermute(array, AXES, [(i, i ^ mask) for i in range(device_count)])  28.6 us
    pallas_call x8, Pallas kernels, call(): pl.pallas_call(kernel, in_specs=specs, out_specs=[in_vmem] * len(outs), o...  27 us
  transfers between devices with their start and end apart: 24, of which 10 were waited for; matrix products, arithmetic and copies ran while one was open for 3% of the time, Pallas kernels for 21%

profile of v7, /device:TPU:0, one launch (start us, length us, event | category | flops | bytes accessed | tf_op | source)
XLA Modules:
  0.0 98.8 jit_solution(9725444771158022765)
XLA Ops:
  0.7 0.8 copy-done
  1.5 3.0 %collective-permute-start.2 = (bf16[1,16,1024]{2,1,0:T(8,128)(2,1)S(1)}, bf16[1,16,1024]{2,1,0:T(8,128)(2,1)S(1)}, u32[]{:S(2)}, u32[]{:S(2)}) collective-permute-start(bf16[1,16,1024]{2,1,0:T(8,128)(2,1)S(1)} %dynamic-slice_bitcast_fusion.9), channel_id=1, source_target_pairs={{0,1},{1,0},{2,3},{3,2},{4,5},{5,4},{6,7},{7,6},{8,9},{9,8},{10,11... | collective-permute-start | bytes 98312 | tf_op jit(solution)/shard_map/ppermute | solution.py:261
  5.2 0.8 select_reduce_fusion.1
  6.4 2.1 %collective-permute-start.3 = (bf16[2,16,1024]{2,1,0:T(8,128)(2,1)S(1)}, bf16[2,16,1024]{2,1,0:T(8,128)(2,1)S(1)}, u32[]{:S(2)}, u32[]{:S(2)}) collective-permute-start(bf16[2,16,1024]{2,1,0:T(8,128)(2,1)S(1)} %pad_maximum_fusion.4), channel_id=1, source_target_pairs={{0,2},{1,3},{2,0},{3,1},{4,6},{5,7},{6,4},{7,5},{8,10},{9,11},{10,... | collective-permute-start | bytes 196616 | tf_op jit(solution)/shard_map/ppermute | solution.py:261
  8.6 2.2 %collective-permute-done.3 = bf16[2,16,1024]{2,1,0:T(8,128)(2,1)S(1)} collective-permute-done((bf16[2,16,1024]{2,1,0:T(8,128)(2,1)S(1)}, bf16[2,16,1024]{2,1,0:T(8,128)(2,1)S(1)}, u32[]{:S(2)}, u32[]{:S(2)}) %collective-permute-start.3) | collective-permute-done | bytes 65568 | tf_op jit(solution)/shard_map/ppermute | solution.py:261
  10.8 3.1 %collective-permute-start.4 = (bf16[4,16,1024]{2,1,0:T(8,128)(2,1)S(1)}, bf16[4,16,1024]{2,1,0:T(8,128)(2,1)S(1)}, u32[]{:S(2)}, u32[]{:S(2)}) collective-permute-start(bf16[4,16,1024]{2,1,0:T(8,128)(2,1)S(1)} %pad_maximum_fusion.1), channel_id=1, source_target_pairs={{0,4},{1,5},{2,6},{3,7},{4,0},{5,1},{6,2},{7,3},{8,12},{9,13},{10,... | collective-permute-start | bytes 393224 | tf_op jit(solution)/shard_map/ppermute | solution.py:261
  14.0 4.3 %collective-permute-done.4 = bf16[4,16,1024]{2,1,0:T(8,128)(2,1)S(1)} collective-permute-done((bf16[4,16,1024]{2,1,0:T(8,128)(2,1)S(1)}, bf16[4,16,1024]{2,1,0:T(8,128)(2,1)S(1)}, u32[]{:S(2)}, u32[]{:S(2)}) %collective-permute-start.4) | collective-permute-done | bytes 131104 | tf_op jit(solution)/shard_map/ppermute | solution.py:261
  18.4 2.2 %shard_map.111.wkv_ref = bf16[4,1024,256]{2,1,0:T(8,128)(2,1)S(1)} custom-call(s32[2]{0:T(128)S(1)} %pad_add_fusion.place_ref, bf16[1024,1024]{1,0:T(8,128)(2,1)} %wk_ref.1, bf16[1024,1024]{1,0:T(8,128)(2,1)} %wv_ref.1), custom_call_target="tpu_custom_call" | custom-call | flops 1073741824 | bytes 1048576 | tf_op jit(solution)/shard_map/pallas_call | solution.py:275
  20.6 3.9 %shard_map.112.q_ref = bf16[512,1024]{1,0:T(8,128)(2,1)S(1)} custom-call(s32[2]{0:T(128)S(1)} %pad_add_fusion.place_ref, bf16[1024,1024]{1,0:T(8,128)(2,1)} %weight_ref.5, bf16[512,1024]{1,0:T(8,128)(2,1)} %own_ref.9, bf16[512,1024]{1,0:T(8,128)(2,1)S(1)} %collective-permute-done.partner_ref), custom_call_target="tpu_custom_call" | custom-call | flops 1073741824 | bytes 1048576 | tf_op jit(solution)/shard_map/pallas_call | solution.py:275
  24.6 3.3 %shard_map.113.g_ref = bf16[512,1024]{1,0:T(8,128)(2,1)S(1)} custom-call(s32[2]{0:T(128)S(1)} %pad_add_fusion.place_ref, bf16[1024,1024]{1,0:T(8,128)(2,1)} %weight_ref.4, bf16[512,1024]{1,0:T(8,128)(2,1)} %own_ref.7, bf16[512,1024]{1,0:T(8,128)(2,1)S(1)} %collective-permute-done.1.partner_ref), custom_call_target="tpu_custom_call" | custom-call | flops 1073741824 | bytes 1048576 | tf_op jit(solution)/shard_map/pallas_call | solution.py:275
  27.9 6.4 %shard_map.114 = (bf16[2,512,256]{2,1,0:T(8,128)(2,1)S(1)}, bf16[8,256,1024]{2,1,0:T(8,128)(2,1)S(1)}, f32[8,1024]{1,0:T(8,128)S(1)}, bf16[512,1024]{1,0:T(8,128)(2,1)S(1)}) custom-call(s32[2]{0:T(128)S(1)} %pad_add_fusion.place_ref, bf16[8,16,1024]{2,1,0:T(8,128)(2,1)S(1)} %pad_maximum_fusion.mine_ref, ...), custom_call_target="tpu_custom_call" | custom-call | flops 2147483648 | bytes 1048576 | tf_op jit(solution)/shard_map/pallas_call | solution.py:275
  34.5 1.8 %collective-permute-start.12 = (bf16[2,2,32,1024]{3,2,0,1:T(8,128)(2,1)S(1)}, bf16[2,2,32,1024]{3,2,0,1:T(8,128)(2,1)S(1)}, u32[]{:S(2)}, u32[]{:S(2)}) collective-permute-start(bf16[2,2,32,1024]{3,2,0,1:T(8,128)(2,1)S(1)} %bitcast.126), channel_id=1, source_target_pairs={{0,16},{1,17},{2,18},{3,19},{4,20},{5,21},{6,22},{7,23},{8,24},{9,... | collective-permute-start | bytes 786440 | tf_op jit(solution)/shard_map/ppermute | solution.py:261
  36.3 6.8 %shard_map.115 = (bf16[512,512]{1,0:T(8,128)(2,1)S(1)}, bf16[512,512]{1,0:T(8,128)(2,1)S(1)}, f32[2,64,1024]{2,1,0:T(8,128)S(1)}, bf16[2,64,1024]{2,1,0:T(8,128)(2,1)S(1)}) custom-call(s32[2]{0:T(128)S(1)} %pad_add_fusion.place_ref, bf16[4,1024,256]{2,1,0:T(8,128)(2,1)S(1)} %shard_map.111.wkv_ref, bf16[512,1024]{1,0:T(8,128)(2,1)S(1)} %shard_map.112.q_ref, ...), custom_call_target="tpu_custom_call" | custom-call | flops 1610612736 | bytes 1048576 | tf_op jit(solution)/shard_map/pallas_call | solution.py:275
  43.3 0.8 shard_map.117
  44.2 0.8 shard_map.118
  45.4 1.7 %collective-permute-start.18 = (bf16[2,2,64,256]{3,2,1,0:T(8,128)(2,1)S(1)}, bf16[2,2,64,256]{3,2,1,0:T(8,128)(2,1)S(1)}, u32[]{:S(2)}, u32[]{:S(2)}) collective-permute-start(bf16[2,2,64,256]{3,2,1,0:T(8,128)(2,1)S(1)} %get-tuple-element.30), channel_id=1, source_target_pairs={{0,1},{1,0},{2,3},{3,2},{4,5},{5,4},{6,7},{7,6},{8,9},{9,8},{10,11... | collective-permute-start | bytes 393224 | tf_op jit(solution)/shard_map/ppermute | solution.py:261
  47.2 1.4 %collective-permute-start.19 = (bf16[2,2,64,256]{3,2,1,0:T(8,128)(2,1)S(1)}, bf16[2,2,64,256]{3,2,1,0:T(8,128)(2,1)S(1)}, u32[]{:S(2)}, u32[]{:S(2)}) collective-permute-start(bf16[2,2,64,256]{3,2,1,0:T(8,128)(2,1)S(1)} %get-tuple-element.31), channel_id=1, source_target_pairs={{0,17},{1,16},{2,19},{3,18},{4,21},{5,20},{6,23},{7,22},{8,25},{9,... | collective-permute-start | bytes 393224 | tf_op jit(solution)/shard_map/ppermute | solution.py:261
  48.7 2.8 %collective-permute-done.17 = bf16[2,2,64,256]{3,2,1,0:T(8,128)(2,1)S(1)} collective-permute-done((bf16[2,2,64,256]{3,2,1,0:T(8,128)(2,1)S(1)}, bf16[2,2,64,256]{3,2,1,0:T(8,128)(2,1)S(1)}, u32[]{:S(2)}, u32[]{:S(2)}) %collective-permute-start.17) | collective-permute-done | bytes 131104 | tf_op jit(solution)/shard_map/ppermute | solution.py:261
  51.5 1.5 %collective-permute-start.13 = (bf16[2,2,32,1024]{3,2,0,1:T(8,128)(2,1)S(1)}, bf16[2,2,32,1024]{3,2,0,1:T(8,128)(2,1)S(1)}, u32[]{:S(2)}, u32[]{:S(2)}) collective-permute-start(bf16[2,2,32,1024]{3,2,0,1:T(8,128)(2,1)S(1)} %bitcast.128), channel_id=1, source_target_pairs={{0,1},{1,0},{2,3},{3,2},{4,5},{5,4},{6,7},{7,6},{8,9},{9,8},{10,11... | collective-permute-start | bytes 786440 | tf_op jit(solution)/shard_map/ppermute | solution.py:261
  53.0 4.3 %collective-permute-start.14 = (bf16[2,2,32,1024]{3,2,0,1:T(8,128)(2,1)S(1)}, bf16[2,2,32,1024]{3,2,0,1:T(8,128)(2,1)S(1)}, u32[]{:S(2)}, u32[]{:S(2)}) collective-permute-start(bf16[2,2,32,1024]{3,2,0,1:T(8,128)(2,1)S(1)} %bitcast.127), channel_id=1, source_target_pairs={{0,17},{1,16},{2,19},{3,18},{4,21},{5,20},{6,23},{7,22},{8,25},{9,... | collective-permute-start | bytes 786440 | tf_op jit(solution)/shard_map/ppermute | solution.py:261
  57.4 1.4 %collective-permute-done.7 = bf16[2,64,1024]{2,1,0:T(8,128)(2,1)S(1)} collective-permute-done((bf16[2,64,1024]{2,1,0:T(8,128)(2,1)S(1)}, bf16[2,64,1024]{2,1,0:T(8,128)(2,1)S(1)}, u32[]{:S(2)}, u32[]{:S(2)}) %collective-permute-start.7) | collective-permute-done | bytes 262176 | tf_op jit(solution)/shard_map/ppermute | solution.py:261
  58.8 0.7 collective-permute-start.20
  59.8 10.2 %collective-permute-done.13 = bf16[2,2,32,1024]{3,2,0,1:T(8,128)(2,1)S(1)} collective-permute-done((bf16[2,2,32,1024]{3,2,0,1:T(8,128)(2,1)S(1)}, bf16[2,2,32,1024]{3,2,0,1:T(8,128)(2,1)S(1)}, u32[]{:S(2)}, u32[]{:S(2)}) %collective-permute-start.13) | collective-permute-done | bytes 262176 | tf_op jit(solution)/shard_map/ppermute | solution.py:261
  70.0 0.8 collective-permute-start.8
  70.8 1.5 %collective-permute-start.9 = (bf16[2,2,96,256]{3,2,1,0:T(8,128)(2,1)S(1)}, bf16[2,2,96,256]{3,2,1,0:T(8,128)(2,1)S(1)}, u32[]{:S(2)}, u32[]{:S(2)}) collective-permute-start(bf16[2,2,96,256]{3,2,1,0:T(8,128)(2,1)S(1)} %get-tuple-element.28), channel_id=1, source_target_pairs={{0,1},{1,0},{2,3},{3,2},{4,5},{5,4},{6,7},{7,6},{8,9},{9,8},{10,11... | collective-permute-start | bytes 589832 | tf_op jit(solution)/shard_map/ppermute | solution.py:261
  72.6 1.3 %collective-permute-start.21 = (bf16[64,256]{1,0:T(8,128)(2,1)S(1)}, bf16[64,256]{1,0:T(8,128)(2,1)S(1)}, u32[]{:S(2)}, u32[]{:S(2)}) collective-permute-start(bf16[64,256]{1,0:T(8,128)(2,1)S(1)} %get-tuple-element.48), channel_id=1, source_target_pairs={{0,4},{1,5},{2,6},{3,7},{4,0},{5,1},{6,2},{7,3},{8,12},{9,13},{10,... | collective-permute-start | bytes 98312 | tf_op jit(solution)/shard_map/ppermute | solution.py:261
  73.9 2.6 %collective-permute-done.8 = bf16[2,2,96,256]{3,2,1,0:T(8,128)(2,1)S(1)} collective-permute-done((bf16[2,2,96,256]{3,2,1,0:T(8,128)(2,1)S(1)}, bf16[2,2,96,256]{3,2,1,0:T(8,128)(2,1)S(1)}, u32[]{:S(2)}, u32[]{:S(2)}) %collective-permute-start.8) | collective-permute-done | bytes 196640 | tf_op jit(solution)/shard_map/ppermute | solution.py:261
  76.5 3.5 %collective-permute-start.22 = (bf16[64,256]{1,0:T(8,128)(2,1)S(1)}, bf16[64,256]{1,0:T(8,128)(2,1)S(1)}, u32[]{:S(2)}, u32[]{:S(2)}) collective-permute-start(bf16[64,256]{1,0:T(8,128)(2,1)S(1)} %get-tuple-element.47), channel_id=1, source_target_pairs={{0,6},{1,7},{2,4},{3,5},{4,2},{5,3},{6,0},{7,1},{8,14},{9,15},{10,... | collective-permute-start | bytes 98312 | tf_op jit(solution)/shard_map/ppermute | solution.py:261
  80.1 4.8 %collective-permute-done.15 = bf16[2,32,1024]{2,1,0:T(8,128)(2,1)S(1)} collective-permute-done((bf16[2,32,1024]{2,1,0:T(8,128)(2,1)S(1)}, bf16[2,32,1024]{2,1,0:T(8,128)(2,1)S(1)}, u32[]{:S(2)}, u32[]{:S(2)}) %collective-permute-start.15) | collective-permute-done | bytes 131104 | tf_op jit(solution)/shard_map/ppermute | solution.py:261
  85.3 4.2 %collective-permute-done.11 = bf16[2,96,256]{2,1,0:T(8,128)(2,1)S(1)} collective-permute-done((bf16[2,96,256]{2,1,0:T(8,128)(2,1)S(1)}, bf16[2,96,256]{2,1,0:T(8,128)(2,1)S(1)}, u32[]{:S(2)}, u32[]{:S(2)}) %collective-permute-start.11) | collective-permute-done | bytes 98336 | tf_op jit(solution)/shard_map/ppermute | solution.py:261
  89.8 2.8 %shard_map.116 = bf16[512,1024]{1,0:T(8,128)(2,1)} custom-call(s32[2]{0:T(128)S(1)} %pad_add_fusion.place_ref, bf16[512,512]{1,0:T(8,128)(2,1)S(1)} %get-tuple-element.15.mine_ref.qg_own_ref, bf16[512,512]{1,0:T(8,128)(2,1)S(1)} %collective-permute-done.6.theirs_ref, bf16[1024,1024]{1,0:T(8,128)(2,1)S(1)} %copy-done.2), custom_call_target="tpu_custom_call" | custom-call | flops 1073741824 | bytes 1048576 | tf_op jit(solution)/shard_map/pallas_call | solution.py:275
  92.6 4.0 %collective-permute-done.16 = bf16[224,256]{1,0:T(8,128)(2,1)S(1)} collective-permute-done((bf16[224,256]{1,0:T(8,128)(2,1)S(1)}, bf16[224,256]{1,0:T(8,128)(2,1)S(1)}, u32[]{:S(2)}, u32[]{:S(2)}) %collective-permute-start.16) | collective-permute-done | bytes 114720 | tf_op jit(solution)/shard_map/ppermute | solution.py:261
  (83 shorter events, 5.7 us)
Async XLA Ops:
  0.6 0.8 copy-start
  1.5 4.9 %collective-permute-start.2 = (bf16[1,16,1024]{2,1,0:T(8,128)(2,1)S(1)}, bf16[1,16,1024]{2,1,0:T(8,128)(2,1)S(1)}, u32[]{:S(2)}, u32[]{:S(2)}) collective-permute-start(bf16[1,16,1024]{2,1,0:T(8,128)(2,1)S(1)} %dynamic-slice_bitcast_fusion.9), channel_id=1, source_target_pairs={{0,1},{1,0},{2,3},{3,2},{4,5},{5,4},{6,7},{7,6},{8,9},{9,8},{10,11... | collective-permute-start | bytes 98312 | tf_op jit(solution)/shard_map/ppermute | solution.py:261
  4.5 16.2 %collective-permute-start = (bf16[512,1024]{1,0:T(8,128)(2,1)}, bf16[512,1024]{1,0:T(8,128)(2,1)S(1)}, u32[]{:S(2)}, u32[]{:S(2)}) collective-permute-start(bf16[512,1024]{1,0:T(8,128)(2,1)} %own_ref.9), channel_id=1, source_target_pairs={{0,8},{1,9},{2,10},{3,11},{4,12},{5,13},{6,14},{7,15},{8,0},{9,1},... | collective-permute-start | bytes 3145736 | tf_op jit(solution)/shard_map/ppermute | solution.py:261
  4.5 20.1 %collective-permute-start.1 = (bf16[512,1024]{1,0:T(8,128)(2,1)}, bf16[512,1024]{1,0:T(8,128)(2,1)S(1)}, u32[]{:S(2)}, u32[]{:S(2)}) collective-permute-start(bf16[512,1024]{1,0:T(8,128)(2,1)} %own_ref.7), channel_id=1, source_target_pairs={{0,8},{1,9},{2,10},{3,11},{4,12},{5,13},{6,14},{7,15},{8,0},{9,1},... | collective-permute-start | bytes 3145736 | tf_op jit(solution)/shard_map/ppermute | solution.py:261
  6.4 4.4 %collective-permute-start.3 = (bf16[2,16,1024]{2,1,0:T(8,128)(2,1)S(1)}, bf16[2,16,1024]{2,1,0:T(8,128)(2,1)S(1)}, u32[]{:S(2)}, u32[]{:S(2)}) collective-permute-start(bf16[2,16,1024]{2,1,0:T(8,128)(2,1)S(1)} %pad_maximum_fusion.4), channel_id=1, source_target_pairs={{0,2},{1,3},{2,0},{3,1},{4,6},{5,7},{6,4},{7,5},{8,10},{9,11},{10,... | collective-permute-start | bytes 196616 | tf_op jit(solution)/shard_map/ppermute | solution.py:261
  10.8 7.5 %collective-permute-start.4 = (bf16[4,16,1024]{2,1,0:T(8,128)(2,1)S(1)}, bf16[4,16,1024]{2,1,0:T(8,128)(2,1)S(1)}, u32[]{:S(2)}, u32[]{:S(2)}) collective-permute-start(bf16[4,16,1024]{2,1,0:T(8,128)(2,1)S(1)} %pad_maximum_fusion.1), channel_id=1, source_target_pairs={{0,4},{1,5},{2,6},{3,7},{4,0},{5,1},{6,2},{7,3},{8,12},{9,13},{10,... | collective-permute-start | bytes 393224 | tf_op jit(solution)/shard_map/ppermute | solution.py:261
  18.4 9.5 %collective-permute-start.5 = (bf16[8,16,1024]{2,1,0:T(8,128)(2,1)S(1)}, bf16[8,16,1024]{2,1,0:T(8,128)(2,1)S(1)}, u32[]{:S(2)}, u32[]{:S(2)}) collective-permute-start(bf16[8,16,1024]{2,1,0:T(8,128)(2,1)S(1)} %pad_maximum_fusion.mine_ref), channel_id=1, source_target_pairs={{0,8},{1,9},{2,10},{3,11},{4,12},{5,13},{6,14},{7,15},{8,0},{9,1},... | collective-permute-start | bytes 786440 | tf_op jit(solution)/shard_map/ppermute | solution.py:261
  24.6 3.3 %copy-start.3 = (bf16[512,1024]{1,0:T(8,128)(2,1)}, bf16[512,1024]{1,0:T(8,128)(2,1)S(1)}, u32[]{:S(2)}) copy-start(bf16[512,1024]{1,0:T(8,128)(2,1)S(1)} %collective-permute-done.1.partner_ref) | copy-start | bytes 3145732
  34.5 25.2 %collective-permute-start.12 = (bf16[2,2,32,1024]{3,2,0,1:T(8,128)(2,1)S(1)}, bf16[2,2,32,1024]{3,2,0,1:T(8,128)(2,1)S(1)}, u32[]{:S(2)}, u32[]{:S(2)}) collective-permute-start(bf16[2,2,32,1024]{3,2,0,1:T(8,128)(2,1)S(1)} %bitcast.126), channel_id=1, source_target_pairs={{0,16},{1,17},{2,18},{3,19},{4,20},{5,21},{6,22},{7,23},{8,24},{9,... | collective-permute-start | bytes 786440 | tf_op jit(solution)/shard_map/ppermute | solution.py:261
  36.3 7.0 %copy-start.1 = (bf16[512,1024]{1,0:T(8,128)(2,1)S(1)}, bf16[512,1024]{1,0:T(8,128)(2,1)}, u32[]{:S(2)}) copy-start(bf16[512,1024]{1,0:T(8,128)(2,1)} %own_ref.9) | copy-start | bytes 3145732
  43.0 46.8 %collective-permute-start.6 = (bf16[512,512]{1,0:T(8,128)(2,1)S(1)}, bf16[512,512]{1,0:T(8,128)(2,1)S(1)}, u32[]{:S(2)}, u32[]{:S(2)}) collective-permute-start(bf16[512,512]{1,0:T(8,128)(2,1)S(1)} %get-tuple-element.16.qg_partner_ref), channel_id=1, source_target_pairs={{0,8},{1,9},{2,10},{3,11},{4,12},{5,13},{6,14},{7,15},{8,0},{9,1},... | collective-permute-start | bytes 1572872 | tf_op jit(solution)/shard_map/ppermute | solution.py:261
  45.1 6.4 %collective-permute-start.17 = (bf16[2,2,64,256]{3,2,1,0:T(8,128)(2,1)S(1)}, bf16[2,2,64,256]{3,2,1,0:T(8,128)(2,1)S(1)}, u32[]{:S(2)}, u32[]{:S(2)}) collective-permute-start(bf16[2,2,64,256]{3,2,1,0:T(8,128)(2,1)S(1)} %get-tuple-element.29), channel_id=1, source_target_pairs={{0,16},{1,17},{2,18},{3,19},{4,20},{5,21},{6,22},{7,23},{8,24},{9,... | collective-permute-start | bytes 393224 | tf_op jit(solution)/shard_map/ppermute | solution.py:261
  45.4 7.6 %collective-permute-start.18 = (bf16[2,2,64,256]{3,2,1,0:T(8,128)(2,1)S(1)}, bf16[2,2,64,256]{3,2,1,0:T(8,128)(2,1)S(1)}, u32[]{:S(2)}, u32[]{:S(2)}) collective-permute-start(bf16[2,2,64,256]{3,2,1,0:T(8,128)(2,1)S(1)} %get-tuple-element.30), channel_id=1, source_target_pairs={{0,1},{1,0},{2,3},{3,2},{4,5},{5,4},{6,7},{7,6},{8,9},{9,8},{10,11... | collective-permute-start | bytes 393224 | tf_op jit(solution)/shard_map/ppermute | solution.py:261
  47.2 10.1 %collective-permute-start.19 = (bf16[2,2,64,256]{3,2,1,0:T(8,128)(2,1)S(1)}, bf16[2,2,64,256]{3,2,1,0:T(8,128)(2,1)S(1)}, u32[]{:S(2)}, u32[]{:S(2)}) collective-permute-start(bf16[2,2,64,256]{3,2,1,0:T(8,128)(2,1)S(1)} %get-tuple-element.31), channel_id=1, source_target_pairs={{0,17},{1,16},{2,19},{3,18},{4,21},{5,20},{6,23},{7,22},{8,25},{9,... | collective-permute-start | bytes 393224 | tf_op jit(solution)/shard_map/ppermute | solution.py:261
  51.5 18.5 %collective-permute-start.13 = (bf16[2,2,32,1024]{3,2,0,1:T(8,128)(2,1)S(1)}, bf16[2,2,32,1024]{3,2,0,1:T(8,128)(2,1)S(1)}, u32[]{:S(2)}, u32[]{:S(2)}) collective-permute-start(bf16[2,2,32,1024]{3,2,0,1:T(8,128)(2,1)S(1)} %bitcast.128), channel_id=1, source_target_pairs={{0,1},{1,0},{2,3},{3,2},{4,5},{5,4},{6,7},{7,6},{8,9},{9,8},{10,11... | collective-permute-start | bytes 786440 | tf_op jit(solution)/shard_map/ppermute | solution.py:261
  53.0 17.8 %collective-permute-start.14 = (bf16[2,2,32,1024]{3,2,0,1:T(8,128)(2,1)S(1)}, bf16[2,2,32,1024]{3,2,0,1:T(8,128)(2,1)S(1)}, u32[]{:S(2)}, u32[]{:S(2)}) collective-permute-start(bf16[2,2,32,1024]{3,2,0,1:T(8,128)(2,1)S(1)} %bitcast.127), channel_id=1, source_target_pairs={{0,17},{1,16},{2,19},{3,18},{4,21},{5,20},{6,23},{7,22},{8,25},{9,... | collective-permute-start | bytes 786440 | tf_op jit(solution)/shard_map/ppermute | solution.py:261
  57.3 1.5 %collective-permute-start.7 = (bf16[2,64,1024]{2,1,0:T(8,128)(2,1)S(1)}, bf16[2,64,1024]{2,1,0:T(8,128)(2,1)S(1)}, u32[]{:S(2)}, u32[]{:S(2)}) collective-permute-start(bf16[2,64,1024]{2,1,0:T(8,128)(2,1)S(1)} %get-tuple-element.18), channel_id=1, source_target_pairs={{0,8},{1,9},{2,10},{3,11},{4,12},{5,13},{6,14},{7,15},{8,0},{9,1},... | collective-permute-start | bytes 786440 | tf_op jit(solution)/shard_map/ppermute | solution.py:261
  58.8 30.9 %collective-permute-start.20 = (bf16[64,256]{1,0:T(8,128)(2,1)S(1)}, bf16[64,256]{1,0:T(8,128)(2,1)S(1)}, u32[]{:S(2)}, u32[]{:S(2)}) collective-permute-start(bf16[64,256]{1,0:T(8,128)(2,1)S(1)} %get-tuple-element.46), channel_id=1, source_target_pairs={{0,2},{1,3},{2,0},{3,1},{4,6},{5,7},{6,4},{7,5},{8,10},{9,11},{10,... | collective-permute-start | bytes 98312 | tf_op jit(solution)/shard_map/ppermute | solution.py:261
  59.7 30.1 %copy-start.2 = (bf16[1024,1024]{1,0:T(8,128)(2,1)S(1)}, bf16[1024,1024]{1,0:T(8,128)(2,1)}, u32[]{:S(2)}) copy-start(bf16[1024,1024]{1,0:T(8,128)(2,1)} %weight_ref.5) | copy-start | bytes 6291460
  59.7 12.8 %collective-permute-start.10 = (bf16[2,2,96,256]{3,2,1,0:T(8,128)(2,1)S(1)}, bf16[2,2,96,256]{3,2,1,0:T(8,128)(2,1)S(1)}, u32[]{:S(2)}, u32[]{:S(2)}) collective-permute-start(bf16[2,2,96,256]{3,2,1,0:T(8,128)(2,1)S(1)} %get-tuple-element.27), channel_id=1, source_target_pairs={{0,17},{1,16},{2,19},{3,18},{4,21},{5,20},{6,23},{7,22},{8,25},{9,... | collective-permute-start | bytes 589832 | tf_op jit(solution)/shard_map/ppermute | solution.py:261
  70.0 6.5 %collective-permute-start.8 = (bf16[2,2,96,256]{3,2,1,0:T(8,128)(2,1)S(1)}, bf16[2,2,96,256]{3,2,1,0:T(8,128)(2,1)S(1)}, u32[]{:S(2)}, u32[]{:S(2)}) collective-permute-start(bf16[2,2,96,256]{3,2,1,0:T(8,128)(2,1)S(1)} %get-tuple-element.26), channel_id=1, source_target_pairs={{0,16},{1,17},{2,18},{3,19},{4,20},{5,21},{6,22},{7,23},{8,24},{9,... | collective-permute-start | bytes 589832 | tf_op jit(solution)/shard_map/ppermute | solution.py:261
  70.8 9.1 %collective-permute-start.9 = (bf16[2,2,96,256]{3,2,1,0:T(8,128)(2,1)S(1)}, bf16[2,2,96,256]{3,2,1,0:T(8,128)(2,1)S(1)}, u32[]{:S(2)}, u32[]{:S(2)}) collective-permute-start(bf16[2,2,96,256]{3,2,1,0:T(8,128)(2,1)S(1)} %get-tuple-element.28), channel_id=1, source_target_pairs={{0,1},{1,0},{2,3},{3,2},{4,5},{5,4},{6,7},{7,6},{8,9},{9,8},{10,11... | collective-permute-start | bytes 589832 | tf_op jit(solution)/shard_map/ppermute | solution.py:261
  72.6 17.2 %collective-permute-start.21 = (bf16[64,256]{1,0:T(8,128)(2,1)S(1)}, bf16[64,256]{1,0:T(8,128)(2,1)S(1)}, u32[]{:S(2)}, u32[]{:S(2)}) collective-permute-start(bf16[64,256]{1,0:T(8,128)(2,1)S(1)} %get-tuple-element.48), channel_id=1, source_target_pairs={{0,4},{1,5},{2,6},{3,7},{4,0},{5,1},{6,2},{7,3},{8,12},{9,13},{10,... | collective-permute-start | bytes 98312 | tf_op jit(solution)/shard_map/ppermute | solution.py:261
  76.5 13.3 %collective-permute-start.22 = (bf16[64,256]{1,0:T(8,128)(2,1)S(1)}, bf16[64,256]{1,0:T(8,128)(2,1)S(1)}, u32[]{:S(2)}, u32[]{:S(2)}) collective-permute-start(bf16[64,256]{1,0:T(8,128)(2,1)S(1)} %get-tuple-element.47), channel_id=1, source_target_pairs={{0,6},{1,7},{2,4},{3,5},{4,2},{5,3},{6,0},{7,1},{8,14},{9,15},{10,... | collective-permute-start | bytes 98312 | tf_op jit(solution)/shard_map/ppermute | solution.py:261
  80.0 5.0 %collective-permute-start.15 = (bf16[2,32,1024]{2,1,0:T(8,128)(2,1)S(1)}, bf16[2,32,1024]{2,1,0:T(8,128)(2,1)S(1)}, u32[]{:S(2)}, u32[]{:S(2)}) collective-permute-start(bf16[2,32,1024]{2,1,0:T(8,128)(2,1)S(1)} %dynamic-slice_bitcast_fusion.3), channel_id=1, source_target_pairs={{0,2},{1,3},{2,0},{3,1},{4,6},{5,7},{6,4},{7,5},{8,10},{9,11},{10,... | collective-permute-start | bytes 393224 | tf_op jit(solution)/shard_map/ppermute | solution.py:261
  84.9 4.6 %collective-permute-start.11 = (bf16[2,96,256]{2,1,0:T(8,128)(2,1)S(1)}, bf16[2,96,256]{2,1,0:T(8,128)(2,1)S(1)}, u32[]{:S(2)}, u32[]{:S(2)}) collective-permute-start(bf16[2,96,256]{2,1,0:T(8,128)(2,1)S(1)} %dynamic-slice_bitcast_fusion.5), channel_id=1, source_target_pairs={{0,2},{1,3},{2,0},{3,1},{4,6},{5,7},{6,4},{7,5},{8,10},{9,11},{10,... | collective-permute-start | bytes 294920 | tf_op jit(solution)/shard_map/ppermute | solution.py:261
  89.7 7.0 %collective-permute-start.16 = (bf16[224,256]{1,0:T(8,128)(2,1)S(1)}, bf16[224,256]{1,0:T(8,128)(2,1)S(1)}, u32[]{:S(2)}, u32[]{:S(2)}) collective-permute-start(bf16[224,256]{1,0:T(8,128)(2,1)S(1)} %dynamic-slice_bitcast_fusion.4), channel_id=1, source_target_pairs={{0,4},{1,5},{2,6},{3,7},{4,0},{5,1},{6,2},{7,3},{8,12},{9,13},{10,... | collective-permute-start | bytes 344072 | tf_op jit(solution)/shard_map/ppermute | solution.py:261
  96.8 1.4 %collective-permute-start.23 = (f32[2,32,256]{2,1,0:T(8,128)S(1)}, f32[2,32,256]{2,1,0:T(8,128)S(1)}, u32[]{:S(2)}, u32[]{:S(2)}) collective-permute-start(f32[2,32,256]{2,1,0:T(8,128)S(1)} %get-tuple-element.44), channel_id=1, source_target_pairs={{0,8},{1,9},{2,10},{3,11},{4,12},{5,13},{6,14},{7,15},{8,0},{9,1},... | collective-permute-start | bytes 196616 | tf_op jit(solution)/shard_map/ppermute | solution.py:261
